TPU v7x, 32 devices: a whole 2x2x4 slice. The times are simulated.
32 devices in a mesh: row: 8 (over y, x, core), depth: 4 (over z).
Axes of the slice: x: 2, y: 2, z: 4, core: 2. Of those that a mesh axis runs over, the one named last changes fastest.
Arguments:
- density: float32 [64, 128, 1024], P('depth', 'row'), may hold values from 0.2 to 1.5
- velocity: float32 [3, 64, 128, 1024], P(None, 'depth', 'row'), may hold values from -3 to 3
- palette: float32 [3, 4], replicated, may hold values from -6 to 6
Outputs:
- filtered: float32 [4, 128, 1024], P(None, 'row', 'depth')
- settled_density: float32 [64, 128, 1024], P('depth', 'row')
- settled_velocity: float32 [3, 64, 128, 1024], P(None, 'depth', 'row')
All inputs are finite; a program needn't handle non-finite values.
Results may differ from a plain program's by a relative error of at most 0.00013.
Values sent between devices are 32-bit elements; how exact they have to be, the bound alone decides.
No kernel may reach another device: no remote copies, remote signals or barrier semaphores. Data moves between devices by JAX's collectives and lax.ppermute only.
A program may use at most 128 MiB of HBM per device.

v0:
```python
import functools
import math

import jax
import jax.numpy as jnp
from jax import lax
from jax.experimental import pallas as pl
from jax.experimental.pallas import tpu as pltpu
from jax.sharding import PartitionSpec as P


DIFFUSION = 0.1
ADVECTION = 0.25
VISCOSITY = 0.15
FRICTION = 0.2
OPTICAL = 2.0
RANGE_SCALE = 0.1
SPACE_SCALE = 1.5
SUB = 8
LANES = 128
PITCH = 40
AXES = ("row", "depth")


def row_pairs(kind, count):
    pairs = []
    for low in range(kind, count - 1, 2):
        pairs += [(low, low + 1), (low + 1, low)]
    return pairs


def swap_rows(array, kind):
    return lax.ppermute(array, "row", row_pairs(kind, lax.axis_size("row")))


def swap_depths(array, kind):
    return lax.ppermute(array, "depth", row_pairs(kind, lax.axis_size("depth")))


def swap_corners(array, row_kind, depth_kind):
    depths = lax.axis_size("depth")
    pairs = [
        (a * depths + c, b * depths + d)
        for a, b in row_pairs(row_kind, lax.axis_size("row"))
        for c, d in row_pairs(depth_kind, depths)
    ]
    return lax.ppermute(array, AXES, pairs)


def in_vmem(array):
    return pltpu.with_memory_space_constraint(array, pltpu.VMEM)


def pack_kernel(
    den_ref, vel_ref, block, row0_ref, row1_ref, c10_ref, c11_ref, sides, load_sem,
    *, layers, rows, spans, chunks,
):
    row_odd = lax.rem(lax.axis_index("row"), 2)
    depth_odd = lax.rem(lax.axis_index("depth"), 2)
    size = layers // chunks

    def loads(k):
        z = slice(k * size, (k + 1) * size)
        return (
            pltpu.make_async_copy(den_ref.at[z], block.at[0, z], load_sem.at[k, 0]),
            pltpu.make_async_copy(vel_ref.at[:, z], block.at[1:4, z], load_sem.at[k, 1]),
        )

    for k in range(chunks):
        for copy in loads(k):
            copy.start()
    for k in range(chunks):
        for copy in loads(k):
            copy.wait()
        for c in range(4):
            for z in range(k * size, (k + 1) * size):
                for side in range(2):
                    for n in range(2):
                        row = n + side * (rows - 2)
                        for j in range(spans):
                            sides[side, c, z, n, j : j + 1, :] = block[
                                c, z, row : row + 1, j * LANES : (j + 1) * LANES
                            ]
        for c in range(4):
            for z in range(k * size, (k + 1) * size):
                for n in range(2):
                    row0_ref[c, z, n] = sides[1 - row_odd, c, z, n]
                    row1_ref[c, z, n] = sides[row_odd, c, z, n]
    for target, side in ((c10_ref, 1 - depth_odd), (c11_ref, depth_odd)):
        for c in range(4):
            target[c] = row1_ref[c, side * (layers - 1), row_odd]


def pack_depth_kernel(block, row0_ref, depth0_ref, depth1_ref, *, layers, rows, spans):
    row_odd = lax.rem(lax.axis_index("row"), 2)
    depth_odd = lax.rem(lax.axis_index("depth"), 2)
    for target, side in ((depth0_ref, 1 - depth_odd), (depth1_ref, depth_odd)):
        for c in range(4):
            for n in range(2):
                z = side * (layers - 2) + n
                for j in range(spans):
                    target[c, pl.ds((n * spans + j) * rows, rows), :] = block[
                        c, z, :, j * LANES : (j + 1) * LANES
                    ]
            target[c, pl.ds(2 * spans * rows, spans), :] = row0_ref[
                c, side * (layers - 1), row_odd
            ]


def row_of(j, row):
    return PITCH * j + SUB + row


def advance(here, up, down, left, right, front, back):
    around = [
        ((front[c] + back[c]) + (up[c] + down[c])) + (left[c] + right[c]) for c in range(4)
    ]
    flux = (
        (right[0] * right[1] - left[0] * left[1])
        + (down[0] * down[2] - up[0] * up[2])
        + (back[0] * back[3] - front[0] * front[3])
    )
    squared = here[0] * here[0]
    new = [
        (1.0 - 6.0 * DIFFUSION) * here[0] + (DIFFUSION * around[0] - (0.5 * ADVECTION) * flux)
    ]
    inverse = 1.0 / ((1.0 + squared) * (1.0 + FRICTION * squared))
    own_share = (1.0 + (1.0 - 6.0 * VISCOSITY) * squared) * inverse
    near_share = (VISCOSITY * squared) * inverse
    for c in range(1, 4):
        new.append(here[c] * own_share + around[c] * near_share)
    return new, near_share


def late_share(value, neighbour, near_share, along, sign):
    out = [
        value[0]
        + neighbour[0] * (DIFFUSION + (sign * 0.5 * ADVECTION) * neighbour[along])
    ]
    return out + [value[c] + near_share * neighbour[c] for c in range(1, 4)]


def neighbours(cells, slots, t, j, spans, first, last):
    oldest, middle, newest = slots
    row = t * SUB

    def at(which, r, jj=j):
        return [cells[which, c, pl.ds(row_of(jj, r), SUB), :] for c in range(4)]

    here = at(middle, row)
    zeros = [jnp.zeros((SUB, LANES), jnp.float32)] * 4
    before = at(middle, row, j - 1) if j > 0 else zeros
    after = at(middle, row, j + 1) if j < spans - 1 else zeros
    left = [pltpu.roll(jnp.where(last, b, x), 1, 1) for b, x in zip(before, here)]
    right = [pltpu.roll(jnp.where(first, a, x), LANES - 1, 1) for a, x in zip(after, here)]
    return (
        here, at(middle, row - 1), at(middle, row + 1), left, right,
        at(oldest, row), at(newest, row),
    )


def interior_kernel(
    block, early_ref, share_ref, edge_ref, base, *, layers, rows, columns
):
    step = pl.program_id(0)
    own_tiles, spans = rows // SUB, columns // LANES
    lane = lax.broadcasted_iota(jnp.int32, (SUB, LANES), 1)
    first, last = lane == 0, lane == LANES - 1

    @pl.when(step == 0)
    def _():
        line = jnp.zeros((spans, LANES), jnp.float32)
        for slot in range(4):
            for c in range(4):
                for row in (-1, rows):
                    base[slot, c, pl.ds(row_of(0, row), spans, stride=PITCH), :] = line
        base[3] = jnp.zeros((4, spans * PITCH, LANES), jnp.float32)
        base[2] = jnp.zeros((4, spans * PITCH, LANES), jnp.float32)

    def first_step(z, slots):
        for j in range(spans):
            for t in range(own_tiles):
                new, share = advance(*neighbours(base, slots, t, j, spans, first, last))
                cells = pl.ds(j * rows + t * SUB, SUB)
                share_ref[z, cells, :] = share
                for c in range(4):
                    early_ref[z, c, cells, :] = new[c]

    for q in range(4):
        z = 4 * step + q
        for t in range(own_tiles):
            for j in range(spans):
                there = (slice(t * SUB, (t + 1) * SUB), slice(j * LANES, (j + 1) * LANES))
                for c in range(4):
                    base[q, c, pl.ds(row_of(j, t * SUB), SUB), :] = block[(c, z) + there]
        for side, row in ((0, 0), (1, rows - 1)):
            for c in range(4):
                edge_ref[z, side, c] = base[q, c, pl.ds(row_of(0, row), spans, stride=PITCH), :]
        first_step(jnp.maximum(z - 1, 0), ((q + 2) % 4, (q + 3) % 4, q))

    @pl.when(step == layers // 4 - 1)
    def _():
        base[0] = jnp.zeros((4, spans * PITCH, LANES), jnp.float32)
        first_step(layers - 1, (2, 3, 0))


def settle_kernel(
    palette_ref, block, row0_ref, row1_ref, depth0_ref, depth1_ref, c10_ref, c11_ref,
    early_ref, share_ref, edge_ref, den_out, vel_out, *rest,
    layers, rows, columns, depth_count, row_count,
):
    pieces = rest[:depth_count]
    rowbuf, base, sbase, accum = rest[depth_count:]
    step = pl.program_id(0)
    steps = layers // 4
    own_tiles, spans = rows // SUB, columns // LANES
    row_rank, depth_rank = lax.axis_index("row"), lax.axis_index("depth")
    row_odd, depth_odd = lax.rem(row_rank, 2), lax.rem(depth_rank, 2)
    above, below = 1 - row_odd, row_odd
    sub = lax.broadcasted_iota(jnp.int32, (SUB, LANES), 0)
    lane = lax.broadcasted_iota(jnp.int32, (SUB, LANES), 1)
    first, last = lane == 0, lane == LANES - 1
    from_front = jnp.full((SUB, LANES), depth_odd, jnp.int32) == 1

    tiles = [(t, j) for j in range(spans) for t in range(own_tiles)]

    def tile_of(t, j):
        return slice(t * SUB, (t + 1) * SUB), slice(j * LANES, (j + 1) * LANES)

    def cells_of(t, j):
        return pl.ds(j * rows + t * SUB, SUB)

    def line(row):
        return pl.ds(row_of(0, row), spans, stride=PITCH)

    def outer_step(slot, front):
        kept = (depth_rank > 0) if front else (depth_rank < depth_count - 1)
        keep = jnp.full((SUB, LANES), jnp.where(kept, 1, 0), jnp.int32) == 1
        chosen = from_front if front else jnp.logical_not(from_front)
        far, near = (0, 1) if front else (1, 0)
        for t, j in tiles:
            there = tile_of(t, j)
            for c in range(4):
                for k, n in ((0, far), (1, near)):
                    cells = pl.ds((n * spans + j) * rows + t * SUB, SUB)
                    base[k, c, pl.ds(row_of(j, t * SUB), SUB), :] = jnp.where(
                        chosen, depth0_ref[c, cells, :], depth1_ref[c, cells, :]
                    )
                base[2, c, pl.ds(row_of(j, t * SUB), SUB), :] = block[
                    (c, 0 if front else layers - 1) + there
                ]
        z = 0 if front else layers + 1
        for c in range(4):
            base[1, c, line(-1), :] = rowbuf[above, c, z, 1]
            base[1, c, line(rows), :] = rowbuf[below, c, z, 0]
        slots = (0, 1, 2) if front else (2, 1, 0)
        for t, j in tiles:
            new, _ = advance(*neighbours(base, slots, t, j, spans, first, last))
            for c in range(4):
                sbase[slot, c, pl.ds(row_of(j, t * SUB), SUB), :] = jnp.where(keep, new[c], 0.0)

    def add_layer(z, slot, sign):
        for t, j in tiles:
            cells = pl.ds(row_of(j, t * SUB), SUB)
            new = late_share(
                [sbase[slot, c, cells, :] for c in range(4)],
                [base[1, c, cells, :] for c in range(4)],
                share_ref[z, cells_of(t, j), :], 3, sign,
            )
            for c in range(4):
                sbase[slot, c, cells, :] = new[c]

    def take_layer(z, slot):
        for t, j in tiles:
            for c in range(4):
                sbase[slot, c, pl.ds(row_of(j, t * SUB), SUB), :] = early_ref[z, c, cells_of(t, j), :]
        for side, kind, k, row, exists in (
            (0, above, 1, -1, row_rank > 0), (1, below, 0, rows, row_rank < row_count - 1),
        ):
            own_row = 0 if side == 0 else rows - 1
            own_cells = pl.ds(own_row, spans, stride=rows)

            def halo(layer, n):
                return [rowbuf[kind, c, layer, n] for c in range(4)]

            here, farther = halo(z + 1, k), halo(z + 1, 1 - k)
            own = [edge_ref[z, side, c] for c in range(4)]
            new = late_share(
                [early_ref[z, c, own_cells, :] for c in range(4)], here,
                share_ref[z, own_cells, :], 2, 1.0 if side == 0 else -1.0,
            )
            for c in range(4):
                sbase[slot, c, line(own_row), :] = new[c]
            left, right = [], []
            for value in here:
                before = jnp.where(sub == 0, 0.0, pltpu.roll(value, 1, 0))
                after = jnp.where(sub == SUB - 1, 0.0, pltpu.roll(value, SUB - 1, 0))
                left.append(pltpu.roll(jnp.where(last, before, value), 1, 1))
                right.append(pltpu.roll(jnp.where(first, after, value), LANES - 1, 1))
            up, down = (farther, own) if side == 0 else (own, farther)
            new, _ = advance(here, up, down, left, right, halo(z, k), halo(z + 2, k))
            inside = jnp.full((SUB, LANES), jnp.where(exists, 1, 0), jnp.int32) == 1
            for c in range(4):
                sbase[slot, c, line(row), :] = jnp.where(inside, new[c], 0.0)

    @pl.when(step == 0)
    def _():
        for kind, source in ((0, row0_ref), (1, row1_ref)):
            for c in range(4):
                for z in range(layers):
                    for k in range(2):
                        rowbuf[kind, c, z + 1, k] = source[c, z, k]
        beside = pl.ds(2 * spans * rows, spans)
        corners = (
            (0, 0, lambda c: depth0_ref[c, beside, :]), (0, 1, lambda c: depth1_ref[c, beside, :]),
            (1, 0, lambda c: c10_ref[c]), (1, 1, lambda c: c11_ref[c]),
        )
        for row_kind, depth_kind, source in corners:
            is_above = row_odd if row_kind == 0 else 1 - row_odd
            is_front = depth_odd if depth_kind == 0 else 1 - depth_odd
            for c in range(4):
                rowbuf[row_kind, c, (1 - is_front) * (layers + 1), is_above] = source(c)
        for c in range(3):
            accum[c] = jnp.zeros((spans * rows, LANES), jnp.float32)
        accum[3] = jnp.ones((spans * rows, LANES), jnp.float32)
        outer_step(3, True)
        take_layer(0, 0)
        add_layer(0, 0, 1.0)

    rate = -OPTICAL / (layers * depth_count) / math.log(2.0)
    mix = [[0.5 * palette_ref[c, k] for k in range(4)] for c in range(3)]

    def second_step(q):
        for t, j in tiles:
            slots = ((q + 3) % 4, q, (q + 1) % 4)
            new, _ = advance(*neighbours(sbase, slots, t, j, spans, first, last))
            there = tile_of(t, j)
            den_out[(q,) + there] = new[0]
            for c in range(3):
                vel_out[(c, q) + there] = new[c + 1]
            pixels = cells_of(t, j)
            before = accum[3, pixels, :]
            passed = before * jnp.exp2(rate * (new[0] * new[0]))
            weight = before - passed
            accum[3, pixels, :] = passed
            for c in range(3):
                mixed = (mix[c][0] * new[0] + mix[c][1] * new[1]) + (
                    mix[c][2] * new[2] + mix[c][3] * new[3]
                )
                accum[c, pixels, :] = accum[c, pixels, :] + weight * jnp.tanh(mixed)

    for q in range(3):
        take_layer(4 * step + q + 1, q + 1)
        if q == 2:

            @pl.when(step == steps - 1)
            def _():
                outer_step(0, False)
                add_layer(layers - 1, 3, -1.0)

        second_step(q)

    @pl.when(step < steps - 1)
    def _():
        take_layer(4 * step + 4, 0)

    second_step(3)

    @pl.when(step == steps - 1)
    def _():
        width = columns // depth_count
        per_piece = width // LANES

        def channels(j, t):
            pixels = pl.ds(j * rows + t * SUB, SUB)
            through = accum[3, pixels, :]
            return [0.5 * (accum[c, pixels, :] + (1.0 - through)) for c in range(3)] + [through]

        for k in range(depth_count):
            piece = depth_rank ^ k
            start = piece * per_piece
            for t in range(own_tiles):
                r = slice(t * SUB, (t + 1) * SUB)
                for jj in range(per_piece):
                    values = channels(start + jj, t)
                    for c in range(4):
                        pieces[k][r, c * width + jj * LANES : c * width + (jj + 1) * LANES] = (
                            values[c]
                        )
                before = channels(jnp.maximum(start - 1, 0), t)
                after = channels(jnp.minimum(start + per_piece, spans - 1), t)
                edge = jnp.zeros((SUB, LANES), jnp.float32)
                for c in range(4):
                    for values, low in ((before, 4 * c), (after, 4 * c + 2)):
                        turned = pltpu.roll(values[c], (4 * c + 2) % LANES, 1)
                        edge = jnp.where((lane >= low) & (lane < low + 2), turned, edge)
                pieces[k][r, 4 * width : 4 * width + LANES] = edge


def transfer_order(count):
    return sorted(range(count), key=lambda k: (k != 0, k % 2, k)) if count > 2 else list(range(count))


def over_kernel(*refs, count, width):
    parts = [refs[transfer_order(count).index(k)] for k in range(count)]
    picture_ref, swap0_ref, swap1_ref = refs[count:]
    rows = picture_ref.shape[0]
    depth_rank = lax.axis_index("depth")
    row_odd = lax.rem(lax.axis_index("row"), 2)
    lane = lax.broadcasted_iota(jnp.int32, (rows, LANES), 1)

    def split(ref):
        return [ref[:, c * width : (c + 1) * width] for c in range(4)] + [
            ref[:, 4 * width : 4 * width + LANES]
        ]

    def spread_through(edge):
        out = jnp.ones_like(edge)
        for c in range(3):
            turned = pltpu.roll(edge, LANES - 12 + 4 * c, 1)
            out = jnp.where((lane >= 4 * c) & (lane < 4 * c + 4), turned, out)
        return out

    def over(swapped, a, b):
        near = [jnp.where(swapped, y, x) for x, y in zip(a, b)]
        far = [jnp.where(swapped, x, y) for x, y in zip(a, b)]
        out = [near[c] + near[3] * far[c] for c in range(3)]
        out.append(near[3] * far[3])
        edge = near[4] + spread_through(near[4]) * far[4]
        out.append(jnp.where(lane >= 12, near[4] * far[4], edge))
        return out

    values = [split(ref) for ref in parts]
    bit = 0
    while len(values) > 1:
        swapped = (depth_rank >> bit & 1) == 1
        values = [over(swapped, values[k], values[k + 1]) for k in range(0, len(values), 2)]
        bit += 1
    final = values[0]
    for c in range(4):
        picture_ref[:, c * width : (c + 1) * width] = (1.0 - final[3]) if c == 3 else final[c]
    edge = jnp.where((lane >= 12) & (lane < 16), 1.0 - final[4], final[4])
    picture_ref[:, 4 * width : 4 * width + LANES] = edge
    top, bottom = picture_ref[0:2, :], picture_ref[rows - 2 : rows, :]
    odd = row_odd == 1
    swap0_ref[...] = jnp.where(odd, top, bottom)
    swap1_ref[...] = jnp.where(odd, bottom, top)


def filter_kernel(picture_ref, swap0_ref, swap1_ref, out_ref, *, width, row_count, depth_count):
    row_rank, depth_rank = lax.axis_index("row"), lax.axis_index("depth")
    odd = lax.rem(row_rank, 2) == 1
    rows = picture_ref.shape[0]
    own_tiles = rows // SUB
    spans = width // LANES
    lane = lax.broadcasted_iota(jnp.int32, (SUB, LANES), 1)
    sub = lax.broadcasted_iota(jnp.int32, (SUB, LANES), 0)

    def tile(t, c, j):
        if j == -1 or j == spans:
            cols = slice(4 * width, 4 * width + LANES)
        else:
            cols = slice(c * width + j * LANES, c * width + (j + 1) * LANES)
        if t == -1:
            v = jnp.where(odd, swap0_ref[:, cols], swap1_ref[:, cols])
            v = jnp.concatenate([jnp.zeros((SUB - 2, LANES), jnp.float32), v], 0)
        elif t == own_tiles:
            v = jnp.where(odd, swap1_ref[:, cols], swap0_ref[:, cols])
            v = jnp.concatenate([v, jnp.zeros((SUB - 2, LANES), jnp.float32)], 0)
        else:
            v = picture_ref[t * SUB : (t + 1) * SUB, cols]
        if j == -1:
            v = pltpu.roll(v, LANES - 2 - 4 * c, 1)
        elif j == spans:
            v = pltpu.roll(v, (LANES - 2 - 4 * c) % LANES, 1)
        return v

    tiles = {}
    for t in range(-1, own_tiles + 1):
        for j in range(-1, spans + 1):
            four = [tile(t, c, j) for c in range(4)]
            tiles[t, j] = four + [(four[0] + four[1] + four[2]) / 3.0]

    def column_shift(t, j, q, dx):
        if dx == 0:
            return tiles[t, j][q]
        if dx > 0:
            mixed = jnp.where(lane < dx, tiles[t, j + 1][q], tiles[t, j][q])
        else:
            mixed = jnp.where(lane >= LANES + dx, tiles[t, j - 1][q], tiles[t, j][q])
        return pltpu.roll(mixed, (-dx) % LANES, 1)

    no_above, no_below = row_rank == 0, row_rank == row_count - 1
    no_west, no_east = depth_rank == 0, depth_rank == depth_count - 1
    for j in range(spans):
        sums = [[None] * 5 for _ in range(own_tiles)]
        for dx in range(-2, 3):
            shifted = {
                t: [column_shift(t, j, q, dx) for q in range(5)] for t in range(-1, own_tiles + 1)
            }
            for dy in range(-2, 3):
                spatial = -(dx * dx + dy * dy) / (2.0 * SPACE_SCALE * SPACE_SCALE)
                for t in range(own_tiles):
                    if dy == 0:
                        near = shifted[t]
                    elif dy > 0:
                        near = [
                            pltpu.roll(
                                jnp.where(sub < dy, shifted[t + 1][q], shifted[t][q]), SUB - dy, 0
                            )
                            for q in range(5)
                        ]
                    else:
                        near = [
                            pltpu.roll(
                                jnp.where(sub >= SUB + dy, shifted[t - 1][q], shifted[t][q]), -dy, 0
                            )
                            for q in range(5)
                        ]
                    diff = near[4] - tiles[t, j][4]
                    weight = jnp.exp(
                        spatial - diff * diff * (1.0 / (2.0 * RANGE_SCALE * RANGE_SCALE))
                    )
                    blocked = None
                    if t == 0 and dy < 0:
                        blocked = no_above & (sub < -dy)
                    if t == own_tiles - 1 and dy > 0:
                        blocked = no_below & (sub >= SUB - dy)
                    if j == 0 and dx < 0:
                        side = no_west & (lane < -dx)
                        blocked = side if blocked is None else blocked | side
                    if j == spans - 1 and dx > 0:
                        side = no_east & (lane >= LANES - dx)
                        blocked = side if blocked is None else blocked | side
                    if blocked is not None:
                        weight = jnp.where(blocked, 0.0, weight)
                    terms = [weight * near[c] for c in range(4)] + [weight]
                    sums[t] = terms if sums[t][0] is None else [a + b for a, b in zip(sums[t], terms)]
        for t in range(own_tiles):
            inverse = 1.0 / sums[t][4]
            for c in range(4):
                out_ref[c, t * SUB : (t + 1) * SUB, j * LANES : (j + 1) * LANES] = (
                    sums[t][c] * inverse
                )


def compute(density, velocity, palette):
    layers, rows, columns = density.shape
    depth_count, row_count = lax.axis_size("depth"), lax.axis_size("row")
    spans = columns // LANES
    width = columns // depth_count
    line = 4 * width + LANES
    assert spans == SUB and rows % SUB == 0 and width % LANES == 0 and layers % 4 == 0
    vmem = pl.BlockSpec(memory_space=pltpu.VMEM)
    smem = pl.BlockSpec(memory_space=pltpu.SMEM)
    f32 = jnp.float32

    def shape(*dims):
        return jax.ShapeDtypeStruct(dims, f32)

    def local(*dims):
        return pltpu.VMEM(dims, f32)

    def params(mebibytes):
        return pltpu.CompilerParams(vmem_limit_bytes=mebibytes << 20)

    row_shape = (4, layers, 2, spans, LANES)
    depth_shape = (4, (2 * rows + 1) * spans, LANES)
    corner_shape = (4, spans, LANES)
    block, row0, row1, corner0, corner1 = pl.pallas_call(
        functools.partial(pack_kernel, layers=layers, rows=rows, spans=spans, chunks=4),
        out_shape=(
            local(4, layers, rows, columns), local(*row_shape), local(*row_shape),
            local(*corner_shape), local(*corner_shape),
        ),
        in_specs=[pl.BlockSpec(memory_space=pltpu.HBM)] * 2,
        out_specs=(vmem,) * 5,
        scratch_shapes=[pltpu.VMEM((2,) + row_shape, f32), pltpu.SemaphoreType.DMA((4, 2))],
        name="pack",
        compiler_params=params(8),
    )(
        pltpu.with_memory_space_constraint(density, pltpu.HBM),
        pltpu.with_memory_space_constraint(velocity, pltpu.HBM),
    )
    row1 = swap_rows(row1, 1)
    row0 = swap_rows(row0, 0)
    depth0, depth1 = pl.pallas_call(
        functools.partial(pack_depth_kernel, layers=layers, rows=rows, spans=spans),
        out_shape=(local(*depth_shape), local(*depth_shape)),
        in_specs=[vmem] * 2,
        out_specs=(vmem,) * 2,
        name="pack_depth",
        compiler_params=params(8),
    )(in_vmem(block), in_vmem(row0))
    depth0, depth1 = swap_depths(depth0, 0), swap_depths(depth1, 1)
    corner0, corner1 = swap_corners(corner0, 1, 0), swap_corners(corner1, 1, 1)

    early, share, edge = pl.pallas_call(
        functools.partial(interior_kernel, layers=layers, rows=rows, columns=columns),
        grid=(layers // 4,),
        out_shape=(
            pltpu.VMEM((layers, 4, spans * rows, LANES), f32),
            pltpu.VMEM((layers, spans * rows, LANES), f32),
            pltpu.VMEM((layers, 2, 4, spans, LANES), f32),
        ),
        in_specs=[vmem],
        out_specs=(vmem,) * 3,
        scratch_shapes=[pltpu.VMEM((4, 4, spans * PITCH, LANES), f32)],
        cost_estimate=pl.CostEstimate(
            flops=80 * layers * rows * columns, bytes_accessed=16 * layers * rows * columns,
            transcendentals=layers * rows * columns,
        ),
        name="interior",
        compiler_params=pltpu.CompilerParams(vmem_limit_bytes=24 << 20),
    )(in_vmem(block))

    settled, moving, *parts = pl.pallas_call(
        functools.partial(
            settle_kernel, layers=layers, rows=rows, columns=columns,
            depth_count=depth_count, row_count=row_count,
        ),
        grid=(layers // 4,),
        out_shape=(shape(layers, rows, columns), shape(3, layers, rows, columns))
        + (shape(rows, line),) * depth_count,
        in_specs=[smem] + [vmem] * 10,
        out_specs=(
            pl.BlockSpec((4, rows, columns), lambda i: (i, 0, 0)),
            pl.BlockSpec((3, 4, rows, columns), lambda i: (0, i, 0, 0)),
        )
        + (vmem,) * depth_count,
        scratch_shapes=[
            pltpu.VMEM((2, 4, layers + 2, 2, spans, LANES), f32),
            pltpu.VMEM((3, 4, spans * PITCH, LANES), f32),
            pltpu.VMEM((4, 4, spans * PITCH, LANES), f32),
            pltpu.VMEM((4, spans * rows, LANES), f32),
        ],
        name="settle",
        compiler_params=pltpu.CompilerParams(vmem_limit_bytes=32 << 20),
    )(
        palette,
        *(
            in_vmem(x)
            for x in (block, row0, row1, depth0, depth1, corner0, corner1, early, share, edge)
        ),
    )

    parts = [
        lax.ppermute(part, "depth", [(i, i ^ k) for i in range(depth_count)]) if k else part
        for k, part in enumerate(parts)
    ]
    composed, swap0, swap1 = pl.pallas_call(
        functools.partial(over_kernel, count=depth_count, width=width),
        out_shape=(shape(rows, line), shape(2, line), shape(2, line)),
        in_specs=[vmem] * depth_count,
        out_specs=(vmem, vmem, vmem),
        name="over",
        compiler_params=pltpu.CompilerParams(vmem_limit_bytes=8 << 20),
    )(parts[0], *(in_vmem(parts[k]) for k in transfer_order(depth_count)[1:]))

    swap1, swap0 = swap_rows(swap1, 1), swap_rows(swap0, 0)
    filtered = pl.pallas_call(
        functools.partial(
            filter_kernel, width=width, row_count=row_count, depth_count=depth_count
        ),
        out_shape=shape(4, rows, width),
        in_specs=[vmem] * 3,
        out_specs=vmem,
        name="bilateral",
        compiler_params=pltpu.CompilerParams(vmem_limit_bytes=8 << 20),
    )(composed, in_vmem(swap0), in_vmem(swap1))
    return (filtered, settled, moving)


def solution(mesh):
    in_specs = (P("depth", "row", None), P(None, "depth", "row", None), P())
    out_specs = (P(None, "row", "depth"), P("depth", "row", None), P(None, "depth", "row", None))
    return jax.shard_map(
        compute, mesh=mesh, in_specs=in_specs, out_specs=out_specs, check_vma=False
    )
```

profile of v0, /device:TPU:5, one launch (start us, length us, event | category | flops | bytes accessed | tf_op | source)
XLA Modules:
  0.0 50.0 jit_solution(13707866235308978731)
XLA Ops:
  0.6 2.4 %pack.1 = (f32[4,16,16,1024]{3,2,1,0:T(8,128)S(1)}, f32[4,16,2,8,128]{4,3,2,1,0:T(8,128)S(1)}, f32[4,16,2,8,128]{4,3,2,1,0:T(8,128)S(1)}, f32[4,8,128]{2,1,0:T(8,128)S(1)}, f32[4,8,128]{2,1,0:T(8,128)S(1)}) custom-call(f32[16,16,1024]{2,1,0:T(8,128)} %den_ref.1, f32[3,16,16,1024]{3,2,1,0:T(8,128)} %vel_ref.1), custom_call_target="tpu_custom_call" | custom-call | tf_op jit(solution)/shard_map/pack/pallas_call | solution.py:570
  3.1 0.7 %collective-permute-start = (f32[4,16,2,8,128]{4,3,2,1,0:T(8,128)S(1)}, f32[4,16,2,8,128]{4,3,2,1,0:T(8,128)S(1)}, u32[]{:S(2)}, u32[]{:S(2)}) collective-permute-start(f32[4,16,2,8,128]{4,3,2,1,0:T(8,128)S(1)} %get-tuple-element.23), channel_id=1, source_target_pairs={{0,4},{4,0},{8,12},{12,8},{16,20},{20,16},{24,28},{28,24},{1,5},{5... | collective-permute-start | bytes 1572872 | tf_op jit(solution)/shard_map/ppermute | solution.py:33
  3.8 1.5 %collective-permute-done.row0_ref = f32[4,16,2,8,128]{4,3,2,1,0:T(8,128)S(1)} collective-permute-done((f32[4,16,2,8,128]{4,3,2,1,0:T(8,128)S(1)}, f32[4,16,2,8,128]{4,3,2,1,0:T(8,128)S(1)}, u32[]{:S(2)}, u32[]{:S(2)}) %collective-permute-start) | collective-permute-done | bytes 524320 | tf_op jit(solution)/shard_map/ppermute | solution.py:33
  5.4 0.1 pack_depth.1
  5.4 1.4 %collective-permute-start.2 = (f32[4,264,128]{2,1,0:T(8,128)S(1)}, f32[4,264,128]{2,1,0:T(8,128)S(1)}, u32[]{:S(2)}, u32[]{:S(2)}) collective-permute-start(f32[4,264,128]{2,1,0:T(8,128)S(1)} %get-tuple-element.25), channel_id=1, source_target_pairs={{0,1},{1,0},{2,3},{3,2},{4,5},{5,4},{6,7},{7,6},{8,9},{9,8},{10,11... | collective-permute-start | bytes 1622024 | tf_op jit(solution)/shard_map/ppermute | solution.py:37
  6.8 0.7 %collective-permute-start.3 = (f32[4,264,128]{2,1,0:T(8,128)S(1)}, f32[4,264,128]{2,1,0:T(8,128)S(1)}, u32[]{:S(2)}, u32[]{:S(2)}) collective-permute-start(f32[4,264,128]{2,1,0:T(8,128)S(1)} %get-tuple-element.26), channel_id=1, source_target_pairs={{1,2},{2,1},{5,6},{6,5},{9,10},{10,9},{13,14},{14,13},{17,18},{18,... | collective-permute-start | bytes 1622024 | tf_op jit(solution)/shard_map/ppermute | solution.py:37
  7.5 3.7 %collective-permute-start.1 = (f32[4,16,2,8,128]{4,3,2,1,0:T(8,128)S(1)}, f32[4,16,2,8,128]{4,3,2,1,0:T(8,128)S(1)}, u32[]{:S(2)}, u32[]{:S(2)}) collective-permute-start(f32[4,16,2,8,128]{4,3,2,1,0:T(8,128)S(1)} %get-tuple-element.24), channel_id=1, source_target_pairs={{4,8},{8,4},{12,16},{16,12},{20,24},{24,20},{5,9},{9,5},{13,17},{1... | collective-permute-start | bytes 1572872 | tf_op jit(solution)/shard_map/ppermute | solution.py:33
  11.2 5.7 %collective-permute-start.4 = (f32[4,8,128]{2,1,0:T(8,128)S(1)}, f32[4,8,128]{2,1,0:T(8,128)S(1)}, u32[]{:S(2)}, u32[]{:S(2)}) collective-permute-start(f32[4,8,128]{2,1,0:T(8,128)S(1)} %get-tuple-element.27), channel_id=1, source_target_pairs={{4,9},{5,8},{6,11},{7,10},{8,5},{9,4},{10,7},{11,6},{12,17},{13,16... | collective-permute-start | bytes 49160 | tf_op jit(solution)/shard_map/ppermute | solution.py:47
  16.9 0.7 %collective-permute-start.5 = (f32[4,8,128]{2,1,0:T(8,128)S(1)}, f32[4,8,128]{2,1,0:T(8,128)S(1)}, u32[]{:S(2)}, u32[]{:S(2)}) collective-permute-start(f32[4,8,128]{2,1,0:T(8,128)S(1)} %get-tuple-element.28), channel_id=1, source_target_pairs={{5,10},{6,9},{9,6},{10,5},{13,18},{14,17},{17,14},{18,13},{21,26},... | collective-permute-start | bytes 49160 | tf_op jit(solution)/shard_map/ppermute | solution.py:47
  17.6 3.4 %interior.1 = (f32[16,4,128,128]{3,2,1,0:T(8,128)S(1)}, f32[16,128,128]{2,1,0:T(8,128)S(1)}, f32[16,2,4,8,128]{4,3,2,1,0:T(8,128)S(1)}) custom-call(f32[4,16,16,1024]{3,2,1,0:T(8,128)S(1)} %get-tuple-element.22.block), custom_call_target="tpu_custom_call" | custom-call | flops 20971520 | bytes 4194304 | tf_op jit(solution)/shard_map/interior/pallas_call | solution.py:598
  20.9 0.0 collective-permute-done.4.c10_ref
  20.9 0.0 collective-permute-done.5.c11_ref
  20.9 2.3 %collective-permute-done.1.row1_ref = f32[4,16,2,8,128]{4,3,2,1,0:T(8,128)S(1)} collective-permute-done((f32[4,16,2,8,128]{4,3,2,1,0:T(8,128)S(1)}, f32[4,16,2,8,128]{4,3,2,1,0:T(8,128)S(1)}, u32[]{:S(2)}, u32[]{:S(2)}) %collective-permute-start.1) | collective-permute-done | bytes 524320 | tf_op jit(solution)/shard_map/ppermute | solution.py:33
  23.2 7.5 %settle.1 = (f32[16,16,1024]{2,1,0:T(8,128)}, f32[3,16,16,1024]{3,2,1,0:T(8,128)}, f32[16,1152]{1,0:T(8,128)S(1)}, f32[16,1152]{1,0:T(8,128)S(1)}, f32[16,1152]{1,0:T(8,128)S(1)}, /*index=5*/f32[16,1152]{1,0:T(8,128)S(1)}) custom-call(f32[3,4]{1,0:T(4,128)S(1)} %copy-done, f32[4,16,16,1024]{3,2,1,0:T(8,128)S(1)} %get-tuple-element.22.block, ...), custom_call_target="tpu_custom_call" | custom-call | tf_op jit(solution)/shard_map/settle/pallas_call | solution.py:617
  30.8 3.9 %collective-permute-start.6 = (f32[16,1152]{1,0:T(8,128)S(1)}, f32[16,1152]{1,0:T(8,128)S(1)}, u32[]{:S(2)}, u32[]{:S(2)}) collective-permute-start(f32[16,1152]{1,0:T(8,128)S(1)} %get-tuple-element.33), channel_id=1, source_target_pairs={{0,2},{1,3},{2,0},{3,1},{4,6},{5,7},{6,4},{7,5},{8,10},{9,11},{10,... | collective-permute-start | bytes 221192 | tf_op jit(solution)/shard_map/ppermute | solution.py:648
  34.6 0.2 collective-permute-start.7
  34.9 2.1 %collective-permute-start.8 = (f32[16,1152]{1,0:T(8,128)S(1)}, f32[16,1152]{1,0:T(8,128)S(1)}, u32[]{:S(2)}, u32[]{:S(2)}) collective-permute-start(f32[16,1152]{1,0:T(8,128)S(1)} %get-tuple-element.35), channel_id=1, source_target_pairs={{0,3},{1,2},{2,1},{3,0},{4,7},{5,6},{6,5},{7,4},{8,11},{9,10},{10,... | collective-permute-start | bytes 221192 | tf_op jit(solution)/shard_map/ppermute | solution.py:648
  37.0 1.7 %collective-permute-done.7.refs_2_ = f32[16,1152]{1,0:T(8,128)S(1)} collective-permute-done((f32[16,1152]{1,0:T(8,128)S(1)}, f32[16,1152]{1,0:T(8,128)S(1)}, u32[]{:S(2)}, u32[]{:S(2)}) %collective-permute-start.7) | collective-permute-done | bytes 73760 | tf_op jit(solution)/shard_map/ppermute | solution.py:648
  38.6 1.9 %collective-permute-done.8.refs_3_ = f32[16,1152]{1,0:T(8,128)S(1)} collective-permute-done((f32[16,1152]{1,0:T(8,128)S(1)}, f32[16,1152]{1,0:T(8,128)S(1)}, u32[]{:S(2)}, u32[]{:S(2)}) %collective-permute-start.8) | collective-permute-done | bytes 73760 | tf_op jit(solution)/shard_map/ppermute | solution.py:648
  40.5 0.2 over.1
  40.7 2.9 %collective-permute-start.9 = (f32[2,1152]{1,0:T(2,128)S(1)}, f32[2,1152]{1,0:T(2,128)S(1)}, u32[]{:S(2)}, u32[]{:S(2)}) collective-permute-start(f32[2,1152]{1,0:T(2,128)S(1)} %get-tuple-element.37), channel_id=1, source_target_pairs={{0,4},{4,0},{8,12},{12,8},{16,20},{20,16},{24,28},{28,24},{1,5},{5... | collective-permute-start | bytes 27656 | tf_op jit(solution)/shard_map/ppermute | solution.py:33
  43.6 2.5 %collective-permute-start.10 = (f32[2,1152]{1,0:T(2,128)S(1)}, f32[2,1152]{1,0:T(2,128)S(1)}, u32[]{:S(2)}, u32[]{:S(2)}) collective-permute-start(f32[2,1152]{1,0:T(2,128)S(1)} %get-tuple-element.38), channel_id=1, source_target_pairs={{4,8},{8,4},{12,16},{16,12},{20,24},{24,20},{5,9},{9,5},{13,17},{1... | collective-permute-start | bytes 27656 | tf_op jit(solution)/shard_map/ppermute | solution.py:33
  46.2 2.7 %collective-permute-done.10.swap1_ref = f32[2,1152]{1,0:T(2,128)S(1)} collective-permute-done((f32[2,1152]{1,0:T(2,128)S(1)}, f32[2,1152]{1,0:T(2,128)S(1)}, u32[]{:S(2)}, u32[]{:S(2)}) %collective-permute-start.10) | collective-permute-done | bytes 9248 | tf_op jit(solution)/shard_map/ppermute | solution.py:33
  48.9 1.1 %bilateral.1 = f32[4,16,256]{2,1,0:T(8,128)} custom-call(f32[16,1152]{1,0:T(8,128)S(1)} %get-tuple-element.36.picture_ref, f32[2,1152]{1,0:T(2,128)S(1)} %collective-permute-done.9.swap0_ref, f32[2,1152]{1,0:T(2,128)S(1)} %collective-permute-done.10.swap1_ref), custom_call_target="tpu_custom_call" | custom-call | tf_op jit(solution)/shard_map/bilateral/pallas_call | solution.py:661
  (6 shorter events, 0.0 us)
Async XLA Ops:
  3.1 2.3 %collective-permute-start = (f32[4,16,2,8,128]{4,3,2,1,0:T(8,128)S(1)}, f32[4,16,2,8,128]{4,3,2,1,0:T(8,128)S(1)}, u32[]{:S(2)}, u32[]{:S(2)}) collective-permute-start(f32[4,16,2,8,128]{4,3,2,1,0:T(8,128)S(1)} %get-tuple-element.23), channel_id=1, source_target_pairs={{0,4},{4,0},{8,12},{12,8},{16,20},{20,16},{24,28},{28,24},{1,5},{5... | collective-permute-start | bytes 1572872 | tf_op jit(solution)/shard_map/ppermute | solution.py:33
  5.4 17.9 %copy-start = (f32[3,4]{1,0:T(4,128)S(1)}, f32[3,4]{1,0:T(4,128)}, u32[]{:S(2)}) copy-start(f32[3,4]{1,0:T(4,128)} %palette_ref.1) | copy-start | bytes 148
  5.4 17.8 %collective-permute-start.2 = (f32[4,264,128]{2,1,0:T(8,128)S(1)}, f32[4,264,128]{2,1,0:T(8,128)S(1)}, u32[]{:S(2)}, u32[]{:S(2)}) collective-permute-start(f32[4,264,128]{2,1,0:T(8,128)S(1)} %get-tuple-element.25), channel_id=1, source_target_pairs={{0,1},{1,0},{2,3},{3,2},{4,5},{5,4},{6,7},{7,6},{8,9},{9,8},{10,11... | collective-permute-start | bytes 1622024 | tf_op jit(solution)/shard_map/ppermute | solution.py:37
  6.8 16.4 %collective-permute-start.3 = (f32[4,264,128]{2,1,0:T(8,128)S(1)}, f32[4,264,128]{2,1,0:T(8,128)S(1)}, u32[]{:S(2)}, u32[]{:S(2)}) collective-permute-start(f32[4,264,128]{2,1,0:T(8,128)S(1)} %get-tuple-element.26), channel_id=1, source_target_pairs={{1,2},{2,1},{5,6},{6,5},{9,10},{10,9},{13,14},{14,13},{17,18},{18,... | collective-permute-start | bytes 1622024 | tf_op jit(solution)/shard_map/ppermute | solution.py:37
  7.5 15.7 %collective-permute-start.1 = (f32[4,16,2,8,128]{4,3,2,1,0:T(8,128)S(1)}, f32[4,16,2,8,128]{4,3,2,1,0:T(8,128)S(1)}, u32[]{:S(2)}, u32[]{:S(2)}) collective-permute-start(f32[4,16,2,8,128]{4,3,2,1,0:T(8,128)S(1)} %get-tuple-element.24), channel_id=1, source_target_pairs={{4,8},{8,4},{12,16},{16,12},{20,24},{24,20},{5,9},{9,5},{13,17},{1... | collective-permute-start | bytes 1572872 | tf_op jit(solution)/shard_map/ppermute | solution.py:33
  11.2 9.8 %collective-permute-start.4 = (f32[4,8,128]{2,1,0:T(8,128)S(1)}, f32[4,8,128]{2,1,0:T(8,128)S(1)}, u32[]{:S(2)}, u32[]{:S(2)}) collective-permute-start(f32[4,8,128]{2,1,0:T(8,128)S(1)} %get-tuple-element.27), channel_id=1, source_target_pairs={{4,9},{5,8},{6,11},{7,10},{8,5},{9,4},{10,7},{11,6},{12,17},{13,16... | collective-permute-start | bytes 49160 | tf_op jit(solution)/shard_map/ppermute | solution.py:47
  16.9 4.0 %collective-permute-start.5 = (f32[4,8,128]{2,1,0:T(8,128)S(1)}, f32[4,8,128]{2,1,0:T(8,128)S(1)}, u32[]{:S(2)}, u32[]{:S(2)}) collective-permute-start(f32[4,8,128]{2,1,0:T(8,128)S(1)} %get-tuple-element.28), channel_id=1, source_target_pairs={{5,10},{6,9},{9,6},{10,5},{13,18},{14,17},{17,14},{18,13},{21,26},... | collective-permute-start | bytes 49160 | tf_op jit(solution)/shard_map/ppermute | solution.py:47
  30.8 6.2 %collective-permute-start.6 = (f32[16,1152]{1,0:T(8,128)S(1)}, f32[16,1152]{1,0:T(8,128)S(1)}, u32[]{:S(2)}, u32[]{:S(2)}) collective-permute-start(f32[16,1152]{1,0:T(8,128)S(1)} %get-tuple-element.33), channel_id=1, source_target_pairs={{0,2},{1,3},{2,0},{3,1},{4,6},{5,7},{6,4},{7,5},{8,10},{9,11},{10,... | collective-permute-start | bytes 221192 | tf_op jit(solution)/shard_map/ppermute | solution.py:648
  34.6 4.0 %collective-permute-start.7 = (f32[16,1152]{1,0:T(8,128)S(1)}, f32[16,1152]{1,0:T(8,128)S(1)}, u32[]{:S(2)}, u32[]{:S(2)}) collective-permute-start(f32[16,1152]{1,0:T(8,128)S(1)} %get-tuple-element.34), channel_id=1, source_target_pairs={{0,1},{1,0},{2,3},{3,2},{4,5},{5,4},{6,7},{7,6},{8,9},{9,8},{10,11... | collective-permute-start | bytes 221192 | tf_op jit(solution)/shard_map/ppermute | solution.py:648
  34.9 5.6 %collective-permute-start.8 = (f32[16,1152]{1,0:T(8,128)S(1)}, f32[16,1152]{1,0:T(8,128)S(1)}, u32[]{:S(2)}, u32[]{:S(2)}) collective-permute-start(f32[16,1152]{1,0:T(8,128)S(1)} %get-tuple-element.35), channel_id=1, source_target_pairs={{0,3},{1,2},{2,1},{3,0},{4,7},{5,6},{6,5},{7,4},{8,11},{9,10},{10,... | collective-permute-start | bytes 221192 | tf_op jit(solution)/shard_map/ppermute | solution.py:648
  40.7 5.4 %collective-permute-start.9 = (f32[2,1152]{1,0:T(2,128)S(1)}, f32[2,1152]{1,0:T(2,128)S(1)}, u32[]{:S(2)}, u32[]{:S(2)}) collective-permute-start(f32[2,1152]{1,0:T(2,128)S(1)} %get-tuple-element.37), channel_id=1, source_target_pairs={{0,4},{4,0},{8,12},{12,8},{16,20},{20,16},{24,28},{28,24},{1,5},{5... | collective-permute-start | bytes 27656 | tf_op jit(solution)/shard_map/ppermute | solution.py:33
  43.6 5.3 %collective-permute-start.10 = (f32[2,1152]{1,0:T(2,128)S(1)}, f32[2,1152]{1,0:T(2,128)S(1)}, u32[]{:S(2)}, u32[]{:S(2)}) collective-permute-start(f32[2,1152]{1,0:T(2,128)S(1)} %get-tuple-element.38), channel_id=1, source_target_pairs={{4,8},{8,4},{12,16},{16,12},{20,24},{24,20},{5,9},{9,5},{13,17},{1... | collective-permute-start | bytes 27656 | tf_op jit(solution)/shard_map/ppermute | solution.py:33
where the time goes:
time: 50.2 us; the launch traced here: 50 us
  starting transfers between devices  24.5 us (49%)
  Pallas kernels  14.6 us (29%)
  waiting for transfers between devices  10.1 us (20%)
  between operations  0.72 us (1%)
    ppermute x4, starting transfers between devices, swap_rows(): return lax.ppermute(array, 'row', row_pairs(kind, lax.axis_size('row')))  9.83 us
    pallas_call x1, Pallas kernels, compute(): pl.pallas_call(functools.partial(settle_kernel, layers=layers, rows=rows,...  7.52 us
    ppermute x4, waiting for transfers between devices, swap_rows(): return lax.ppermute(array, 'row', row_pairs(kind, lax.axis_size('row')))  6.54 us
    ppermute x2, starting transfers between devices, swap_corners(): return lax.ppermute(array, AXES, pairs)  6.38 us
    ppermute x3, starting transfers between devices, compute(): lax.ppermute(part, 'depth', [(i, i ^ k) for i in range(depth_count)])  6.22 us
    ppermute x3, waiting for transfers between devices, compute(): lax.ppermute(part, 'depth', [(i, i ^ k) for i in range(depth_count)])  3.57 us
    pallas_call x1, Pallas kernels, compute(): pl.pallas_call(functools.partial(interior_kernel, layers=layers, rows=row...  3.35 us
    pallas_call x1, Pallas kernels, compute(): pl.pallas_call(functools.partial(pack_kernel, layers=layers, rows=rows, s...  2.45 us
  transfers between devices with their start and end apart: 11, of which 5 were waited for; matrix products, arithmetic and copies ran while one was open for 0% of the time, Pallas kernels for 7%

commit v1 on v0

--- a/solution.py
+++ b/solution.py
@@ -159,8 +159,36 @@
     )
 
 
+def render(accum, pixels, cells, rate, mix):
+    before = accum[3, pixels, :]
+    passed = before * jnp.exp2(rate * (cells[0] * cells[0]))
+    weight = before - passed
+    accum[3, pixels, :] = passed
+    for c in range(3):
+        mixed = (mix[c][0] * cells[0] + mix[c][1] * cells[1]) + (
+            mix[c][2] * cells[2] + mix[c][3] * cells[3]
+        )
+        accum[c, pixels, :] = accum[c, pixels, :] + weight * jnp.tanh(mixed)
+
+
+def beside_in_lines(lines, sub, first, last):
+    left, right = [], []
+    for value in lines:
+        before = jnp.where(sub == 0, 0.0, pltpu.roll(value, 1, 0))
+        after = jnp.where(sub == SUB - 1, 0.0, pltpu.roll(value, SUB - 1, 0))
+        left.append(pltpu.roll(jnp.where(last, before, value), 1, 1))
+        right.append(pltpu.roll(jnp.where(first, after, value), LANES - 1, 1))
+    return left, right
+
+
+def constants(palette_ref, depth_total):
+    rate = -OPTICAL / depth_total / math.log(2.0)
+    return rate, [[0.5 * palette_ref[c, k] for k in range(4)] for c in range(3)]
+
+
 def interior_kernel(
-    block, early_ref, share_ref, edge_ref, base, *, layers, rows, columns
+    palette_ref, block, early_ref, share_ref, edge_ref, late_ref, part_ref, base,
+    *, layers, rows, columns, depth_count,
 ):
     step = pl.program_id(0)
     own_tiles, spans = rows // SUB, columns // LANES
@@ -176,6 +204,9 @@
                     base[slot, c, pl.ds(row_of(0, row), spans, stride=PITCH), :] = line
         base[3] = jnp.zeros((4, spans * PITCH, LANES), jnp.float32)
         base[2] = jnp.zeros((4, spans * PITCH, LANES), jnp.float32)
+        for c in range(3):
+            part_ref[c] = jnp.zeros((spans * rows, LANES), jnp.float32)
+        part_ref[3] = jnp.ones((spans * rows, LANES), jnp.float32)
 
     def first_step(z, slots):
         for j in range(spans):
@@ -198,6 +229,42 @@
                 edge_ref[z, side, c] = base[q, c, pl.ds(row_of(0, row), spans, stride=PITCH), :]
         first_step(jnp.maximum(z - 1, 0), ((q + 2) % 4, (q + 3) % 4, q))
 
+    rate, mix = constants(palette_ref, layers * depth_count)
+
+    def inner_neighbours(z, t, j):
+        row = j * rows + t * SUB
+
+        def at(layer, start):
+            return [early_ref[layer, c, pl.ds(start, SUB), :] for c in range(4)]
+
+        here = at(z, row)
+        zeros = [jnp.zeros((SUB, LANES), jnp.float32)] * 4
+        before = at(z, row - rows) if j > 0 else zeros
+        after = at(z, row + rows) if j < spans - 1 else zeros
+        if row > 0:
+            up = at(z, row - 1)
+        else:
+            up = [pltpu.roll(x, 1, 0) for x in here]
+        if row + SUB < spans * rows:
+            down = at(z, row + 1)
+        else:
+            down = [pltpu.roll(x, SUB - 1, 0) for x in here]
+        left = [pltpu.roll(jnp.where(last, b, x), 1, 1) for b, x in zip(before, here)]
+        right = [pltpu.roll(jnp.where(first, a, x), LANES - 1, 1) for a, x in zip(after, here)]
+        return here, up, down, left, right, at(z - 1, row), at(z + 1, row)
+
+    @pl.when(step > 0)
+    def _():
+        for q in range(4):
+            z = 4 * step + q - 2
+            for j in range(spans):
+                for t in range(own_tiles):
+                    new, _ = advance(*inner_neighbours(z, t, j))
+                    cells = pl.ds(j * rows + t * SUB, SUB)
+                    for c in range(4):
+                        late_ref[z, c, cells, :] = new[c]
+                    render(part_ref, cells, new, rate, mix)
+
     @pl.when(step == layers // 4 - 1)
     def _():
         base[0] = jnp.zeros((4, spans * PITCH, LANES), jnp.float32)
@@ -206,11 +273,11 @@
 
 def settle_kernel(
     palette_ref, block, row0_ref, row1_ref, depth0_ref, depth1_ref, c10_ref, c11_ref,
-    early_ref, share_ref, edge_ref, den_out, vel_out, *rest,
+    early_ref, share_ref, edge_ref, late_ref, part_ref, den_out, vel_out, *rest,
     layers, rows, columns, depth_count, row_count,
 ):
     pieces = rest[:depth_count]
-    rowbuf, base, sbase, accum = rest[depth_count:]
+    rowbuf, srow, line_buffer, base, sbase, accum = rest[depth_count:]
     step = pl.program_id(0)
     steps = layers // 4
     own_tiles, spans = rows // SUB, columns // LANES
@@ -221,8 +288,8 @@
     lane = lax.broadcasted_iota(jnp.int32, (SUB, LANES), 1)
     first, last = lane == 0, lane == LANES - 1
     from_front = jnp.full((SUB, LANES), depth_odd, jnp.int32) == 1
-
     tiles = [(t, j) for j in range(spans) for t in range(own_tiles)]
+    rate, mix = constants(palette_ref, layers * depth_count)
 
     def tile_of(t, j):
         return slice(t * SUB, (t + 1) * SUB), slice(j * LANES, (j + 1) * LANES)
@@ -270,15 +337,11 @@
             for c in range(4):
                 sbase[slot, c, cells, :] = new[c]
 
-    def take_layer(z, slot):
-        for t, j in tiles:
-            for c in range(4):
-                sbase[slot, c, pl.ds(row_of(j, t * SUB), SUB), :] = early_ref[z, c, cells_of(t, j), :]
-        for side, kind, k, row, exists in (
-            (0, above, 1, -1, row_rank > 0), (1, below, 0, rows, row_rank < row_count - 1),
+    def edge_rows(z):
+        for side, kind, k, exists in (
+            (0, above, 1, row_rank > 0), (1, below, 0, row_rank < row_count - 1),
         ):
-            own_row = 0 if side == 0 else rows - 1
-            own_cells = pl.ds(own_row, spans, stride=rows)
+            own_cells = pl.ds(0 if side == 0 else rows - 1, spans, stride=rows)
 
             def halo(layer, n):
                 return [rowbuf[kind, c, layer, n] for c in range(4)]
@@ -290,18 +353,58 @@
                 share_ref[z, own_cells, :], 2, 1.0 if side == 0 else -1.0,
             )
             for c in range(4):
-                sbase[slot, c, line(own_row), :] = new[c]
-            left, right = [], []
-            for value in here:
-                before = jnp.where(sub == 0, 0.0, pltpu.roll(value, 1, 0))
-                after = jnp.where(sub == SUB - 1, 0.0, pltpu.roll(value, SUB - 1, 0))
-                left.append(pltpu.roll(jnp.where(last, before, value), 1, 1))
-                right.append(pltpu.roll(jnp.where(first, after, value), LANES - 1, 1))
+                srow[z, 1 + side, c] = new[c]
+            left, right = beside_in_lines(here, sub, first, last)
             up, down = (farther, own) if side == 0 else (own, farther)
             new, _ = advance(here, up, down, left, right, halo(z, k), halo(z + 2, k))
             inside = jnp.full((SUB, LANES), jnp.where(exists, 1, 0), jnp.int32) == 1
             for c in range(4):
-                sbase[slot, c, line(row), :] = jnp.where(inside, new[c], 0.0)
+                srow[z, 3 * side, c] = jnp.where(inside, new[c], 0.0)
+
+    def take_layer(z, slot):
+        for t, j in tiles:
+            for c in range(4):
+                sbase[slot, c, pl.ds(row_of(j, t * SUB), SUB), :] = early_ref[z, c, cells_of(t, j), :]
+        for n, row in enumerate((-1, 0, rows - 1, rows)):
+            for c in range(4):
+                sbase[slot, c, line(row), :] = srow[z, n, c]
+
+    def whole_layer(q, slots):
+        for t, j in tiles:
+            new, _ = advance(*neighbours(sbase, slots, t, j, spans, first, last))
+            there = tile_of(t, j)
+            den_out[(q,) + there] = new[0]
+            for c in range(3):
+                vel_out[(c, q) + there] = new[c + 1]
+            render(accum, cells_of(t, j), new, rate, mix)
+
+    def outer_rows(z, q):
+        def values(layer, row):
+            n = {-1: 0, 0: 1, rows - 1: 2, rows: 3}.get(row)
+            if n is not None:
+                return [srow[layer, n, c] for c in range(4)]
+            return [early_ref[layer, c, pl.ds(row, spans, stride=rows), :] for c in range(4)]
+
+        for t, j in tiles:
+            there = tile_of(t, j)
+            den_out[(q,) + there] = late_ref[z, 0, cells_of(t, j), :]
+            for c in range(3):
+                vel_out[(c, q) + there] = late_ref[z, c + 1, cells_of(t, j), :]
+        for n, row in enumerate((0, 1, rows - 2, rows - 1)):
+            here = values(z, row)
+            left, right = beside_in_lines(here, sub, first, last)
+            new, _ = advance(
+                here, values(z, row - 1), values(z, row + 1), left, right,
+                values(z - 1, row), values(z + 1, row),
+            )
+            render(accum, pl.ds(row, spans, stride=rows), new, rate, mix)
+            for c in range(4):
+                line_buffer[q, n, c] = new[c]
+            for j in range(spans):
+                there = (slice(row, row + 1), slice(j * LANES, (j + 1) * LANES))
+                den_out[(q,) + there] = line_buffer[q, n, 0, j : j + 1, :]
+                for c in range(3):
+                    vel_out[(c, q) + there] = line_buffer[q, n, c + 1, j : j + 1, :]
 
     @pl.when(step == 0)
     def _():
@@ -323,51 +426,52 @@
         for c in range(3):
             accum[c] = jnp.zeros((spans * rows, LANES), jnp.float32)
         accum[3] = jnp.ones((spans * rows, LANES), jnp.float32)
+
+        @pl.loop(0, layers // 2)
+        def _(pair):
+            edge_rows(2 * pair)
+            edge_rows(2 * pair + 1)
+
         outer_step(3, True)
         take_layer(0, 0)
         add_layer(0, 0, 1.0)
-
-    rate = -OPTICAL / (layers * depth_count) / math.log(2.0)
-    mix = [[0.5 * palette_ref[c, k] for k in range(4)] for c in range(3)]
-
-    def second_step(q):
+        take_layer(1, 1)
+        take_layer(2, 2)
+        whole_layer(0, (3, 0, 1))
+        whole_layer(1, (0, 1, 2))
         for t, j in tiles:
-            slots = ((q + 3) % 4, q, (q + 1) % 4)
-            new, _ = advance(*neighbours(sbase, slots, t, j, spans, first, last))
-            there = tile_of(t, j)
-            den_out[(q,) + there] = new[0]
+            pixels = cells_of(t, j)
+            through = accum[3, pixels, :]
+            inner = jnp.full((SUB, LANES), True)
+            if t == 0:
+                inner = sub >= 2
+            if t == own_tiles - 1:
+                inner = (sub < SUB - 2) if t > 0 else inner & (sub < SUB - 2)
             for c in range(3):
-                vel_out[(c, q) + there] = new[c + 1]
-            pixels = cells_of(t, j)
-            before = accum[3, pixels, :]
-            passed = before * jnp.exp2(rate * (new[0] * new[0]))
-            weight = before - passed
-            accum[3, pixels, :] = passed
-            for c in range(3):
-                mixed = (mix[c][0] * new[0] + mix[c][1] * new[1]) + (
-                    mix[c][2] * new[2] + mix[c][3] * new[3]
+                value = accum[c, pixels, :]
+                accum[c, pixels, :] = jnp.where(
+                    inner, value + through * part_ref[c, pixels, :], value
                 )
-                accum[c, pixels, :] = accum[c, pixels, :] + weight * jnp.tanh(mixed)
-
-    for q in range(3):
-        take_layer(4 * step + q + 1, q + 1)
-        if q == 2:
-
-            @pl.when(step == steps - 1)
-            def _():
-                outer_step(0, False)
-                add_layer(layers - 1, 3, -1.0)
-
-        second_step(q)
-
-    @pl.when(step < steps - 1)
+            accum[3, pixels, :] = jnp.where(inner, through * part_ref[3, pixels, :], through)
+        outer_rows(2, 2)
+        outer_rows(3, 3)
+
+    @pl.when((step > 0) & (step < steps - 1))
     def _():
-        take_layer(4 * step + 4, 0)
-
-    second_step(3)
+        for q in range(4):
+            outer_rows(4 * step + q, q)
 
     @pl.when(step == steps - 1)
     def _():
+        outer_rows(layers - 4, 0)
+        outer_rows(layers - 3, 1)
+        take_layer(layers - 3, 0)
+        take_layer(layers - 2, 1)
+        take_layer(layers - 1, 2)
+        outer_step(3, False)
+        add_layer(layers - 1, 2, -1.0)
+        whole_layer(2, (0, 1, 2))
+        whole_layer(3, (1, 2, 3))
         width = columns // depth_count
         per_piece = width // LANES
 
@@ -550,7 +654,7 @@
     spans = columns // LANES
     width = columns // depth_count
     line = 4 * width + LANES
-    assert spans == SUB and rows % SUB == 0 and width % LANES == 0 and layers % 4 == 0
+    assert spans == SUB and rows % SUB == 0 and width % LANES == 0 and layers % 4 == 0 and layers >= 8
     vmem = pl.BlockSpec(memory_space=pltpu.VMEM)
     smem = pl.BlockSpec(memory_space=pltpu.SMEM)
     f32 = jnp.float32
@@ -595,16 +699,19 @@
     depth0, depth1 = swap_depths(depth0, 0), swap_depths(depth1, 1)
     corner0, corner1 = swap_corners(corner0, 1, 0), swap_corners(corner1, 1, 1)
 
-    early, share, edge = pl.pallas_call(
-        functools.partial(interior_kernel, layers=layers, rows=rows, columns=columns),
+    early, share, edge, late, part = pl.pallas_call(
+        functools.partial(
+            interior_kernel, layers=layers, rows=rows, columns=columns, depth_count=depth_count
+        ),
         grid=(layers // 4,),
         out_shape=(
             pltpu.VMEM((layers, 4, spans * rows, LANES), f32),
             pltpu.VMEM((layers, spans * rows, LANES), f32),
-            pltpu.VMEM((layers, 2, 4, spans, LANES), f32),
+            local(layers, 2, 4, spans, LANES), local(layers, 4, spans * rows, LANES),
+            local(4, spans * rows, LANES),
         ),
-        in_specs=[vmem],
-        out_specs=(vmem,) * 3,
+        in_specs=[smem, vmem],
+        out_specs=(vmem,) * 5,
         scratch_shapes=[pltpu.VMEM((4, 4, spans * PITCH, LANES), f32)],
         cost_estimate=pl.CostEstimate(
             flops=80 * layers * rows * columns, bytes_accessed=16 * layers * rows * columns,
@@ -612,7 +719,7 @@
         ),
         name="interior",
         compiler_params=pltpu.CompilerParams(vmem_limit_bytes=24 << 20),
-    )(in_vmem(block))
+    )(palette, in_vmem(block))
 
     settled, moving, *parts = pl.pallas_call(
         functools.partial(
@@ -622,7 +729,7 @@
         grid=(layers // 4,),
         out_shape=(shape(layers, rows, columns), shape(3, layers, rows, columns))
         + (shape(rows, line),) * depth_count,
-        in_specs=[smem] + [vmem] * 10,
+        in_specs=[smem] + [vmem] * 12,
         out_specs=(
             pl.BlockSpec((4, rows, columns), lambda i: (i, 0, 0)),
             pl.BlockSpec((3, 4, rows, columns), lambda i: (0, i, 0, 0)),
@@ -630,6 +737,8 @@
         + (vmem,) * depth_count,
         scratch_shapes=[
             pltpu.VMEM((2, 4, layers + 2, 2, spans, LANES), f32),
+            pltpu.VMEM((layers, 4, 4, spans, LANES), f32),
+            pltpu.VMEM((4, 4, 4, spans, LANES), f32),
             pltpu.VMEM((3, 4, spans * PITCH, LANES), f32),
             pltpu.VMEM((4, 4, spans * PITCH, LANES), f32),
             pltpu.VMEM((4, spans * rows, LANES), f32),
@@ -640,7 +749,7 @@
         palette,
         *(
             in_vmem(x)
-            for x in (block, row0, row1, depth0, depth1, corner0, corner1, early, share, edge)
+            for x in (block, row0, row1, depth0, depth1, corner0, corner1, early, share, edge, late, part)
         ),
     )
 
@@ -674,6 +783,4 @@
 def solution(mesh):
     in_specs = (P("depth", "row", None), P(None, "depth", "row", None), P())
     out_specs = (P(None, "row", "depth"), P("depth", "row", None), P(None, "depth", "row", None))
-    return jax.shard_map(
-        compute, mesh=mesh, in_specs=in_specs, out_specs=out_specs, check_vma=False
-    )
+    return jax.shard_map(compute, mesh=mesh, in_specs=in_specs, out_specs=out_specs, check_vma=False)

time: 50.2 us -> 49.8 us (level)
  the two profiles are of different devices: /device:TPU:5 before, /device:TPU:1 now
where the time goes in v1:
time: 49.8 us; the launch traced here: 48.9 us
  starting transfers between devices  22.9 us (46%)
  Pallas kernels  17.8 us (36%)
  waiting for transfers between devices  7.48 us (15%)
  between operations  0.77 us (2%)
    ppermute x4, starting transfers between devices, swap_rows(): return lax.ppermute(array, 'row', row_pairs(kind, lax.axis_size('row')))  8.36 us
    pallas_call x1, Pallas kernels, compute(): pl.pallas_call(functools.partial(settle_kernel, layers=layers, rows=rows,...  7.05 us
    pallas_call x1, Pallas kernels, compute(): pl.pallas_call(functools.partial(interior_kernel, layers=layers, rows=row...  7.01 us
    ppermute x2, starting transfers between devices, swap_corners(): return lax.ppermute(array, AXES, pairs)  6.38 us
    ppermute x3, starting transfers between devices, compute(): lax.ppermute(part, 'depth', [(i, i ^ k) for i in range(depth_count)])  4.95 us
    ppermute x3, waiting for transfers between devices, compute(): lax.ppermute(part, 'depth', [(i, i ^ k) for i in range(depth_count)])  4.25 us
    ppermute x4, waiting for transfers between devices, swap_rows(): return lax.ppermute(array, 'row', row_pairs(kind, lax.axis_size('row')))  3.22 us
    ppermute x2, starting transfers between devices, swap_depths(): return lax.ppermute(array, 'depth', row_pairs(kind, lax.axis_size('depth')))  3.16 us
  transfers between devices with their start and end apart: 11, of which 5 were waited for; matrix products, arithmetic and copies ran while one was open for 0% of the time, Pallas kernels for 14%

profile of v1, /device:TPU:1, one launch (start us, length us, event | category | flops | bytes accessed | tf_op | source)
XLA Modules:
  0.0 48.9 jit_solution(18087905322174599889)
XLA Ops:
  0.6 2.4 %pack.1 = (f32[4,16,16,1024]{3,2,1,0:T(8,128)S(1)}, f32[4,16,2,8,128]{4,3,2,1,0:T(8,128)S(1)}, f32[4,16,2,8,128]{4,3,2,1,0:T(8,128)S(1)}, f32[4,8,128]{2,1,0:T(8,128)S(1)}, f32[4,8,128]{2,1,0:T(8,128)S(1)}) custom-call(f32[16,16,1024]{2,1,0:T(8,128)} %den_ref.1, f32[3,16,16,1024]{3,2,1,0:T(8,128)} %vel_ref.1), custom_call_target="tpu_custom_call" | custom-call | tf_op jit(solution)/shard_map/pack/pallas_call | solution.py:674
  3.1 0.1 collective-permute-start
  3.2 1.9 %collective-permute-done.row0_ref = f32[4,16,2,8,128]{4,3,2,1,0:T(8,128)S(1)} collective-permute-done((f32[4,16,2,8,128]{4,3,2,1,0:T(8,128)S(1)}, f32[4,16,2,8,128]{4,3,2,1,0:T(8,128)S(1)}, u32[]{:S(2)}, u32[]{:S(2)}) %collective-permute-start) | collective-permute-done | bytes 524320 | tf_op jit(solution)/shard_map/ppermute | solution.py:33
  5.1 0.1 pack_depth.1
  5.1 2.5 %collective-permute-start.2 = (f32[4,264,128]{2,1,0:T(8,128)S(1)}, f32[4,264,128]{2,1,0:T(8,128)S(1)}, u32[]{:S(2)}, u32[]{:S(2)}) collective-permute-start(f32[4,264,128]{2,1,0:T(8,128)S(1)} %get-tuple-element.27), channel_id=1, source_target_pairs={{0,1},{1,0},{2,3},{3,2},{4,5},{5,4},{6,7},{7,6},{8,9},{9,8},{10,11... | collective-permute-start | bytes 1622024 | tf_op jit(solution)/shard_map/ppermute | solution.py:37
  7.6 0.7 %collective-permute-start.3 = (f32[4,264,128]{2,1,0:T(8,128)S(1)}, f32[4,264,128]{2,1,0:T(8,128)S(1)}, u32[]{:S(2)}, u32[]{:S(2)}) collective-permute-start(f32[4,264,128]{2,1,0:T(8,128)S(1)} %get-tuple-element.28), channel_id=1, source_target_pairs={{1,2},{2,1},{5,6},{6,5},{9,10},{10,9},{13,14},{14,13},{17,18},{18,... | collective-permute-start | bytes 1622024 | tf_op jit(solution)/shard_map/ppermute | solution.py:37
  8.3 3.7 %collective-permute-start.1 = (f32[4,16,2,8,128]{4,3,2,1,0:T(8,128)S(1)}, f32[4,16,2,8,128]{4,3,2,1,0:T(8,128)S(1)}, u32[]{:S(2)}, u32[]{:S(2)}) collective-permute-start(f32[4,16,2,8,128]{4,3,2,1,0:T(8,128)S(1)} %get-tuple-element.26), channel_id=1, source_target_pairs={{4,8},{8,4},{12,16},{16,12},{20,24},{24,20},{5,9},{9,5},{13,17},{1... | collective-permute-start | bytes 1572872 | tf_op jit(solution)/shard_map/ppermute | solution.py:33
  12.0 5.7 %collective-permute-start.4 = (f32[4,8,128]{2,1,0:T(8,128)S(1)}, f32[4,8,128]{2,1,0:T(8,128)S(1)}, u32[]{:S(2)}, u32[]{:S(2)}) collective-permute-start(f32[4,8,128]{2,1,0:T(8,128)S(1)} %get-tuple-element.29), channel_id=1, source_target_pairs={{4,9},{5,8},{6,11},{7,10},{8,5},{9,4},{10,7},{11,6},{12,17},{13,16... | collective-permute-start | bytes 49160 | tf_op jit(solution)/shard_map/ppermute | solution.py:47
  17.7 0.7 %collective-permute-start.5 = (f32[4,8,128]{2,1,0:T(8,128)S(1)}, f32[4,8,128]{2,1,0:T(8,128)S(1)}, u32[]{:S(2)}, u32[]{:S(2)}) collective-permute-start(f32[4,8,128]{2,1,0:T(8,128)S(1)} %get-tuple-element.30), channel_id=1, source_target_pairs={{5,10},{6,9},{9,6},{10,5},{13,18},{14,17},{17,14},{18,13},{21,26},... | collective-permute-start | bytes 49160 | tf_op jit(solution)/shard_map/ppermute | solution.py:47
  18.4 7.0 %interior.1 = (f32[16,4,128,128]{3,2,1,0:T(8,128)S(1)}, f32[16,128,128]{2,1,0:T(8,128)S(1)}, f32[16,2,4,8,128]{4,3,2,1,0:T(8,128)S(1)}, f32[16,4,128,128]{3,2,1,0:T(8,128)S(1)}, f32[4,128,128]{2,1,0:T(8,128)S(1)}) custom-call(f32[3,4]{1,0:T(4,128)S(1)} %copy-done, f32[4,16,16,1024]{3,2,1,0:T(8,128)S(1)} %get-tuple-element.24.block), custom_call_target="tpu_custom_call" | custom-call | flops 20971520 | bytes 4194304 | tf_op jit(solution)/shard_map/interior/pallas_call | solution.py:702
  25.4 0.0 collective-permute-done.1.row1_ref
  25.4 0.0 collective-permute-done.2.depth0_ref
  25.5 7.1 %settle.1 = (f32[16,16,1024]{2,1,0:T(8,128)}, f32[3,16,16,1024]{3,2,1,0:T(8,128)}, f32[16,1152]{1,0:T(8,128)S(1)}, f32[16,1152]{1,0:T(8,128)S(1)}, f32[16,1152]{1,0:T(8,128)S(1)}, /*index=5*/f32[16,1152]{1,0:T(8,128)S(1)}) custom-call(f32[3,4]{1,0:T(4,128)S(1)} %copy-done, f32[4,16,16,1024]{3,2,1,0:T(8,128)S(1)} %get-tuple-element.24.block, ...), custom_call_target="tpu_custom_call" | custom-call | tf_op jit(solution)/shard_map/settle/pallas_call | solution.py:724
  32.5 2.4 %collective-permute-start.6 = (f32[16,1152]{1,0:T(8,128)S(1)}, f32[16,1152]{1,0:T(8,128)S(1)}, u32[]{:S(2)}, u32[]{:S(2)}) collective-permute-start(f32[16,1152]{1,0:T(8,128)S(1)} %get-tuple-element.37), channel_id=1, source_target_pairs={{0,2},{1,3},{2,0},{3,1},{4,6},{5,7},{6,4},{7,5},{8,10},{9,11},{10,... | collective-permute-start | bytes 221192 | tf_op jit(solution)/shard_map/ppermute | solution.py:757
  35.0 0.4 collective-permute-start.7
  35.4 2.1 %collective-permute-start.8 = (f32[16,1152]{1,0:T(8,128)S(1)}, f32[16,1152]{1,0:T(8,128)S(1)}, u32[]{:S(2)}, u32[]{:S(2)}) collective-permute-start(f32[16,1152]{1,0:T(8,128)S(1)} %get-tuple-element.39), channel_id=1, source_target_pairs={{0,3},{1,2},{2,1},{3,0},{4,7},{5,6},{6,5},{7,4},{8,11},{9,10},{10,... | collective-permute-start | bytes 221192 | tf_op jit(solution)/shard_map/ppermute | solution.py:757
  37.5 0.1 collective-permute-done.6.refs_1_
  37.6 2.0 %collective-permute-done.7.refs_2_ = f32[16,1152]{1,0:T(8,128)S(1)} collective-permute-done((f32[16,1152]{1,0:T(8,128)S(1)}, f32[16,1152]{1,0:T(8,128)S(1)}, u32[]{:S(2)}, u32[]{:S(2)}) %collective-permute-start.7) | collective-permute-done | bytes 73760 | tf_op jit(solution)/shard_map/ppermute | solution.py:757
  39.6 2.1 %collective-permute-done.8.refs_3_ = f32[16,1152]{1,0:T(8,128)S(1)} collective-permute-done((f32[16,1152]{1,0:T(8,128)S(1)}, f32[16,1152]{1,0:T(8,128)S(1)}, u32[]{:S(2)}, u32[]{:S(2)}) %collective-permute-start.8) | collective-permute-done | bytes 73760 | tf_op jit(solution)/shard_map/ppermute | solution.py:757
  41.7 0.2 over.1
  41.9 0.1 collective-permute-start.9
  42.0 4.6 %collective-permute-start.10 = (f32[2,1152]{1,0:T(2,128)S(1)}, f32[2,1152]{1,0:T(2,128)S(1)}, u32[]{:S(2)}, u32[]{:S(2)}) collective-permute-start(f32[2,1152]{1,0:T(2,128)S(1)} %get-tuple-element.42), channel_id=1, source_target_pairs={{4,8},{8,4},{12,16},{16,12},{20,24},{24,20},{5,9},{9,5},{13,17},{1... | collective-permute-start | bytes 27656 | tf_op jit(solution)/shard_map/ppermute | solution.py:33
  46.5 1.3 %collective-permute-done.10.swap1_ref = f32[2,1152]{1,0:T(2,128)S(1)} collective-permute-done((f32[2,1152]{1,0:T(2,128)S(1)}, f32[2,1152]{1,0:T(2,128)S(1)}, u32[]{:S(2)}, u32[]{:S(2)}) %collective-permute-start.10) | collective-permute-done | bytes 9248 | tf_op jit(solution)/shard_map/ppermute | solution.py:33
  47.9 1.1 %bilateral.1 = f32[4,16,256]{2,1,0:T(8,128)} custom-call(f32[16,1152]{1,0:T(8,128)S(1)} %get-tuple-element.40.picture_ref, f32[2,1152]{1,0:T(2,128)S(1)} %collective-permute-done.9.swap0_ref, f32[2,1152]{1,0:T(2,128)S(1)} %collective-permute-done.10.swap1_ref), custom_call_target="tpu_custom_call" | custom-call | tf_op jit(solution)/shard_map/bilateral/pallas_call | solution.py:770
  (6 shorter events, 0.0 us)
Async XLA Ops:
  0.6 17.8 %copy-start = (f32[3,4]{1,0:T(4,128)S(1)}, f32[3,4]{1,0:T(4,128)}, u32[]{:S(2)}) copy-start(f32[3,4]{1,0:T(4,128)} %palette_ref.3) | copy-start | bytes 148
  3.1 2.0 %collective-permute-start = (f32[4,16,2,8,128]{4,3,2,1,0:T(8,128)S(1)}, f32[4,16,2,8,128]{4,3,2,1,0:T(8,128)S(1)}, u32[]{:S(2)}, u32[]{:S(2)}) collective-permute-start(f32[4,16,2,8,128]{4,3,2,1,0:T(8,128)S(1)} %get-tuple-element.25), channel_id=1, source_target_pairs={{0,4},{4,0},{8,12},{12,8},{16,20},{20,16},{24,28},{28,24},{1,5},{5... | collective-permute-start | bytes 1572872 | tf_op jit(solution)/shard_map/ppermute | solution.py:33
  5.1 20.3 %collective-permute-start.2 = (f32[4,264,128]{2,1,0:T(8,128)S(1)}, f32[4,264,128]{2,1,0:T(8,128)S(1)}, u32[]{:S(2)}, u32[]{:S(2)}) collective-permute-start(f32[4,264,128]{2,1,0:T(8,128)S(1)} %get-tuple-element.27), channel_id=1, source_target_pairs={{0,1},{1,0},{2,3},{3,2},{4,5},{5,4},{6,7},{7,6},{8,9},{9,8},{10,11... | collective-permute-start | bytes 1622024 | tf_op jit(solution)/shard_map/ppermute | solution.py:37
  7.6 17.8 %collective-permute-start.3 = (f32[4,264,128]{2,1,0:T(8,128)S(1)}, f32[4,264,128]{2,1,0:T(8,128)S(1)}, u32[]{:S(2)}, u32[]{:S(2)}) collective-permute-start(f32[4,264,128]{2,1,0:T(8,128)S(1)} %get-tuple-element.28), channel_id=1, source_target_pairs={{1,2},{2,1},{5,6},{6,5},{9,10},{10,9},{13,14},{14,13},{17,18},{18,... | collective-permute-start | bytes 1622024 | tf_op jit(solution)/shard_map/ppermute | solution.py:37
  8.3 17.1 %collective-permute-start.1 = (f32[4,16,2,8,128]{4,3,2,1,0:T(8,128)S(1)}, f32[4,16,2,8,128]{4,3,2,1,0:T(8,128)S(1)}, u32[]{:S(2)}, u32[]{:S(2)}) collective-permute-start(f32[4,16,2,8,128]{4,3,2,1,0:T(8,128)S(1)} %get-tuple-element.26), channel_id=1, source_target_pairs={{4,8},{8,4},{12,16},{16,12},{20,24},{24,20},{5,9},{9,5},{13,17},{1... | collective-permute-start | bytes 1572872 | tf_op jit(solution)/shard_map/ppermute | solution.py:33
  12.0 13.4 %collective-permute-start.4 = (f32[4,8,128]{2,1,0:T(8,128)S(1)}, f32[4,8,128]{2,1,0:T(8,128)S(1)}, u32[]{:S(2)}, u32[]{:S(2)}) collective-permute-start(f32[4,8,128]{2,1,0:T(8,128)S(1)} %get-tuple-element.29), channel_id=1, source_target_pairs={{4,9},{5,8},{6,11},{7,10},{8,5},{9,4},{10,7},{11,6},{12,17},{13,16... | collective-permute-start | bytes 49160 | tf_op jit(solution)/shard_map/ppermute | solution.py:47
  17.7 7.7 %collective-permute-start.5 = (f32[4,8,128]{2,1,0:T(8,128)S(1)}, f32[4,8,128]{2,1,0:T(8,128)S(1)}, u32[]{:S(2)}, u32[]{:S(2)}) collective-permute-start(f32[4,8,128]{2,1,0:T(8,128)S(1)} %get-tuple-element.30), channel_id=1, source_target_pairs={{5,10},{6,9},{9,6},{10,5},{13,18},{14,17},{17,14},{18,13},{21,26},... | collective-permute-start | bytes 49160 | tf_op jit(solution)/shard_map/ppermute | solution.py:47
  32.5 5.1 %collective-permute-start.6 = (f32[16,1152]{1,0:T(8,128)S(1)}, f32[16,1152]{1,0:T(8,128)S(1)}, u32[]{:S(2)}, u32[]{:S(2)}) collective-permute-start(f32[16,1152]{1,0:T(8,128)S(1)} %get-tuple-element.37), channel_id=1, source_target_pairs={{0,2},{1,3},{2,0},{3,1},{4,6},{5,7},{6,4},{7,5},{8,10},{9,11},{10,... | collective-permute-start | bytes 221192 | tf_op jit(solution)/shard_map/ppermute | solution.py:757
  35.0 4.6 %collective-permute-start.7 = (f32[16,1152]{1,0:T(8,128)S(1)}, f32[16,1152]{1,0:T(8,128)S(1)}, u32[]{:S(2)}, u32[]{:S(2)}) collective-permute-start(f32[16,1152]{1,0:T(8,128)S(1)} %get-tuple-element.38), channel_id=1, source_target_pairs={{0,1},{1,0},{2,3},{3,2},{4,5},{5,4},{6,7},{7,6},{8,9},{9,8},{10,11... | collective-permute-start | bytes 221192 | tf_op jit(solution)/shard_map/ppermute | solution.py:757
  35.4 6.3 %collective-permute-start.8 = (f32[16,1152]{1,0:T(8,128)S(1)}, f32[16,1152]{1,0:T(8,128)S(1)}, u32[]{:S(2)}, u32[]{:S(2)}) collective-permute-start(f32[16,1152]{1,0:T(8,128)S(1)} %get-tuple-element.39), channel_id=1, source_target_pairs={{0,3},{1,2},{2,1},{3,0},{4,7},{5,6},{6,5},{7,4},{8,11},{9,10},{10,... | collective-permute-start | bytes 221192 | tf_op jit(solution)/shard_map/ppermute | solution.py:757
  41.9 4.6 %collective-permute-start.9 = (f32[2,1152]{1,0:T(2,128)S(1)}, f32[2,1152]{1,0:T(2,128)S(1)}, u32[]{:S(2)}, u32[]{:S(2)}) collective-permute-start(f32[2,1152]{1,0:T(2,128)S(1)} %get-tuple-element.41), channel_id=1, source_target_pairs={{0,4},{4,0},{8,12},{12,8},{16,20},{20,16},{24,28},{28,24},{1,5},{5... | collective-permute-start | bytes 27656 | tf_op jit(solution)/shard_map/ppermute | solution.py:33
  42.0 5.9 %collective-permute-start.10 = (f32[2,1152]{1,0:T(2,128)S(1)}, f32[2,1152]{1,0:T(2,128)S(1)}, u32[]{:S(2)}, u32[]{:S(2)}) collective-permute-start(f32[2,1152]{1,0:T(2,128)S(1)} %get-tuple-element.42), channel_id=1, source_target_pairs={{4,8},{8,4},{12,16},{16,12},{20,24},{24,20},{5,9},{9,5},{13,17},{1... | collective-permute-start | bytes 27656 | tf_op jit(solution)/shard_map/ppermute | solution.py:33

commit v2 on v1

--- a/solution.py
+++ b/solution.py
@@ -273,13 +273,11 @@
 
 def settle_kernel(
     palette_ref, block, row0_ref, row1_ref, depth0_ref, depth1_ref, c10_ref, c11_ref,
-    early_ref, share_ref, edge_ref, late_ref, part_ref, den_out, vel_out, *rest,
+    early_ref, share_ref, edge_ref, part_ref, whole_ref, lines_ref, *rest,
     layers, rows, columns, depth_count, row_count,
 ):
     pieces = rest[:depth_count]
-    rowbuf, srow, line_buffer, base, sbase, accum = rest[depth_count:]
-    step = pl.program_id(0)
-    steps = layers // 4
+    rowbuf, srow, base, sbase, accum = rest[depth_count:]
     own_tiles, spans = rows // SUB, columns // LANES
     row_rank, depth_rank = lax.axis_index("row"), lax.axis_index("depth")
     row_odd, depth_odd = lax.rem(row_rank, 2), lax.rem(depth_rank, 2)
@@ -369,27 +367,20 @@
             for c in range(4):
                 sbase[slot, c, line(row), :] = srow[z, n, c]
 
-    def whole_layer(q, slots):
+    def whole_layer(n, slots):
         for t, j in tiles:
             new, _ = advance(*neighbours(sbase, slots, t, j, spans, first, last))
-            there = tile_of(t, j)
-            den_out[(q,) + there] = new[0]
-            for c in range(3):
-                vel_out[(c, q) + there] = new[c + 1]
+            for c in range(4):
+                whole_ref[n, c, cells_of(t, j), :] = new[c]
             render(accum, cells_of(t, j), new, rate, mix)
 
-    def outer_rows(z, q):
+    def outer_rows(z):
         def values(layer, row):
             n = {-1: 0, 0: 1, rows - 1: 2, rows: 3}.get(row)
             if n is not None:
                 return [srow[layer, n, c] for c in range(4)]
             return [early_ref[layer, c, pl.ds(row, spans, stride=rows), :] for c in range(4)]
 
-        for t, j in tiles:
-            there = tile_of(t, j)
-            den_out[(q,) + there] = late_ref[z, 0, cells_of(t, j), :]
-            for c in range(3):
-                vel_out[(c, q) + there] = late_ref[z, c + 1, cells_of(t, j), :]
         for n, row in enumerate((0, 1, rows - 2, rows - 1)):
             here = values(z, row)
             left, right = beside_in_lines(here, sub, first, last)
@@ -399,106 +390,135 @@
             )
             render(accum, pl.ds(row, spans, stride=rows), new, rate, mix)
             for c in range(4):
-                line_buffer[q, n, c] = new[c]
+                lines_ref[z, n, c] = new[c]
+
+    for kind, source in ((0, row0_ref), (1, row1_ref)):
+        for c in range(4):
+            for z in range(layers):
+                for k in range(2):
+                    rowbuf[kind, c, z + 1, k] = source[c, z, k]
+    beside = pl.ds(2 * spans * rows, spans)
+    corners = (
+        (0, 0, lambda c: depth0_ref[c, beside, :]), (0, 1, lambda c: depth1_ref[c, beside, :]),
+        (1, 0, lambda c: c10_ref[c]), (1, 1, lambda c: c11_ref[c]),
+    )
+    for row_kind, depth_kind, source in corners:
+        is_above = row_odd if row_kind == 0 else 1 - row_odd
+        is_front = depth_odd if depth_kind == 0 else 1 - depth_odd
+        for c in range(4):
+            rowbuf[row_kind, c, (1 - is_front) * (layers + 1), is_above] = source(c)
+    for c in range(3):
+        accum[c] = jnp.zeros((spans * rows, LANES), jnp.float32)
+    accum[3] = jnp.ones((spans * rows, LANES), jnp.float32)
+
+    @pl.loop(0, layers // 2)
+    def _(pair):
+        edge_rows(2 * pair)
+        edge_rows(2 * pair + 1)
+
+    outer_step(3, True)
+    take_layer(0, 0)
+    add_layer(0, 0, 1.0)
+    take_layer(1, 1)
+    take_layer(2, 2)
+    whole_layer(0, (3, 0, 1))
+    whole_layer(1, (0, 1, 2))
+    for t, j in tiles:
+        pixels = cells_of(t, j)
+        through = accum[3, pixels, :]
+        inner = jnp.full((SUB, LANES), True)
+        if t == 0:
+            inner = sub >= 2
+        if t == own_tiles - 1:
+            inner = (sub < SUB - 2) if t > 0 else inner & (sub < SUB - 2)
+        for c in range(3):
+            value = accum[c, pixels, :]
+            accum[c, pixels, :] = jnp.where(inner, value + through * part_ref[c, pixels, :], value)
+        accum[3, pixels, :] = jnp.where(inner, through * part_ref[3, pixels, :], through)
+
+    @pl.loop(0, (layers - 4) // 2)
+    def _(pair):
+        outer_rows(2 * pair + 2)
+        outer_rows(2 * pair + 3)
+
+    take_layer(layers - 3, 0)
+    take_layer(layers - 2, 1)
+    take_layer(layers - 1, 2)
+    outer_step(3, False)
+    add_layer(layers - 1, 2, -1.0)
+    whole_layer(2, (0, 1, 2))
+    whole_layer(3, (1, 2, 3))
+
+    width = columns // depth_count
+    per_piece = width // LANES
+
+    def channels(j, t):
+        pixels = pl.ds(j * rows + t * SUB, SUB)
+        through = accum[3, pixels, :]
+        return [0.5 * (accum[c, pixels, :] + (1.0 - through)) for c in range(3)] + [through]
+
+    for k in range(depth_count):
+        piece = depth_rank ^ k
+        start = piece * per_piece
+        for t in range(own_tiles):
+            r = slice(t * SUB, (t + 1) * SUB)
+            for jj in range(per_piece):
+                values = channels(start + jj, t)
+                for c in range(4):
+                    pieces[k][r, c * width + jj * LANES : c * width + (jj + 1) * LANES] = (
+                        values[c]
+                    )
+            before = channels(jnp.maximum(start - 1, 0), t)
+            after = channels(jnp.minimum(start + per_piece, spans - 1), t)
+            edge = jnp.zeros((SUB, LANES), jnp.float32)
+            for c in range(4):
+                for values, low in ((before, 4 * c), (after, 4 * c + 2)):
+                    turned = pltpu.roll(values[c], (4 * c + 2) % LANES, 1)
+                    edge = jnp.where((lane >= low) & (lane < low + 2), turned, edge)
+            pieces[k][r, 4 * width : 4 * width + LANES] = edge
+
+
+def assemble_kernel(whole_ref, lines_ref, late_ref, den_out, vel_out, *, layers, rows, columns):
+    step = pl.program_id(0)
+    own_tiles, spans = rows // SUB, columns // LANES
+
+    def put(q, c, there, value):
+        if c == 0:
+            den_out[(q,) + there] = value
+        else:
+            vel_out[(c - 1, q) + there] = value
+
+    def copy_layer(source, z, q):
+        for j in range(spans):
+            lanes = slice(j * LANES, (j + 1) * LANES)
+            for c in range(4):
+                for t in range(own_tiles):
+                    value = source[z, c, pl.ds(j * rows + t * SUB, SUB), :]
+                    put(q, c, (slice(t * SUB, (t + 1) * SUB), lanes), value)
+
+    def inner_layer(z, q):
+        copy_layer(late_ref, z, q)
+        for n, row in enumerate((0, 1, rows - 2, rows - 1)):
             for j in range(spans):
-                there = (slice(row, row + 1), slice(j * LANES, (j + 1) * LANES))
-                den_out[(q,) + there] = line_buffer[q, n, 0, j : j + 1, :]
-                for c in range(3):
-                    vel_out[(c, q) + there] = line_buffer[q, n, c + 1, j : j + 1, :]
-
-    @pl.when(step == 0)
-    def _():
-        for kind, source in ((0, row0_ref), (1, row1_ref)):
-            for c in range(4):
-                for z in range(layers):
-                    for k in range(2):
-                        rowbuf[kind, c, z + 1, k] = source[c, z, k]
-        beside = pl.ds(2 * spans * rows, spans)
-        corners = (
-            (0, 0, lambda c: depth0_ref[c, beside, :]), (0, 1, lambda c: depth1_ref[c, beside, :]),
-            (1, 0, lambda c: c10_ref[c]), (1, 1, lambda c: c11_ref[c]),
-        )
-        for row_kind, depth_kind, source in corners:
-            is_above = row_odd if row_kind == 0 else 1 - row_odd
-            is_front = depth_odd if depth_kind == 0 else 1 - depth_odd
-            for c in range(4):
-                rowbuf[row_kind, c, (1 - is_front) * (layers + 1), is_above] = source(c)
-        for c in range(3):
-            accum[c] = jnp.zeros((spans * rows, LANES), jnp.float32)
-        accum[3] = jnp.ones((spans * rows, LANES), jnp.float32)
-
-        @pl.loop(0, layers // 2)
-        def _(pair):
-            edge_rows(2 * pair)
-            edge_rows(2 * pair + 1)
-
-        outer_step(3, True)
-        take_layer(0, 0)
-        add_layer(0, 0, 1.0)
-        take_layer(1, 1)
-        take_layer(2, 2)
-        whole_layer(0, (3, 0, 1))
-        whole_layer(1, (0, 1, 2))
-        for t, j in tiles:
-            pixels = cells_of(t, j)
-            through = accum[3, pixels, :]
-            inner = jnp.full((SUB, LANES), True)
-            if t == 0:
-                inner = sub >= 2
-            if t == own_tiles - 1:
-                inner = (sub < SUB - 2) if t > 0 else inner & (sub < SUB - 2)
-            for c in range(3):
-                value = accum[c, pixels, :]
-                accum[c, pixels, :] = jnp.where(
-                    inner, value + through * part_ref[c, pixels, :], value
-                )
-            accum[3, pixels, :] = jnp.where(inner, through * part_ref[3, pixels, :], through)
-        outer_rows(2, 2)
-        outer_rows(3, 3)
-
-    @pl.when((step > 0) & (step < steps - 1))
-    def _():
-        for q in range(4):
-            outer_rows(4 * step + q, q)
-
-    @pl.when(step == steps - 1)
-    def _():
-        outer_rows(layers - 4, 0)
-        outer_rows(layers - 3, 1)
-        take_layer(layers - 3, 0)
-        take_layer(layers - 2, 1)
-        take_layer(layers - 1, 2)
-        outer_step(3, False)
-        add_layer(layers - 1, 2, -1.0)
-        whole_layer(2, (0, 1, 2))
-        whole_layer(3, (1, 2, 3))
-        width = columns // depth_count
-        per_piece = width // LANES
-
-        def channels(j, t):
-            pixels = pl.ds(j * rows + t * SUB, SUB)
-            through = accum[3, pixels, :]
-            return [0.5 * (accum[c, pixels, :] + (1.0 - through)) for c in range(3)] + [through]
-
-        for k in range(depth_count):
-            piece = depth_rank ^ k
-            start = piece * per_piece
-            for t in range(own_tiles):
-                r = slice(t * SUB, (t + 1) * SUB)
-                for jj in range(per_piece):
-                    values = channels(start + jj, t)
-                    for c in range(4):
-                        pieces[k][r, c * width + jj * LANES : c * width + (jj + 1) * LANES] = (
-                            values[c]
-                        )
-                before = channels(jnp.maximum(start - 1, 0), t)
-                after = channels(jnp.minimum(start + per_piece, spans - 1), t)
-                edge = jnp.zeros((SUB, LANES), jnp.float32)
                 for c in range(4):
-                    for values, low in ((before, 4 * c), (after, 4 * c + 2)):
-                        turned = pltpu.roll(values[c], (4 * c + 2) % LANES, 1)
-                        edge = jnp.where((lane >= low) & (lane < low + 2), turned, edge)
-                pieces[k][r, 4 * width : 4 * width + LANES] = edge
+                    there = (slice(row, row + 1), slice(j * LANES, (j + 1) * LANES))
+                    put(q, c, there, lines_ref[z, n, c, j : j + 1, :])
+
+    for q in range(4):
+        if q < 2:
+
+            @pl.when(step == 0)
+            def _():
+                copy_layer(whole_ref, q, q)
+
+            pl.when(step > 0)(functools.partial(inner_layer, 4 * step + q, q))
+        else:
+
+            @pl.when(step == layers // 4 - 1)
+            def _():
+                copy_layer(whole_ref, q, q)
+
+            pl.when(step < layers // 4 - 1)(functools.partial(inner_layer, 4 * step + q, q))
 
 
 def transfer_order(count):
@@ -721,42 +741,51 @@
         compiler_params=pltpu.CompilerParams(vmem_limit_bytes=24 << 20),
     )(palette, in_vmem(block))
 
-    settled, moving, *parts = pl.pallas_call(
+    whole, lines, *parts = pl.pallas_call(
         functools.partial(
             settle_kernel, layers=layers, rows=rows, columns=columns,
             depth_count=depth_count, row_count=row_count,
         ),
-        grid=(layers // 4,),
-        out_shape=(shape(layers, rows, columns), shape(3, layers, rows, columns))
-        + (shape(rows, line),) * depth_count,
-        in_specs=[smem] + [vmem] * 12,
-        out_specs=(
-            pl.BlockSpec((4, rows, columns), lambda i: (i, 0, 0)),
-            pl.BlockSpec((3, 4, rows, columns), lambda i: (0, i, 0, 0)),
-        )
-        + (vmem,) * depth_count,
+        out_shape=(local(4, 4, spans * rows, LANES), local(layers, 4, 4, spans, LANES))
+        + (local(rows, line),) * depth_count,
+        in_specs=[smem] + [vmem] * 11,
+        out_specs=(vmem,) * (2 + depth_count),
         scratch_shapes=[
             pltpu.VMEM((2, 4, layers + 2, 2, spans, LANES), f32),
             pltpu.VMEM((layers, 4, 4, spans, LANES), f32),
-            pltpu.VMEM((4, 4, 4, spans, LANES), f32),
             pltpu.VMEM((3, 4, spans * PITCH, LANES), f32),
             pltpu.VMEM((4, 4, spans * PITCH, LANES), f32),
             pltpu.VMEM((4, spans * rows, LANES), f32),
         ],
         name="settle",
-        compiler_params=pltpu.CompilerParams(vmem_limit_bytes=32 << 20),
+        compiler_params=params(24),
     )(
         palette,
         *(
             in_vmem(x)
-            for x in (block, row0, row1, depth0, depth1, corner0, corner1, early, share, edge, late, part)
+            for x in (block, row0, row1, depth0, depth1, corner0, corner1, early, share, edge, part)
         ),
     )
 
-    parts = [
-        lax.ppermute(part, "depth", [(i, i ^ k) for i in range(depth_count)]) if k else part
-        for k, part in enumerate(parts)
-    ]
+    settled, moving = pl.pallas_call(
+        functools.partial(assemble_kernel, layers=layers, rows=rows, columns=columns),
+        grid=(layers // 4,),
+        out_shape=(shape(layers, rows, columns), shape(3, layers, rows, columns)),
+        in_specs=[vmem] * 3,
+        out_specs=(
+            pl.BlockSpec((4, rows, columns), lambda i: (i, 0, 0)),
+            pl.BlockSpec((3, 4, rows, columns), lambda i: (0, i, 0, 0)),
+        ),
+        cost_estimate=pl.CostEstimate(
+            flops=20 * layers * rows * columns, bytes_accessed=16 * layers * rows * columns,
+            transcendentals=0,
+        ),
+        name="assemble",
+        compiler_params=params(16),
+    )(in_vmem(whole), in_vmem(lines), in_vmem(late))
+
+    for k in range(1, depth_count):
+        parts[k] = lax.ppermute(parts[k], "depth", [(i, i ^ k) for i in range(depth_count)])
     composed, swap0, swap1 = pl.pallas_call(
         functools.partial(over_kernel, count=depth_count, width=width),
         out_shape=(shape(rows, line), shape(2, line), shape(2, line)),

time: 49.8 us -> 48.4 us (0.972); the launches traced: 48.9 us -> 48.2 us
  waiting for transfers between devices: 7.48 us -> 6.16 us
  Pallas kernels: 17.8 us -> 18.3 us
    pallas_call x0 -> x1, Pallas kernels: none -> 2.75 us  [compute(): pl.pallas_call(functools.partial(assemble_kernel, layers=layers, rows=row...]
    pallas_call x1, Pallas kernels: 7.05 us -> 4.82 us  [compute(): pl.pallas_call(functools.partial(settle_kernel, layers=layers, rows=rows,...]
    ppermute x4, waiting for transfers between devices: 3.22 us -> 1.9 us  [swap_rows(): return lax.ppermute(array, 'row', row_pairs(kind, lax.axis_size('row')))]
  transfers between devices with their start and end apart: 11 -> 11, of which waited for: 5 -> 3; matrix products, arithmetic and copies ran while one was open for 0% -> 0% of each run, Pallas kernels for 14% -> 20%
where the time goes in v2:
time: 48.4 us; the launch traced here: 48.2 us
  starting transfers between devices  23 us (48%)
  Pallas kernels  18.3 us (38%)
  waiting for transfers between devices  6.16 us (13%)
  between operations  0.77 us (2%)
    ppermute x4, starting transfers between devices, swap_rows(): return lax.ppermute(array, 'row', row_pairs(kind, lax.axis_size('row')))  8.36 us
    pallas_call x1, Pallas kernels, compute(): pl.pallas_call(functools.partial(interior_kernel, layers=layers, rows=row...  6.91 us
    ppermute x2, starting transfers between devices, swap_corners(): return lax.ppermute(array, AXES, pairs)  6.38 us
    ppermute x3, starting transfers between devices, compute(): lax.ppermute(parts[k], 'depth', [(i, i ^ k) for i in range(depth_count)])  5.12 us
    pallas_call x1, Pallas kernels, compute(): pl.pallas_call(functools.partial(settle_kernel, layers=layers, rows=rows,...  4.82 us
    ppermute x3, waiting for transfers between devices, compute(): lax.ppermute(parts[k], 'depth', [(i, i ^ k) for i in range(depth_count)])  4.25 us
    ppermute x2, starting transfers between devices, swap_depths(): return lax.ppermute(array, 'depth', row_pairs(kind, lax.axis_size('depth')))  3.16 us
    pallas_call x1, Pallas kernels, compute(): pl.pallas_call(functools.partial(assemble_kernel, layers=layers, rows=row...  2.75 us
  transfers between devices with their start and end apart: 11, of which 3 were waited for; matrix products, arithmetic and copies ran while one was open for 0% of the time, Pallas kernels for 20%

profile of v2, /device:TPU:1, one launch (start us, length us, event | category | flops | bytes accessed | tf_op | source)
XLA Modules:
  0.0 48.2 jit_solution(5837710519848815503)
XLA Ops:
  0.6 2.4 %pack.1 = (f32[4,16,16,1024]{3,2,1,0:T(8,128)S(1)}, f32[4,16,2,8,128]{4,3,2,1,0:T(8,128)S(1)}, f32[4,16,2,8,128]{4,3,2,1,0:T(8,128)S(1)}, f32[4,8,128]{2,1,0:T(8,128)S(1)}, f32[4,8,128]{2,1,0:T(8,128)S(1)}) custom-call(f32[16,16,1024]{2,1,0:T(8,128)} %den_ref.1, f32[3,16,16,1024]{3,2,1,0:T(8,128)} %vel_ref.1), custom_call_target="tpu_custom_call" | custom-call | tf_op jit(solution)/shard_map/pack/pallas_call | solution.py:694
  3.1 0.1 collective-permute-start
  3.2 1.9 %collective-permute-done.row0_ref = f32[4,16,2,8,128]{4,3,2,1,0:T(8,128)S(1)} collective-permute-done((f32[4,16,2,8,128]{4,3,2,1,0:T(8,128)S(1)}, f32[4,16,2,8,128]{4,3,2,1,0:T(8,128)S(1)}, u32[]{:S(2)}, u32[]{:S(2)}) %collective-permute-start) | collective-permute-done | bytes 524320 | tf_op jit(solution)/shard_map/ppermute | solution.py:33
  5.1 0.1 pack_depth.1
  5.1 2.5 %collective-permute-start.2 = (f32[4,264,128]{2,1,0:T(8,128)S(1)}, f32[4,264,128]{2,1,0:T(8,128)S(1)}, u32[]{:S(2)}, u32[]{:S(2)}) collective-permute-start(f32[4,264,128]{2,1,0:T(8,128)S(1)} %get-tuple-element.29), channel_id=1, source_target_pairs={{0,1},{1,0},{2,3},{3,2},{4,5},{5,4},{6,7},{7,6},{8,9},{9,8},{10,11... | collective-permute-start | bytes 1622024 | tf_op jit(solution)/shard_map/ppermute | solution.py:37
  7.6 0.7 %collective-permute-start.3 = (f32[4,264,128]{2,1,0:T(8,128)S(1)}, f32[4,264,128]{2,1,0:T(8,128)S(1)}, u32[]{:S(2)}, u32[]{:S(2)}) collective-permute-start(f32[4,264,128]{2,1,0:T(8,128)S(1)} %get-tuple-element.30), channel_id=1, source_target_pairs={{1,2},{2,1},{5,6},{6,5},{9,10},{10,9},{13,14},{14,13},{17,18},{18,... | collective-permute-start | bytes 1622024 | tf_op jit(solution)/shard_map/ppermute | solution.py:37
  8.3 3.7 %collective-permute-start.1 = (f32[4,16,2,8,128]{4,3,2,1,0:T(8,128)S(1)}, f32[4,16,2,8,128]{4,3,2,1,0:T(8,128)S(1)}, u32[]{:S(2)}, u32[]{:S(2)}) collective-permute-start(f32[4,16,2,8,128]{4,3,2,1,0:T(8,128)S(1)} %get-tuple-element.28), channel_id=1, source_target_pairs={{4,8},{8,4},{12,16},{16,12},{20,24},{24,20},{5,9},{9,5},{13,17},{1... | collective-permute-start | bytes 1572872 | tf_op jit(solution)/shard_map/ppermute | solution.py:33
  12.0 5.7 %collective-permute-start.4 = (f32[4,8,128]{2,1,0:T(8,128)S(1)}, f32[4,8,128]{2,1,0:T(8,128)S(1)}, u32[]{:S(2)}, u32[]{:S(2)}) collective-permute-start(f32[4,8,128]{2,1,0:T(8,128)S(1)} %get-tuple-element.31), channel_id=1, source_target_pairs={{4,9},{5,8},{6,11},{7,10},{8,5},{9,4},{10,7},{11,6},{12,17},{13,16... | collective-permute-start | bytes 49160 | tf_op jit(solution)/shard_map/ppermute | solution.py:47
  17.7 0.7 %collective-permute-start.5 = (f32[4,8,128]{2,1,0:T(8,128)S(1)}, f32[4,8,128]{2,1,0:T(8,128)S(1)}, u32[]{:S(2)}, u32[]{:S(2)}) collective-permute-start(f32[4,8,128]{2,1,0:T(8,128)S(1)} %get-tuple-element.32), channel_id=1, source_target_pairs={{5,10},{6,9},{9,6},{10,5},{13,18},{14,17},{17,14},{18,13},{21,26},... | collective-permute-start | bytes 49160 | tf_op jit(solution)/shard_map/ppermute | solution.py:47
  18.4 6.9 %interior.1 = (f32[16,4,128,128]{3,2,1,0:T(8,128)S(1)}, f32[16,128,128]{2,1,0:T(8,128)S(1)}, f32[16,2,4,8,128]{4,3,2,1,0:T(8,128)S(1)}, f32[16,4,128,128]{3,2,1,0:T(8,128)S(1)}, f32[4,128,128]{2,1,0:T(8,128)S(1)}) custom-call(f32[3,4]{1,0:T(4,128)S(1)} %copy-done, f32[4,16,16,1024]{3,2,1,0:T(8,128)S(1)} %get-tuple-element.26.block), custom_call_target="tpu_custom_call" | custom-call | flops 20971520 | bytes 4194304 | tf_op jit(solution)/shard_map/interior/pallas_call | solution.py:722
  25.3 0.0 collective-permute-done.5.c11_ref
  25.4 0.0 collective-permute-done.3.depth1_ref
  25.4 4.8 %settle.1 = (f32[4,4,128,128]{3,2,1,0:T(8,128)S(1)}, f32[16,4,4,8,128]{4,3,2,1,0:T(8,128)S(1)}, f32[16,1152]{1,0:T(8,128)S(1)}, f32[16,1152]{1,0:T(8,128)S(1)}, ...) custom-call(f32[3,4]{1,0:T(4,128)S(1)} %copy-done, f32[4,16,16,1024]{3,2,1,0:T(8,128)S(1)} %get-tuple-element.26.block, ...), custom_call_target="tpu_custom_call" | custom-call | tf_op jit(solution)/shard_map/settle/pallas_call | solution.py:744
  30.2 2.5 %collective-permute-start.6 = (f32[16,1152]{1,0:T(8,128)S(1)}, f32[16,1152]{1,0:T(8,128)S(1)}, u32[]{:S(2)}, u32[]{:S(2)}) collective-permute-start(f32[16,1152]{1,0:T(8,128)S(1)} %get-tuple-element.38), channel_id=1, source_target_pairs={{0,2},{1,3},{2,0},{3,1},{4,6},{5,7},{6,4},{7,5},{8,10},{9,11},{10,... | collective-permute-start | bytes 221192 | tf_op jit(solution)/shard_map/ppermute | solution.py:788
  32.7 0.6 %collective-permute-start.7 = (f32[16,1152]{1,0:T(8,128)S(1)}, f32[16,1152]{1,0:T(8,128)S(1)}, u32[]{:S(2)}, u32[]{:S(2)}) collective-permute-start(f32[16,1152]{1,0:T(8,128)S(1)} %get-tuple-element.39), channel_id=1, source_target_pairs={{0,1},{1,0},{2,3},{3,2},{4,5},{5,4},{6,7},{7,6},{8,9},{9,8},{10,11... | collective-permute-start | bytes 221192 | tf_op jit(solution)/shard_map/ppermute | solution.py:788
  33.3 2.0 %collective-permute-start.8 = (f32[16,1152]{1,0:T(8,128)S(1)}, f32[16,1152]{1,0:T(8,128)S(1)}, u32[]{:S(2)}, u32[]{:S(2)}) collective-permute-start(f32[16,1152]{1,0:T(8,128)S(1)} %get-tuple-element.40), channel_id=1, source_target_pairs={{0,3},{1,2},{2,1},{3,0},{4,7},{5,6},{6,5},{7,4},{8,11},{9,10},{10,... | collective-permute-start | bytes 221192 | tf_op jit(solution)/shard_map/ppermute | solution.py:788
  35.3 0.0 collective-permute-done.6.refs_1_
  35.3 1.8 %collective-permute-done.7.refs_2_ = f32[16,1152]{1,0:T(8,128)S(1)} collective-permute-done((f32[16,1152]{1,0:T(8,128)S(1)}, f32[16,1152]{1,0:T(8,128)S(1)}, u32[]{:S(2)}, u32[]{:S(2)}) %collective-permute-start.7) | collective-permute-done | bytes 73760 | tf_op jit(solution)/shard_map/ppermute | solution.py:788
  37.2 2.4 %collective-permute-done.8.refs_3_ = f32[16,1152]{1,0:T(8,128)S(1)} collective-permute-done((f32[16,1152]{1,0:T(8,128)S(1)}, f32[16,1152]{1,0:T(8,128)S(1)}, u32[]{:S(2)}, u32[]{:S(2)}) %collective-permute-start.8) | collective-permute-done | bytes 73760 | tf_op jit(solution)/shard_map/ppermute | solution.py:788
  39.6 0.2 over.1
  39.7 0.1 collective-permute-start.9
  39.8 4.6 %collective-permute-start.10 = (f32[2,1152]{1,0:T(2,128)S(1)}, f32[2,1152]{1,0:T(2,128)S(1)}, u32[]{:S(2)}, u32[]{:S(2)}) collective-permute-start(f32[2,1152]{1,0:T(2,128)S(1)} %get-tuple-element.43), channel_id=1, source_target_pairs={{4,8},{8,4},{12,16},{16,12},{20,24},{24,20},{5,9},{9,5},{13,17},{1... | collective-permute-start | bytes 27656 | tf_op jit(solution)/shard_map/ppermute | solution.py:33
  44.4 2.7 %assemble.1 = (f32[16,16,1024]{2,1,0:T(8,128)}, f32[3,16,16,1024]{3,2,1,0:T(8,128)}) custom-call(f32[4,4,128,128]{3,2,1,0:T(8,128)S(1)} %get-tuple-element.44.whole_ref, f32[16,4,4,8,128]{4,3,2,1,0:T(8,128)S(1)} %get-tuple-element.45.lines_ref, f32[16,4,128,128]{3,2,1,0:T(8,128)S(1)} %get-tuple-element.46.late_ref), custom_call_target="tpu_custom_call" | custom-call | flops 5242880 | bytes 4194304 | tf_op jit(solution)/shard_map/assemble/pallas_call | solution.py:770
  47.1 1.1 %bilateral.1 = f32[4,16,256]{2,1,0:T(8,128)} custom-call(f32[16,1152]{1,0:T(8,128)S(1)} %get-tuple-element.41.picture_ref, f32[2,1152]{1,0:T(2,128)S(1)} %collective-permute-done.9.swap0_ref, f32[2,1152]{1,0:T(2,128)S(1)} %collective-permute-done.10.swap1_ref), custom_call_target="tpu_custom_call" | custom-call | tf_op jit(solution)/shard_map/bilateral/pallas_call | solution.py:799
  (7 shorter events, 0.0 us)
Async XLA Ops:
  0.6 17.8 %copy-start = (f32[3,4]{1,0:T(4,128)S(1)}, f32[3,4]{1,0:T(4,128)}, u32[]{:S(2)}) copy-start(f32[3,4]{1,0:T(4,128)} %palette_ref.3) | copy-start | bytes 148
  3.1 2.0 %collective-permute-start = (f32[4,16,2,8,128]{4,3,2,1,0:T(8,128)S(1)}, f32[4,16,2,8,128]{4,3,2,1,0:T(8,128)S(1)}, u32[]{:S(2)}, u32[]{:S(2)}) collective-permute-start(f32[4,16,2,8,128]{4,3,2,1,0:T(8,128)S(1)} %get-tuple-element.27), channel_id=1, source_target_pairs={{0,4},{4,0},{8,12},{12,8},{16,20},{20,16},{24,28},{28,24},{1,5},{5... | collective-permute-start | bytes 1572872 | tf_op jit(solution)/shard_map/ppermute | solution.py:33
  5.1 20.2 %collective-permute-start.2 = (f32[4,264,128]{2,1,0:T(8,128)S(1)}, f32[4,264,128]{2,1,0:T(8,128)S(1)}, u32[]{:S(2)}, u32[]{:S(2)}) collective-permute-start(f32[4,264,128]{2,1,0:T(8,128)S(1)} %get-tuple-element.29), channel_id=1, source_target_pairs={{0,1},{1,0},{2,3},{3,2},{4,5},{5,4},{6,7},{7,6},{8,9},{9,8},{10,11... | collective-permute-start | bytes 1622024 | tf_op jit(solution)/shard_map/ppermute | solution.py:37
  7.6 17.7 %collective-permute-start.3 = (f32[4,264,128]{2,1,0:T(8,128)S(1)}, f32[4,264,128]{2,1,0:T(8,128)S(1)}, u32[]{:S(2)}, u32[]{:S(2)}) collective-permute-start(f32[4,264,128]{2,1,0:T(8,128)S(1)} %get-tuple-element.30), channel_id=1, source_target_pairs={{1,2},{2,1},{5,6},{6,5},{9,10},{10,9},{13,14},{14,13},{17,18},{18,... | collective-permute-start | bytes 1622024 | tf_op jit(solution)/shard_map/ppermute | solution.py:37
  8.3 17.0 %collective-permute-start.1 = (f32[4,16,2,8,128]{4,3,2,1,0:T(8,128)S(1)}, f32[4,16,2,8,128]{4,3,2,1,0:T(8,128)S(1)}, u32[]{:S(2)}, u32[]{:S(2)}) collective-permute-start(f32[4,16,2,8,128]{4,3,2,1,0:T(8,128)S(1)} %get-tuple-element.28), channel_id=1, source_target_pairs={{4,8},{8,4},{12,16},{16,12},{20,24},{24,20},{5,9},{9,5},{13,17},{1... | collective-permute-start | bytes 1572872 | tf_op jit(solution)/shard_map/ppermute | solution.py:33
  12.0 13.3 %collective-permute-start.4 = (f32[4,8,128]{2,1,0:T(8,128)S(1)}, f32[4,8,128]{2,1,0:T(8,128)S(1)}, u32[]{:S(2)}, u32[]{:S(2)}) collective-permute-start(f32[4,8,128]{2,1,0:T(8,128)S(1)} %get-tuple-element.31), channel_id=1, source_target_pairs={{4,9},{5,8},{6,11},{7,10},{8,5},{9,4},{10,7},{11,6},{12,17},{13,16... | collective-permute-start | bytes 49160 | tf_op jit(solution)/shard_map/ppermute | solution.py:47
  17.7 7.6 %collective-permute-start.5 = (f32[4,8,128]{2,1,0:T(8,128)S(1)}, f32[4,8,128]{2,1,0:T(8,128)S(1)}, u32[]{:S(2)}, u32[]{:S(2)}) collective-permute-start(f32[4,8,128]{2,1,0:T(8,128)S(1)} %get-tuple-element.32), channel_id=1, source_target_pairs={{5,10},{6,9},{9,6},{10,5},{13,18},{14,17},{17,14},{18,13},{21,26},... | collective-permute-start | bytes 49160 | tf_op jit(solution)/shard_map/ppermute | solution.py:47
  30.2 5.1 %collective-permute-start.6 = (f32[16,1152]{1,0:T(8,128)S(1)}, f32[16,1152]{1,0:T(8,128)S(1)}, u32[]{:S(2)}, u32[]{:S(2)}) collective-permute-start(f32[16,1152]{1,0:T(8,128)S(1)} %get-tuple-element.38), channel_id=1, source_target_pairs={{0,2},{1,3},{2,0},{3,1},{4,6},{5,7},{6,4},{7,5},{8,10},{9,11},{10,... | collective-permute-start | bytes 221192 | tf_op jit(solution)/shard_map/ppermute | solution.py:788
  32.7 4.5 %collective-permute-start.7 = (f32[16,1152]{1,0:T(8,128)S(1)}, f32[16,1152]{1,0:T(8,128)S(1)}, u32[]{:S(2)}, u32[]{:S(2)}) collective-permute-start(f32[16,1152]{1,0:T(8,128)S(1)} %get-tuple-element.39), channel_id=1, source_target_pairs={{0,1},{1,0},{2,3},{3,2},{4,5},{5,4},{6,7},{7,6},{8,9},{9,8},{10,11... | collective-permute-start | bytes 221192 | tf_op jit(solution)/shard_map/ppermute | solution.py:788
  33.3 6.3 %collective-permute-start.8 = (f32[16,1152]{1,0:T(8,128)S(1)}, f32[16,1152]{1,0:T(8,128)S(1)}, u32[]{:S(2)}, u32[]{:S(2)}) collective-permute-start(f32[16,1152]{1,0:T(8,128)S(1)} %get-tuple-element.40), channel_id=1, source_target_pairs={{0,3},{1,2},{2,1},{3,0},{4,7},{5,6},{6,5},{7,4},{8,11},{9,10},{10,... | collective-permute-start | bytes 221192 | tf_op jit(solution)/shard_map/ppermute | solution.py:788
  39.7 7.4 %collective-permute-start.9 = (f32[2,1152]{1,0:T(2,128)S(1)}, f32[2,1152]{1,0:T(2,128)S(1)}, u32[]{:S(2)}, u32[]{:S(2)}) collective-permute-start(f32[2,1152]{1,0:T(2,128)S(1)} %get-tuple-element.42), channel_id=1, source_target_pairs={{0,4},{4,0},{8,12},{12,8},{16,20},{20,16},{24,28},{28,24},{1,5},{5... | collective-permute-start | bytes 27656 | tf_op jit(solution)/shard_map/ppermute | solution.py:33
  39.8 7.3 %collective-permute-start.10 = (f32[2,1152]{1,0:T(2,128)S(1)}, f32[2,1152]{1,0:T(2,128)S(1)}, u32[]{:S(2)}, u32[]{:S(2)}) collective-permute-start(f32[2,1152]{1,0:T(2,128)S(1)} %get-tuple-element.43), channel_id=1, source_target_pairs={{4,8},{8,4},{12,16},{16,12},{20,24},{24,20},{5,9},{9,5},{13,17},{1... | collective-permute-start | bytes 27656 | tf_op jit(solution)/shard_map/ppermute | solution.py:33

commit v3 on v2

--- a/solution.py
+++ b/solution.py
@@ -271,13 +271,98 @@
         first_step(layers - 1, (2, 3, 0))
 
 
+def edge_rows(z, rowbuf, early_ref, share_ref, edge_ref, srow, places, rows, spans):
+    above, below, has_above, has_below = places
+    sub = lax.broadcasted_iota(jnp.int32, (SUB, LANES), 0)
+    lane = lax.broadcasted_iota(jnp.int32, (SUB, LANES), 1)
+    first, last = lane == 0, lane == LANES - 1
+    for side, kind, k, exists in ((0, above, 1, has_above), (1, below, 0, has_below)):
+        own_cells = pl.ds(0 if side == 0 else rows - 1, spans, stride=rows)
+
+        def halo(layer, n):
+            return [rowbuf[kind, c, layer, n] for c in range(4)]
+
+        here, farther = halo(z + 1, k), halo(z + 1, 1 - k)
+        own = [edge_ref[z, side, c] for c in range(4)]
+        new = late_share(
+            [early_ref[z, c, own_cells, :] for c in range(4)], here,
+            share_ref[z, own_cells, :], 2, 1.0 if side == 0 else -1.0,
+        )
+        for c in range(4):
+            srow[z, 1 + side, c] = new[c]
+        left, right = beside_in_lines(here, sub, first, last)
+        up, down = (farther, own) if side == 0 else (own, farther)
+        new, _ = advance(here, up, down, left, right, halo(z, k), halo(z + 2, k))
+        inside = jnp.full((SUB, LANES), jnp.where(exists, 1, 0), jnp.int32) == 1
+        for c in range(4):
+            srow[z, 3 * side, c] = jnp.where(inside, new[c], 0.0)
+
+
+def row_places(row_count):
+    row_rank = lax.axis_index("row")
+    row_odd = lax.rem(row_rank, 2)
+    return 1 - row_odd, row_odd, row_rank > 0, row_rank < row_count - 1
+
+
+def outer_kernel(
+    palette_ref, row0_ref, row1_ref, early_ref, share_ref, edge_ref,
+    rowbuf, srow, lines_ref, part_ref, *, layers, rows, columns, depth_count, row_count,
+):
+    spans = columns // LANES
+    sub = lax.broadcasted_iota(jnp.int32, (SUB, LANES), 0)
+    lane = lax.broadcasted_iota(jnp.int32, (SUB, LANES), 1)
+    first, last = lane == 0, lane == LANES - 1
+    places = row_places(row_count)
+    rate, mix = constants(palette_ref, layers * depth_count)
+    for kind, source in ((0, row0_ref), (1, row1_ref)):
+        for c in range(4):
+            for z in range(layers):
+                for k in range(2):
+                    rowbuf[kind, c, z + 1, k] = source[c, z, k]
+    for c in range(3):
+        part_ref[c] = jnp.zeros((4 * spans, LANES), jnp.float32)
+    part_ref[3] = jnp.ones((4 * spans, LANES), jnp.float32)
+
+    def outer_rows(z):
+        def values(layer, row):
+            n = {-1: 0, 0: 1, rows - 1: 2, rows: 3}.get(row)
+            if n is not None:
+                return [srow[layer, n, c] for c in range(4)]
+            return [early_ref[layer, c, pl.ds(row, spans, stride=rows), :] for c in range(4)]
+
+        for n, row in enumerate((0, 1, rows - 2, rows - 1)):
+            here = values(z, row)
+            left, right = beside_in_lines(here, sub, first, last)
+            new, _ = advance(
+                here, values(z, row - 1), values(z, row + 1), left, right,
+                values(z - 1, row), values(z + 1, row),
+            )
+            render(part_ref, pl.ds(n * spans, spans), new, rate, mix)
+            for c in range(4):
+                lines_ref[z, n, c] = new[c]
+
+    def edges(z):
+        edge_rows(z, rowbuf, early_ref, share_ref, edge_ref, srow, places, rows, spans)
+
+    @pl.loop(0, (layers - 2) // 2)
+    def _(pair):
+        edges(2 * pair + 1)
+        edges(2 * pair + 2)
+
+    @pl.loop(0, (layers - 4) // 2)
+    def _(pair):
+        outer_rows(2 * pair + 2)
+        outer_rows(2 * pair + 3)
+
+
 def settle_kernel(
-    palette_ref, block, row0_ref, row1_ref, depth0_ref, depth1_ref, c10_ref, c11_ref,
-    early_ref, share_ref, edge_ref, part_ref, whole_ref, lines_ref, *rest,
+    palette_ref, block, depth0_ref, depth1_ref, c10_ref, c11_ref,
+    early_ref, share_ref, edge_ref, part_ref, rows_part_ref, given_rowbuf, given_srow,
+    whole_ref, rowbuf, srow, *rest,
     layers, rows, columns, depth_count, row_count,
 ):
     pieces = rest[:depth_count]
-    rowbuf, srow, base, sbase, accum = rest[depth_count:]
+    base, sbase, accum = rest[depth_count:]
     own_tiles, spans = rows // SUB, columns // LANES
     row_rank, depth_rank = lax.axis_index("row"), lax.axis_index("depth")
     row_odd, depth_odd = lax.rem(row_rank, 2), lax.rem(depth_rank, 2)
@@ -335,30 +420,6 @@
             for c in range(4):
                 sbase[slot, c, cells, :] = new[c]
 
-    def edge_rows(z):
-        for side, kind, k, exists in (
-            (0, above, 1, row_rank > 0), (1, below, 0, row_rank < row_count - 1),
-        ):
-            own_cells = pl.ds(0 if side == 0 else rows - 1, spans, stride=rows)
-
-            def halo(layer, n):
-                return [rowbuf[kind, c, layer, n] for c in range(4)]
-
-            here, farther = halo(z + 1, k), halo(z + 1, 1 - k)
-            own = [edge_ref[z, side, c] for c in range(4)]
-            new = late_share(
-                [early_ref[z, c, own_cells, :] for c in range(4)], here,
-                share_ref[z, own_cells, :], 2, 1.0 if side == 0 else -1.0,
-            )
-            for c in range(4):
-                srow[z, 1 + side, c] = new[c]
-            left, right = beside_in_lines(here, sub, first, last)
-            up, down = (farther, own) if side == 0 else (own, farther)
-            new, _ = advance(here, up, down, left, right, halo(z, k), halo(z + 2, k))
-            inside = jnp.full((SUB, LANES), jnp.where(exists, 1, 0), jnp.int32) == 1
-            for c in range(4):
-                srow[z, 3 * side, c] = jnp.where(inside, new[c], 0.0)
-
     def take_layer(z, slot):
         for t, j in tiles:
             for c in range(4):
@@ -374,29 +435,6 @@
                 whole_ref[n, c, cells_of(t, j), :] = new[c]
             render(accum, cells_of(t, j), new, rate, mix)
 
-    def outer_rows(z):
-        def values(layer, row):
-            n = {-1: 0, 0: 1, rows - 1: 2, rows: 3}.get(row)
-            if n is not None:
-                return [srow[layer, n, c] for c in range(4)]
-            return [early_ref[layer, c, pl.ds(row, spans, stride=rows), :] for c in range(4)]
-
-        for n, row in enumerate((0, 1, rows - 2, rows - 1)):
-            here = values(z, row)
-            left, right = beside_in_lines(here, sub, first, last)
-            new, _ = advance(
-                here, values(z, row - 1), values(z, row + 1), left, right,
-                values(z - 1, row), values(z + 1, row),
-            )
-            render(accum, pl.ds(row, spans, stride=rows), new, rate, mix)
-            for c in range(4):
-                lines_ref[z, n, c] = new[c]
-
-    for kind, source in ((0, row0_ref), (1, row1_ref)):
-        for c in range(4):
-            for z in range(layers):
-                for k in range(2):
-                    rowbuf[kind, c, z + 1, k] = source[c, z, k]
     beside = pl.ds(2 * spans * rows, spans)
     corners = (
         (0, 0, lambda c: depth0_ref[c, beside, :]), (0, 1, lambda c: depth1_ref[c, beside, :]),
@@ -411,10 +449,10 @@
         accum[c] = jnp.zeros((spans * rows, LANES), jnp.float32)
     accum[3] = jnp.ones((spans * rows, LANES), jnp.float32)
 
-    @pl.loop(0, layers // 2)
-    def _(pair):
-        edge_rows(2 * pair)
-        edge_rows(2 * pair + 1)
+    for z in (0, layers - 1):
+        edge_rows(
+            z, rowbuf, early_ref, share_ref, edge_ref, srow, row_places(row_count), rows, spans
+        )
 
     outer_step(3, True)
     take_layer(0, 0)
@@ -436,10 +474,12 @@
             accum[c, pixels, :] = jnp.where(inner, value + through * part_ref[c, pixels, :], value)
         accum[3, pixels, :] = jnp.where(inner, through * part_ref[3, pixels, :], through)
 
-    @pl.loop(0, (layers - 4) // 2)
-    def _(pair):
-        outer_rows(2 * pair + 2)
-        outer_rows(2 * pair + 3)
+    for n, row in enumerate((0, 1, rows - 2, rows - 1)):
+        pixels, theirs = pl.ds(row, spans, stride=rows), pl.ds(n * spans, spans)
+        through = accum[3, pixels, :]
+        for c in range(3):
+            accum[c, pixels, :] = accum[c, pixels, :] + through * rows_part_ref[c, theirs, :]
+        accum[3, pixels, :] = through * rows_part_ref[3, theirs, :]
 
     take_layer(layers - 3, 0)
     take_layer(layers - 2, 1)
@@ -741,18 +781,38 @@
         compiler_params=pltpu.CompilerParams(vmem_limit_bytes=24 << 20),
     )(palette, in_vmem(block))
 
-    whole, lines, *parts = pl.pallas_call(
+    rowbuf_shape = (2, 4, layers + 2, 2, spans, LANES)
+    srow_shape = (layers, 4, 4, spans, LANES)
+    rowbuf, srow, lines, rows_part = pl.pallas_call(
+        functools.partial(
+            outer_kernel, layers=layers, rows=rows, columns=columns,
+            depth_count=depth_count, row_count=row_count,
+        ),
+        out_shape=(
+            local(*rowbuf_shape), local(*srow_shape), local(*srow_shape),
+            local(4, 4 * spans, LANES),
+        ),
+        in_specs=[smem] + [vmem] * 5,
+        out_specs=(vmem,) * 4,
+        cost_estimate=pl.CostEstimate(
+            flops=40 * layers * rows * columns, bytes_accessed=4 * layers * rows * columns,
+            transcendentals=layers * rows * columns,
+        ),
+        name="outer",
+        compiler_params=params(16),
+    )(palette, *(in_vmem(x) for x in (row0, row1, early, share, edge)))
+
+    whole, unused, unused, *parts = pl.pallas_call(
         functools.partial(
             settle_kernel, layers=layers, rows=rows, columns=columns,
             depth_count=depth_count, row_count=row_count,
         ),
-        out_shape=(local(4, 4, spans * rows, LANES), local(layers, 4, 4, spans, LANES))
+        out_shape=(local(4, 4, spans * rows, LANES), local(*rowbuf_shape), local(*srow_shape))
         + (local(rows, line),) * depth_count,
-        in_specs=[smem] + [vmem] * 11,
-        out_specs=(vmem,) * (2 + depth_count),
+        in_specs=[smem] + [vmem] * 12,
+        out_specs=(vmem,) * (3 + depth_count),
+        input_output_aliases={11: 1, 12: 2},
         scratch_shapes=[
-            pltpu.VMEM((2, 4, layers + 2, 2, spans, LANES), f32),
-            pltpu.VMEM((layers, 4, 4, spans, LANES), f32),
             pltpu.VMEM((3, 4, spans * PITCH, LANES), f32),
             pltpu.VMEM((4, 4, spans * PITCH, LANES), f32),
             pltpu.VMEM((4, spans * rows, LANES), f32),
@@ -763,7 +823,10 @@
         palette,
         *(
             in_vmem(x)
-            for x in (block, row0, row1, depth0, depth1, corner0, corner1, early, share, edge, part)
+            for x in (
+                block, depth0, depth1, corner0, corner1, early, share, edge, part, rows_part,
+                rowbuf, srow,
+            )
         ),
     )
 

time: 48.4 us -> 48.9 us (1.010)
  waiting for transfers between devices: 6.16 us -> 5.22 us
  starting transfers between devices: 23 us -> 23.9 us
  Pallas kernels: 18.3 us -> 18.8 us
    pallas_call x0 -> x1, Pallas kernels: none -> 2.66 us  [compute(): pl.pallas_call(functools.partial(outer_kernel, layers=layers, rows=rows,...]
    pallas_call x1, Pallas kernels: 4.82 us -> 2.55 us  [compute(): pl.pallas_call(functools.partial(settle_kernel, layers=layers, rows=rows,...]
    ppermute x3, waiting for transfers between devices: 4.25 us -> 3.31 us  [compute(): lax.ppermute(parts[k], 'depth', [(i, i ^ k) for i in range(depth_count)])]
    ppermute x4, starting transfers between devices: 8.36 us -> 9.3 us  [swap_rows(): return lax.ppermute(array, 'row', row_pairs(kind, lax.axis_size('row')))]
  transfers between devices with their start and end apart: 11 -> 11, of which waited for: 3 -> 4; matrix products, arithmetic and copies ran while one was open for 0% -> 0% of each run, Pallas kernels for 20% -> 26%
where the time goes in v3:
time: 48.9 us; the launch traced here: 48.6 us
  starting transfers between devices  23.9 us (49%)
  Pallas kernels  18.8 us (38%)
  waiting for transfers between devices  5.22 us (11%)
  between operations  0.77 us (2%)
    ppermute x4, starting transfers between devices, swap_rows(): return lax.ppermute(array, 'row', row_pairs(kind, lax.axis_size('row')))  9.3 us
    pallas_call x1, Pallas kernels, compute(): pl.pallas_call(functools.partial(interior_kernel, layers=layers, rows=row...  7.05 us
    ppermute x2, starting transfers between devices, swap_corners(): return lax.ppermute(array, AXES, pairs)  6.38 us
    ppermute x3, starting transfers between devices, compute(): lax.ppermute(parts[k], 'depth', [(i, i ^ k) for i in range(depth_count)])  5.02 us
    ppermute x3, waiting for transfers between devices, compute(): lax.ppermute(parts[k], 'depth', [(i, i ^ k) for i in range(depth_count)])  3.31 us
    ppermute x2, starting transfers between devices, swap_depths(): return lax.ppermute(array, 'depth', row_pairs(kind, lax.axis_size('depth')))  3.16 us
    pallas_call x1, Pallas kernels, compute(): pl.pallas_call(functools.partial(assemble_kernel, layers=layers, rows=row...  2.75 us
    pallas_call x1, Pallas kernels, compute(): pl.pallas_call(functools.partial(outer_kernel, layers=layers, rows=rows,...  2.66 us
  transfers between devices with their start and end apart: 11, of which 4 were waited for; matrix products, arithmetic and copies ran while one was open for 0% of the time, Pallas kernels for 26%

profile of v3, /device:TPU:1, one launch (start us, length us, event | category | flops | bytes accessed | tf_op | source)
XLA Modules:
  0.0 48.6 jit_solution(12753921002166347840)
XLA Ops:
  0.6 2.4 %pack.1 = (f32[4,16,16,1024]{3,2,1,0:T(8,128)S(1)}, f32[4,16,2,8,128]{4,3,2,1,0:T(8,128)S(1)}, f32[4,16,2,8,128]{4,3,2,1,0:T(8,128)S(1)}, f32[4,8,128]{2,1,0:T(8,128)S(1)}, f32[4,8,128]{2,1,0:T(8,128)S(1)}) custom-call(f32[16,16,1024]{2,1,0:T(8,128)} %den_ref.1, f32[3,16,16,1024]{3,2,1,0:T(8,128)} %vel_ref.1), custom_call_target="tpu_custom_call" | custom-call | tf_op jit(solution)/shard_map/pack/pallas_call | solution.py:734
  3.1 0.0 copy-start
  3.1 0.1 collective-permute-start
  3.2 1.9 %collective-permute-done.row0_ref = f32[4,16,2,8,128]{4,3,2,1,0:T(8,128)S(1)} collective-permute-done((f32[4,16,2,8,128]{4,3,2,1,0:T(8,128)S(1)}, f32[4,16,2,8,128]{4,3,2,1,0:T(8,128)S(1)}, u32[]{:S(2)}, u32[]{:S(2)}) %collective-permute-start) | collective-permute-done | bytes 524320 | tf_op jit(solution)/shard_map/ppermute | solution.py:33
  5.1 0.1 pack_depth.1
  5.1 2.5 %collective-permute-start.1 = (f32[4,264,128]{2,1,0:T(8,128)S(1)}, f32[4,264,128]{2,1,0:T(8,128)S(1)}, u32[]{:S(2)}, u32[]{:S(2)}) collective-permute-start(f32[4,264,128]{2,1,0:T(8,128)S(1)} %get-tuple-element.31), channel_id=1, source_target_pairs={{0,1},{1,0},{2,3},{3,2},{4,5},{5,4},{6,7},{7,6},{8,9},{9,8},{10,11... | collective-permute-start | bytes 1622024 | tf_op jit(solution)/shard_map/ppermute | solution.py:37
  7.6 0.7 %collective-permute-start.2 = (f32[4,264,128]{2,1,0:T(8,128)S(1)}, f32[4,264,128]{2,1,0:T(8,128)S(1)}, u32[]{:S(2)}, u32[]{:S(2)}) collective-permute-start(f32[4,264,128]{2,1,0:T(8,128)S(1)} %get-tuple-element.32), channel_id=1, source_target_pairs={{1,2},{2,1},{5,6},{6,5},{9,10},{10,9},{13,14},{14,13},{17,18},{18,... | collective-permute-start | bytes 1622024 | tf_op jit(solution)/shard_map/ppermute | solution.py:37
  8.3 3.7 %collective-permute-start.5 = (f32[4,16,2,8,128]{4,3,2,1,0:T(8,128)S(1)}, f32[4,16,2,8,128]{4,3,2,1,0:T(8,128)S(1)}, u32[]{:S(2)}, u32[]{:S(2)}) collective-permute-start(f32[4,16,2,8,128]{4,3,2,1,0:T(8,128)S(1)} %get-tuple-element.39), channel_id=1, source_target_pairs={{4,8},{8,4},{12,16},{16,12},{20,24},{24,20},{5,9},{9,5},{13,17},{1... | collective-permute-start | bytes 1572872 | tf_op jit(solution)/shard_map/ppermute | solution.py:33
  12.0 5.7 %collective-permute-start.3 = (f32[4,8,128]{2,1,0:T(8,128)S(1)}, f32[4,8,128]{2,1,0:T(8,128)S(1)}, u32[]{:S(2)}, u32[]{:S(2)}) collective-permute-start(f32[4,8,128]{2,1,0:T(8,128)S(1)} %get-tuple-element.33), channel_id=1, source_target_pairs={{4,9},{5,8},{6,11},{7,10},{8,5},{9,4},{10,7},{11,6},{12,17},{13,16... | collective-permute-start | bytes 49160 | tf_op jit(solution)/shard_map/ppermute | solution.py:47
  17.7 0.7 %collective-permute-start.4 = (f32[4,8,128]{2,1,0:T(8,128)S(1)}, f32[4,8,128]{2,1,0:T(8,128)S(1)}, u32[]{:S(2)}, u32[]{:S(2)}) collective-permute-start(f32[4,8,128]{2,1,0:T(8,128)S(1)} %get-tuple-element.34), channel_id=1, source_target_pairs={{5,10},{6,9},{9,6},{10,5},{13,18},{14,17},{17,14},{18,13},{21,26},... | collective-permute-start | bytes 49160 | tf_op jit(solution)/shard_map/ppermute | solution.py:47
  18.4 7.0 %interior.1 = (f32[16,4,128,128]{3,2,1,0:T(8,128)S(1)}, f32[16,128,128]{2,1,0:T(8,128)S(1)}, f32[16,2,4,8,128]{4,3,2,1,0:T(8,128)S(1)}, f32[16,4,128,128]{3,2,1,0:T(8,128)S(1)}, f32[4,128,128]{2,1,0:T(8,128)S(1)}) custom-call(f32[3,4]{1,0:T(4,128)S(1)} %copy-done, f32[4,16,16,1024]{3,2,1,0:T(8,128)S(1)} %get-tuple-element.29.block), custom_call_target="tpu_custom_call" | custom-call | flops 20971520 | bytes 4194304 | tf_op jit(solution)/shard_map/interior/pallas_call | solution.py:762
  25.5 2.7 %outer.1 = (f32[2,4,18,2,8,128]{5,4,3,2,1,0:T(8,128)S(1)}, f32[16,4,4,8,128]{4,3,2,1,0:T(8,128)S(1)}, f32[16,4,4,8,128]{4,3,2,1,0:T(8,128)S(1)}, f32[4,32,128]{2,1,0:T(8,128)S(1)}) custom-call(f32[3,4]{1,0:T(4,128)S(1)} %copy-done, f32[4,16,2,8,128]{4,3,2,1,0:T(8,128)S(1)} %collective-permute-done.row0_ref, ...), custom_call_target="tpu_custom_call" | custom-call | flops 10485760 | bytes 1048576 | tf_op jit(solution)/shard_map/outer/pallas_call | solution.py:786
  28.2 2.5 %settle.1 = (f32[4,4,128,128]{3,2,1,0:T(8,128)S(1)}, f32[2,4,18,2,8,128]{5,4,3,2,1,0:T(8,128)S(1)}, f32[16,4,4,8,128]{4,3,2,1,0:T(8,128)S(1)}, f32[16,1152]{1,0:...) custom-call(f32[3,4]{1,0:T(4,128)S(1)} %copy-done, ...), custom_call_target="tpu_custom_call", output_to_operand_aliasing={{1}: (11, {}), {2}: (12, {})} | custom-call | tf_op jit(solution)/shard_map/settle/pallas_call | solution.py:805
  30.7 2.5 %collective-permute-start.6 = (f32[16,1152]{1,0:T(8,128)S(1)}, f32[16,1152]{1,0:T(8,128)S(1)}, u32[]{:S(2)}, u32[]{:S(2)}) collective-permute-start(f32[16,1152]{1,0:T(8,128)S(1)} %get-tuple-element.44), channel_id=1, source_target_pairs={{0,2},{1,3},{2,0},{3,1},{4,6},{5,7},{6,4},{7,5},{8,10},{9,11},{10,... | collective-permute-start | bytes 221192 | tf_op jit(solution)/shard_map/ppermute | solution.py:851
  33.2 0.5 %collective-permute-start.7 = (f32[16,1152]{1,0:T(8,128)S(1)}, f32[16,1152]{1,0:T(8,128)S(1)}, u32[]{:S(2)}, u32[]{:S(2)}) collective-permute-start(f32[16,1152]{1,0:T(8,128)S(1)} %get-tuple-element.45), channel_id=1, source_target_pairs={{0,1},{1,0},{2,3},{3,2},{4,5},{5,4},{6,7},{7,6},{8,9},{9,8},{10,11... | collective-permute-start | bytes 221192 | tf_op jit(solution)/shard_map/ppermute | solution.py:851
  33.7 2.0 %collective-permute-start.8 = (f32[16,1152]{1,0:T(8,128)S(1)}, f32[16,1152]{1,0:T(8,128)S(1)}, u32[]{:S(2)}, u32[]{:S(2)}) collective-permute-start(f32[16,1152]{1,0:T(8,128)S(1)} %get-tuple-element.46), channel_id=1, source_target_pairs={{0,3},{1,2},{2,1},{3,0},{4,7},{5,6},{6,5},{7,4},{8,11},{9,10},{10,... | collective-permute-start | bytes 221192 | tf_op jit(solution)/shard_map/ppermute | solution.py:851
  35.7 0.6 %collective-permute-done.6.refs_1_ = f32[16,1152]{1,0:T(8,128)S(1)} collective-permute-done((f32[16,1152]{1,0:T(8,128)S(1)}, f32[16,1152]{1,0:T(8,128)S(1)}, u32[]{:S(2)}, u32[]{:S(2)}) %collective-permute-start.6) | collective-permute-done | bytes 73760 | tf_op jit(solution)/shard_map/ppermute | solution.py:851
  36.4 0.5 %collective-permute-done.7.refs_2_ = f32[16,1152]{1,0:T(8,128)S(1)} collective-permute-done((f32[16,1152]{1,0:T(8,128)S(1)}, f32[16,1152]{1,0:T(8,128)S(1)}, u32[]{:S(2)}, u32[]{:S(2)}) %collective-permute-start.7) | collective-permute-done | bytes 73760 | tf_op jit(solution)/shard_map/ppermute | solution.py:851
  36.9 2.2 %collective-permute-done.8.refs_3_ = f32[16,1152]{1,0:T(8,128)S(1)} collective-permute-done((f32[16,1152]{1,0:T(8,128)S(1)}, f32[16,1152]{1,0:T(8,128)S(1)}, u32[]{:S(2)}, u32[]{:S(2)}) %collective-permute-start.8) | collective-permute-done | bytes 73760 | tf_op jit(solution)/shard_map/ppermute | solution.py:851
  39.1 0.2 over.1
  39.2 0.1 collective-permute-start.9
  39.3 5.5 %collective-permute-start.10 = (f32[2,1152]{1,0:T(2,128)S(1)}, f32[2,1152]{1,0:T(2,128)S(1)}, u32[]{:S(2)}, u32[]{:S(2)}) collective-permute-start(f32[2,1152]{1,0:T(2,128)S(1)} %get-tuple-element.49), channel_id=1, source_target_pairs={{4,8},{8,4},{12,16},{16,12},{20,24},{24,20},{5,9},{9,5},{13,17},{1... | collective-permute-start | bytes 27656 | tf_op jit(solution)/shard_map/ppermute | solution.py:33
  44.8 2.7 %assemble.1 = (f32[16,16,1024]{2,1,0:T(8,128)}, f32[3,16,16,1024]{3,2,1,0:T(8,128)}) custom-call(f32[4,4,128,128]{3,2,1,0:T(8,128)S(1)} %get-tuple-element.50.whole_ref, f32[16,4,4,8,128]{4,3,2,1,0:T(8,128)S(1)} %get-tuple-element.51.lines_ref, f32[16,4,128,128]{3,2,1,0:T(8,128)S(1)} %get-tuple-element.52.late_ref), custom_call_target="tpu_custom_call" | custom-call | flops 5242880 | bytes 4194304 | tf_op jit(solution)/shard_map/assemble/pallas_call | solution.py:833
  47.6 1.1 %bilateral.1 = f32[4,16,256]{2,1,0:T(8,128)} custom-call(f32[16,1152]{1,0:T(8,128)S(1)} %get-tuple-element.47.picture_ref, f32[2,1152]{1,0:T(2,128)S(1)} %collective-permute-done.9.swap0_ref, f32[2,1152]{1,0:T(2,128)S(1)} %collective-permute-done.10.swap1_ref), custom_call_target="tpu_custom_call" | custom-call | tf_op jit(solution)/shard_map/bilateral/pallas_call | solution.py:862
  (8 shorter events, 0.0 us)
Async XLA Ops:
  3.1 15.3 %copy-start = (f32[3,4]{1,0:T(4,128)S(1)}, f32[3,4]{1,0:T(4,128)}, u32[]{:S(2)}) copy-start(f32[3,4]{1,0:T(4,128)} %palette_ref.5) | copy-start | bytes 148
  3.1 2.0 %collective-permute-start = (f32[4,16,2,8,128]{4,3,2,1,0:T(8,128)S(1)}, f32[4,16,2,8,128]{4,3,2,1,0:T(8,128)S(1)}, u32[]{:S(2)}, u32[]{:S(2)}) collective-permute-start(f32[4,16,2,8,128]{4,3,2,1,0:T(8,128)S(1)} %get-tuple-element.30), channel_id=1, source_target_pairs={{0,4},{4,0},{8,12},{12,8},{16,20},{20,16},{24,28},{28,24},{1,5},{5... | collective-permute-start | bytes 1572872 | tf_op jit(solution)/shard_map/ppermute | solution.py:33
  5.1 23.0 %collective-permute-start.1 = (f32[4,264,128]{2,1,0:T(8,128)S(1)}, f32[4,264,128]{2,1,0:T(8,128)S(1)}, u32[]{:S(2)}, u32[]{:S(2)}) collective-permute-start(f32[4,264,128]{2,1,0:T(8,128)S(1)} %get-tuple-element.31), channel_id=1, source_target_pairs={{0,1},{1,0},{2,3},{3,2},{4,5},{5,4},{6,7},{7,6},{8,9},{9,8},{10,11... | collective-permute-start | bytes 1622024 | tf_op jit(solution)/shard_map/ppermute | solution.py:37
  7.6 20.5 %collective-permute-start.2 = (f32[4,264,128]{2,1,0:T(8,128)S(1)}, f32[4,264,128]{2,1,0:T(8,128)S(1)}, u32[]{:S(2)}, u32[]{:S(2)}) collective-permute-start(f32[4,264,128]{2,1,0:T(8,128)S(1)} %get-tuple-element.32), channel_id=1, source_target_pairs={{1,2},{2,1},{5,6},{6,5},{9,10},{10,9},{13,14},{14,13},{17,18},{18,... | collective-permute-start | bytes 1622024 | tf_op jit(solution)/shard_map/ppermute | solution.py:37
  8.3 17.1 %collective-permute-start.5 = (f32[4,16,2,8,128]{4,3,2,1,0:T(8,128)S(1)}, f32[4,16,2,8,128]{4,3,2,1,0:T(8,128)S(1)}, u32[]{:S(2)}, u32[]{:S(2)}) collective-permute-start(f32[4,16,2,8,128]{4,3,2,1,0:T(8,128)S(1)} %get-tuple-element.39), channel_id=1, source_target_pairs={{4,8},{8,4},{12,16},{16,12},{20,24},{24,20},{5,9},{9,5},{13,17},{1... | collective-permute-start | bytes 1572872 | tf_op jit(solution)/shard_map/ppermute | solution.py:33
  12.0 16.1 %collective-permute-start.3 = (f32[4,8,128]{2,1,0:T(8,128)S(1)}, f32[4,8,128]{2,1,0:T(8,128)S(1)}, u32[]{:S(2)}, u32[]{:S(2)}) collective-permute-start(f32[4,8,128]{2,1,0:T(8,128)S(1)} %get-tuple-element.33), channel_id=1, source_target_pairs={{4,9},{5,8},{6,11},{7,10},{8,5},{9,4},{10,7},{11,6},{12,17},{13,16... | collective-permute-start | bytes 49160 | tf_op jit(solution)/shard_map/ppermute | solution.py:47
  17.7 10.4 %collective-permute-start.4 = (f32[4,8,128]{2,1,0:T(8,128)S(1)}, f32[4,8,128]{2,1,0:T(8,128)S(1)}, u32[]{:S(2)}, u32[]{:S(2)}) collective-permute-start(f32[4,8,128]{2,1,0:T(8,128)S(1)} %get-tuple-element.34), channel_id=1, source_target_pairs={{5,10},{6,9},{9,6},{10,5},{13,18},{14,17},{17,14},{18,13},{21,26},... | collective-permute-start | bytes 49160 | tf_op jit(solution)/shard_map/ppermute | solution.py:47
  30.7 5.7 %collective-permute-start.6 = (f32[16,1152]{1,0:T(8,128)S(1)}, f32[16,1152]{1,0:T(8,128)S(1)}, u32[]{:S(2)}, u32[]{:S(2)}) collective-permute-start(f32[16,1152]{1,0:T(8,128)S(1)} %get-tuple-element.44), channel_id=1, source_target_pairs={{0,2},{1,3},{2,0},{3,1},{4,6},{5,7},{6,4},{7,5},{8,10},{9,11},{10,... | collective-permute-start | bytes 221192 | tf_op jit(solution)/shard_map/ppermute | solution.py:851
  33.2 3.7 %collective-permute-start.7 = (f32[16,1152]{1,0:T(8,128)S(1)}, f32[16,1152]{1,0:T(8,128)S(1)}, u32[]{:S(2)}, u32[]{:S(2)}) collective-permute-start(f32[16,1152]{1,0:T(8,128)S(1)} %get-tuple-element.45), channel_id=1, source_target_pairs={{0,1},{1,0},{2,3},{3,2},{4,5},{5,4},{6,7},{7,6},{8,9},{9,8},{10,11... | collective-permute-start | bytes 221192 | tf_op jit(solution)/shard_map/ppermute | solution.py:851
  33.7 5.3 %collective-permute-start.8 = (f32[16,1152]{1,0:T(8,128)S(1)}, f32[16,1152]{1,0:T(8,128)S(1)}, u32[]{:S(2)}, u32[]{:S(2)}) collective-permute-start(f32[16,1152]{1,0:T(8,128)S(1)} %get-tuple-element.46), channel_id=1, source_target_pairs={{0,3},{1,2},{2,1},{3,0},{4,7},{5,6},{6,5},{7,4},{8,11},{9,10},{10,... | collective-permute-start | bytes 221192 | tf_op jit(solution)/shard_map/ppermute | solution.py:851
  39.2 8.3 %collective-permute-start.9 = (f32[2,1152]{1,0:T(2,128)S(1)}, f32[2,1152]{1,0:T(2,128)S(1)}, u32[]{:S(2)}, u32[]{:S(2)}) collective-permute-start(f32[2,1152]{1,0:T(2,128)S(1)} %get-tuple-element.48), channel_id=1, source_target_pairs={{0,4},{4,0},{8,12},{12,8},{16,20},{20,16},{24,28},{28,24},{1,5},{5... | collective-permute-start | bytes 27656 | tf_op jit(solution)/shard_map/ppermute | solution.py:33
  39.3 8.2 %collective-permute-start.10 = (f32[2,1152]{1,0:T(2,128)S(1)}, f32[2,1152]{1,0:T(2,128)S(1)}, u32[]{:S(2)}, u32[]{:S(2)}) collective-permute-start(f32[2,1152]{1,0:T(2,128)S(1)} %get-tuple-element.49), channel_id=1, source_target_pairs={{4,8},{8,4},{12,16},{16,12},{20,24},{24,20},{5,9},{9,5},{13,17},{1... | collective-permute-start | bytes 27656 | tf_op jit(solution)/shard_map/ppermute | solution.py:33

commit v4 on v3

--- a/solution.py
+++ b/solution.py
@@ -19,7 +19,6 @@
 SUB = 8
 LANES = 128
 PITCH = 40
-AXES = ("row", "depth")
 
 
 def row_pairs(kind, count):
@@ -37,26 +36,15 @@
     return lax.ppermute(array, "depth", row_pairs(kind, lax.axis_size("depth")))
 
 
-def swap_corners(array, row_kind, depth_kind):
-    depths = lax.axis_size("depth")
-    pairs = [
-        (a * depths + c, b * depths + d)
-        for a, b in row_pairs(row_kind, lax.axis_size("row"))
-        for c, d in row_pairs(depth_kind, depths)
-    ]
-    return lax.ppermute(array, AXES, pairs)
-
-
 def in_vmem(array):
     return pltpu.with_memory_space_constraint(array, pltpu.VMEM)
 
 
 def pack_kernel(
-    den_ref, vel_ref, block, row0_ref, row1_ref, c10_ref, c11_ref, sides, load_sem,
+    den_ref, vel_ref, block, row0_ref, row1_ref, corner_ref, sides, load_sem,
     *, layers, rows, spans, chunks,
 ):
     row_odd = lax.rem(lax.axis_index("row"), 2)
-    depth_odd = lax.rem(lax.axis_index("depth"), 2)
     size = layers // chunks
 
     def loads(k):
@@ -86,12 +74,12 @@
                 for n in range(2):
                     row0_ref[c, z, n] = sides[1 - row_odd, c, z, n]
                     row1_ref[c, z, n] = sides[row_odd, c, z, n]
-    for target, side in ((c10_ref, 1 - depth_odd), (c11_ref, depth_odd)):
+    for n in range(2):
         for c in range(4):
-            target[c] = row1_ref[c, side * (layers - 1), row_odd]
-
-
-def pack_depth_kernel(block, row0_ref, depth0_ref, depth1_ref, *, layers, rows, spans):
+            corner_ref[n, c] = row1_ref[c, n * (layers - 1), row_odd]
+
+
+def pack_depth_kernel(block, row0_ref, corner_ref, depth0_ref, depth1_ref, *, layers, rows, spans):
     row_odd = lax.rem(lax.axis_index("row"), 2)
     depth_odd = lax.rem(lax.axis_index("depth"), 2)
     for target, side in ((depth0_ref, 1 - depth_odd), (depth1_ref, depth_odd)):
@@ -105,6 +93,7 @@
             target[c, pl.ds(2 * spans * rows, spans), :] = row0_ref[
                 c, side * (layers - 1), row_odd
             ]
+            target[c, pl.ds((2 * rows + 1) * spans, spans), :] = corner_ref[side, c]
 
 
 def row_of(j, row):
@@ -356,7 +345,7 @@
 
 
 def settle_kernel(
-    palette_ref, block, depth0_ref, depth1_ref, c10_ref, c11_ref,
+    palette_ref, block, depth0_ref, depth1_ref,
     early_ref, share_ref, edge_ref, part_ref, rows_part_ref, given_rowbuf, given_srow,
     whole_ref, rowbuf, srow, *rest,
     layers, rows, columns, depth_count, row_count,
@@ -435,16 +424,13 @@
                 whole_ref[n, c, cells_of(t, j), :] = new[c]
             render(accum, cells_of(t, j), new, rate, mix)
 
-    beside = pl.ds(2 * spans * rows, spans)
-    corners = (
-        (0, 0, lambda c: depth0_ref[c, beside, :]), (0, 1, lambda c: depth1_ref[c, beside, :]),
-        (1, 0, lambda c: c10_ref[c]), (1, 1, lambda c: c11_ref[c]),
-    )
-    for row_kind, depth_kind, source in corners:
+    for row_kind, depth_kind in ((0, 0), (0, 1), (1, 0), (1, 1)):
+        received = depth0_ref if depth_kind == 0 else depth1_ref
+        beside = pl.ds((2 * rows + row_kind) * spans, spans)
         is_above = row_odd if row_kind == 0 else 1 - row_odd
         is_front = depth_odd if depth_kind == 0 else 1 - depth_odd
         for c in range(4):
-            rowbuf[row_kind, c, (1 - is_front) * (layers + 1), is_above] = source(c)
+            rowbuf[row_kind, c, (1 - is_front) * (layers + 1), is_above] = received[c, beside, :]
     for c in range(3):
         accum[c] = jnp.zeros((spans * rows, LANES), jnp.float32)
     accum[3] = jnp.ones((spans * rows, LANES), jnp.float32)
@@ -729,16 +715,16 @@
         return pltpu.CompilerParams(vmem_limit_bytes=mebibytes << 20)
 
     row_shape = (4, layers, 2, spans, LANES)
-    depth_shape = (4, (2 * rows + 1) * spans, LANES)
-    corner_shape = (4, spans, LANES)
-    block, row0, row1, corner0, corner1 = pl.pallas_call(
+    depth_shape = (4, (2 * rows + 2) * spans, LANES)
+    corner_shape = (2, 4, spans, LANES)
+    block, row0, row1, corner = pl.pallas_call(
         functools.partial(pack_kernel, layers=layers, rows=rows, spans=spans, chunks=4),
         out_shape=(
             local(4, layers, rows, columns), local(*row_shape), local(*row_shape),
-            local(*corner_shape), local(*corner_shape),
+            local(*corner_shape),
         ),
         in_specs=[pl.BlockSpec(memory_space=pltpu.HBM)] * 2,
-        out_specs=(vmem,) * 5,
+        out_specs=(vmem,) * 4,
         scratch_shapes=[pltpu.VMEM((2,) + row_shape, f32), pltpu.SemaphoreType.DMA((4, 2))],
         name="pack",
         compiler_params=params(8),
@@ -746,18 +732,18 @@
         pltpu.with_memory_space_constraint(density, pltpu.HBM),
         pltpu.with_memory_space_constraint(velocity, pltpu.HBM),
     )
+    corner = swap_rows(corner, 1)
     row1 = swap_rows(row1, 1)
     row0 = swap_rows(row0, 0)
     depth0, depth1 = pl.pallas_call(
         functools.partial(pack_depth_kernel, layers=layers, rows=rows, spans=spans),
         out_shape=(local(*depth_shape), local(*depth_shape)),
-        in_specs=[vmem] * 2,
+        in_specs=[vmem] * 3,
         out_specs=(vmem,) * 2,
         name="pack_depth",
         compiler_params=params(8),
-    )(in_vmem(block), in_vmem(row0))
+    )(in_vmem(block), in_vmem(row0), in_vmem(corner))
     depth0, depth1 = swap_depths(depth0, 0), swap_depths(depth1, 1)
-    corner0, corner1 = swap_corners(corner0, 1, 0), swap_corners(corner1, 1, 1)
 
     early, share, edge, late, part = pl.pallas_call(
         functools.partial(
@@ -809,9 +795,9 @@
         ),
         out_shape=(local(4, 4, spans * rows, LANES), local(*rowbuf_shape), local(*srow_shape))
         + (local(rows, line),) * depth_count,
-        in_specs=[smem] + [vmem] * 12,
+        in_specs=[smem] + [vmem] * 10,
         out_specs=(vmem,) * (3 + depth_count),
-        input_output_aliases={11: 1, 12: 2},
+        input_output_aliases={9: 1, 10: 2},
         scratch_shapes=[
             pltpu.VMEM((3, 4, spans * PITCH, LANES), f32),
             pltpu.VMEM((4, 4, spans * PITCH, LANES), f32),
@@ -824,7 +810,7 @@
         *(
             in_vmem(x)
             for x in (
-                block, depth0, depth1, corner0, corner1, early, share, edge, part, rows_part,
+                block, depth0, depth1, early, share, edge, part, rows_part,
                 rowbuf, srow,
             )
         ),

time: 48.9 us -> 51.4 us (1.051)
  waiting for transfers between devices: 5.22 us -> 10.1 us
  starting transfers between devices: 23.9 us -> 21.5 us
    ppermute x2 -> x0, starting transfers between devices: 6.38 us -> none  [swap_corners(): return lax.ppermute(array, AXES, pairs)]
    ppermute x4 -> x5, waiting for transfers between devices: 1.9 us -> 6.79 us  [swap_rows(): return lax.ppermute(array, 'row', row_pairs(kind, lax.axis_size('row')))]
    ppermute x4 -> x5, starting transfers between devices: 9.3 us -> 13 us  [swap_rows(): return lax.ppermute(array, 'row', row_pairs(kind, lax.axis_size('row')))]
    ppermute x3, starting transfers between devices: 5.02 us -> 5.83 us  [compute(): lax.ppermute(parts[k], 'depth', [(i, i ^ k) for i in range(depth_count)])]
  transfers between devices with their start and end apart: 11 -> 10, of which waited for: 4 -> 4; matrix products, arithmetic and copies ran while one was open for 0% -> 0% of each run, Pallas kernels for 26% -> 24%
where the time goes in v4:
time: 51.4 us; the launch traced here: 51.1 us
  starting transfers between devices  21.5 us (42%)
  Pallas kernels  18.7 us (36%)
  waiting for transfers between devices  10.1 us (20%)
  between operations  0.74 us (1%)
    ppermute x5, starting transfers between devices, swap_rows(): return lax.ppermute(array, 'row', row_pairs(kind, lax.axis_size('row')))  13 us
    pallas_call x1, Pallas kernels, compute(): pl.pallas_call(functools.partial(interior_kernel, layers=layers, rows=row...  7.05 us
    ppermute x5, waiting for transfers between devices, swap_rows(): return lax.ppermute(array, 'row', row_pairs(kind, lax.axis_size('row')))  6.79 us
    ppermute x3, starting transfers between devices, compute(): lax.ppermute(parts[k], 'depth', [(i, i ^ k) for i in range(depth_count)])  5.83 us
    ppermute x3, waiting for transfers between devices, compute(): lax.ppermute(parts[k], 'depth', [(i, i ^ k) for i in range(depth_count)])  3.31 us
    pallas_call x1, Pallas kernels, compute(): pl.pallas_call(functools.partial(assemble_kernel, layers=layers, rows=row...  2.75 us
    ppermute x2, starting transfers between devices, swap_depths(): return lax.ppermute(array, 'depth', row_pairs(kind, lax.axis_size('depth')))  2.71 us
    pallas_call x1, Pallas kernels, compute(): pl.pallas_call(functools.partial(outer_kernel, layers=layers, rows=rows,...  2.65 us
  transfers between devices with their start and end apart: 10, of which 4 were waited for; matrix products, arithmetic and copies ran while one was open for 0% of the time, Pallas kernels for 24%

profile of v4, /device:TPU:1, one launch (start us, length us, event | category | flops | bytes accessed | tf_op | source)
XLA Modules:
  0.0 51.1 jit_solution(12101666198064681252)
XLA Ops:
  0.6 2.4 %pack.1 = (f32[4,16,16,1024]{3,2,1,0:T(8,128)S(1)}, f32[4,16,2,8,128]{4,3,2,1,0:T(8,128)S(1)}, f32[4,16,2,8,128]{4,3,2,1,0:T(8,128)S(1)}, f32[2,4,8,128]{3,2,1,0:T(8,128)S(1)}) custom-call(f32[16,16,1024]{2,1,0:T(8,128)} %den_ref.1, f32[3,16,16,1024]{3,2,1,0:T(8,128)} %vel_ref.1), custom_call_target="tpu_custom_call" | custom-call | tf_op jit(solution)/shard_map/pack/pallas_call | solution.py:720
  3.1 0.0 copy-start
  3.1 0.1 collective-permute-start
  3.2 4.5 %collective-permute-start.1 = (f32[2,4,8,128]{3,2,1,0:T(8,128)S(1)}, f32[2,4,8,128]{3,2,1,0:T(8,128)S(1)}, u32[]{:S(2)}, u32[]{:S(2)}) collective-permute-start(f32[2,4,8,128]{3,2,1,0:T(8,128)S(1)} %get-tuple-element.30), channel_id=1, source_target_pairs={{4,8},{8,4},{12,16},{16,12},{20,24},{24,20},{5,9},{9,5},{13,17},{1... | collective-permute-start | bytes 98312 | tf_op jit(solution)/shard_map/ppermute | solution.py:32
  7.7 1.9 %collective-permute-done.1.corner_ref = f32[2,4,8,128]{3,2,1,0:T(8,128)S(1)} collective-permute-done((f32[2,4,8,128]{3,2,1,0:T(8,128)S(1)}, f32[2,4,8,128]{3,2,1,0:T(8,128)S(1)}, u32[]{:S(2)}, u32[]{:S(2)}) %collective-permute-start.1) | collective-permute-done | bytes 32800 | tf_op jit(solution)/shard_map/ppermute | solution.py:32
  9.6 0.1 pack_depth.1
  9.6 2.0 %collective-permute-start.2 = (f32[4,272,128]{2,1,0:T(8,128)S(1)}, f32[4,272,128]{2,1,0:T(8,128)S(1)}, u32[]{:S(2)}, u32[]{:S(2)}) collective-permute-start(f32[4,272,128]{2,1,0:T(8,128)S(1)} %get-tuple-element.31), channel_id=1, source_target_pairs={{0,1},{1,0},{2,3},{3,2},{4,5},{5,4},{6,7},{7,6},{8,9},{9,8},{10,11... | collective-permute-start | bytes 1671176 | tf_op jit(solution)/shard_map/ppermute | solution.py:36
  11.7 0.7 %collective-permute-start.3 = (f32[4,272,128]{2,1,0:T(8,128)S(1)}, f32[4,272,128]{2,1,0:T(8,128)S(1)}, u32[]{:S(2)}, u32[]{:S(2)}) collective-permute-start(f32[4,272,128]{2,1,0:T(8,128)S(1)} %get-tuple-element.32), channel_id=1, source_target_pairs={{1,2},{2,1},{5,6},{6,5},{9,10},{10,9},{13,14},{14,13},{17,18},{18,... | collective-permute-start | bytes 1671176 | tf_op jit(solution)/shard_map/ppermute | solution.py:36
  12.4 3.0 %collective-permute-start.4 = (f32[4,16,2,8,128]{4,3,2,1,0:T(8,128)S(1)}, f32[4,16,2,8,128]{4,3,2,1,0:T(8,128)S(1)}, u32[]{:S(2)}, u32[]{:S(2)}) collective-permute-start(f32[4,16,2,8,128]{4,3,2,1,0:T(8,128)S(1)} %get-tuple-element.37), channel_id=1, source_target_pairs={{4,8},{8,4},{12,16},{16,12},{20,24},{24,20},{5,9},{9,5},{13,17},{1... | collective-permute-start | bytes 1572872 | tf_op jit(solution)/shard_map/ppermute | solution.py:32
  15.3 7.0 %interior.1 = (f32[16,4,128,128]{3,2,1,0:T(8,128)S(1)}, f32[16,128,128]{2,1,0:T(8,128)S(1)}, f32[16,2,4,8,128]{4,3,2,1,0:T(8,128)S(1)}, f32[16,4,128,128]{3,2,1,0:T(8,128)S(1)}, f32[4,128,128]{2,1,0:T(8,128)S(1)}) custom-call(f32[3,4]{1,0:T(4,128)S(1)} %copy-done, f32[4,16,16,1024]{3,2,1,0:T(8,128)S(1)} %get-tuple-element.28.block), custom_call_target="tpu_custom_call" | custom-call | flops 20971520 | bytes 4194304 | tf_op jit(solution)/shard_map/interior/pallas_call | solution.py:748
  22.4 4.9 %collective-permute-done.4.row1_ref = f32[4,16,2,8,128]{4,3,2,1,0:T(8,128)S(1)} collective-permute-done((f32[4,16,2,8,128]{4,3,2,1,0:T(8,128)S(1)}, f32[4,16,2,8,128]{4,3,2,1,0:T(8,128)S(1)}, u32[]{:S(2)}, u32[]{:S(2)}) %collective-permute-start.4) | collective-permute-done | bytes 524320 | tf_op jit(solution)/shard_map/ppermute | solution.py:32
  27.3 2.7 %outer.1 = (f32[2,4,18,2,8,128]{5,4,3,2,1,0:T(8,128)S(1)}, f32[16,4,4,8,128]{4,3,2,1,0:T(8,128)S(1)}, f32[16,4,4,8,128]{4,3,2,1,0:T(8,128)S(1)}, f32[4,32,128]{2,1,0:T(8,128)S(1)}) custom-call(f32[3,4]{1,0:T(4,128)S(1)} %copy-done, f32[4,16,2,8,128]{4,3,2,1,0:T(8,128)S(1)} %collective-permute-done.row0_ref, ...), custom_call_target="tpu_custom_call" | custom-call | flops 10485760 | bytes 1048576 | tf_op jit(solution)/shard_map/outer/pallas_call | solution.py:772
  30.0 0.0 collective-permute-done.3.depth1_ref
  30.0 2.5 %settle.1 = (f32[4,4,128,128]{3,2,1,0:T(8,128)S(1)}, f32[2,4,18,2,8,128]{5,4,3,2,1,0:T(8,128)S(1)}, f32[16,4,4,8,128]{4,3,2,1,0:T(8,128)S(1)}, f32[16,1152]{1,0:...) custom-call(f32[3,4]{1,0:T(4,128)S(1)} %copy-done, ...), custom_call_target="tpu_custom_call", output_to_operand_aliasing={{1}: (9, {}), {2}: (10, {})} | custom-call | tf_op jit(solution)/shard_map/settle/pallas_call | solution.py:791
  32.5 3.9 %collective-permute-start.5 = (f32[16,1152]{1,0:T(8,128)S(1)}, f32[16,1152]{1,0:T(8,128)S(1)}, u32[]{:S(2)}, u32[]{:S(2)}) collective-permute-start(f32[16,1152]{1,0:T(8,128)S(1)} %get-tuple-element.42), channel_id=1, source_target_pairs={{0,2},{1,3},{2,0},{3,1},{4,6},{5,7},{6,4},{7,5},{8,10},{9,11},{10,... | collective-permute-start | bytes 221192 | tf_op jit(solution)/shard_map/ppermute | solution.py:837
  36.4 0.0 collective-permute-start.6
  36.4 1.9 %collective-permute-start.7 = (f32[16,1152]{1,0:T(8,128)S(1)}, f32[16,1152]{1,0:T(8,128)S(1)}, u32[]{:S(2)}, u32[]{:S(2)}) collective-permute-start(f32[16,1152]{1,0:T(8,128)S(1)} %get-tuple-element.44), channel_id=1, source_target_pairs={{0,3},{1,2},{2,1},{3,0},{4,7},{5,6},{6,5},{7,4},{8,11},{9,10},{10,... | collective-permute-start | bytes 221192 | tf_op jit(solution)/shard_map/ppermute | solution.py:837
  38.3 1.3 %collective-permute-done.6.refs_2_ = f32[16,1152]{1,0:T(8,128)S(1)} collective-permute-done((f32[16,1152]{1,0:T(8,128)S(1)}, f32[16,1152]{1,0:T(8,128)S(1)}, u32[]{:S(2)}, u32[]{:S(2)}) %collective-permute-start.6) | collective-permute-done | bytes 73760 | tf_op jit(solution)/shard_map/ppermute | solution.py:837
  39.6 2.0 %collective-permute-done.7.refs_3_ = f32[16,1152]{1,0:T(8,128)S(1)} collective-permute-done((f32[16,1152]{1,0:T(8,128)S(1)}, f32[16,1152]{1,0:T(8,128)S(1)}, u32[]{:S(2)}, u32[]{:S(2)}) %collective-permute-start.7) | collective-permute-done | bytes 73760 | tf_op jit(solution)/shard_map/ppermute | solution.py:837
  41.7 0.2 over.1
  41.8 0.1 collective-permute-start.8
  41.9 5.4 %collective-permute-start.9 = (f32[2,1152]{1,0:T(2,128)S(1)}, f32[2,1152]{1,0:T(2,128)S(1)}, u32[]{:S(2)}, u32[]{:S(2)}) collective-permute-start(f32[2,1152]{1,0:T(2,128)S(1)} %get-tuple-element.47), channel_id=1, source_target_pairs={{4,8},{8,4},{12,16},{16,12},{20,24},{24,20},{5,9},{9,5},{13,17},{1... | collective-permute-start | bytes 27656 | tf_op jit(solution)/shard_map/ppermute | solution.py:32
  47.3 2.7 %assemble.1 = (f32[16,16,1024]{2,1,0:T(8,128)}, f32[3,16,16,1024]{3,2,1,0:T(8,128)}) custom-call(f32[4,4,128,128]{3,2,1,0:T(8,128)S(1)} %get-tuple-element.48.whole_ref, f32[16,4,4,8,128]{4,3,2,1,0:T(8,128)S(1)} %get-tuple-element.49.lines_ref, f32[16,4,128,128]{3,2,1,0:T(8,128)S(1)} %get-tuple-element.50.late_ref), custom_call_target="tpu_custom_call" | custom-call | flops 5242880 | bytes 4194304 | tf_op jit(solution)/shard_map/assemble/pallas_call | solution.py:819
  50.1 1.1 %bilateral.1 = f32[4,16,256]{2,1,0:T(8,128)} custom-call(f32[16,1152]{1,0:T(8,128)S(1)} %get-tuple-element.45.picture_ref, f32[2,1152]{1,0:T(2,128)S(1)} %collective-permute-done.8.swap0_ref, f32[2,1152]{1,0:T(2,128)S(1)} %collective-permute-done.9.swap1_ref), custom_call_target="tpu_custom_call" | custom-call | tf_op jit(solution)/shard_map/bilateral/pallas_call | solution.py:848
  (6 shorter events, 0.0 us)
Async XLA Ops:
  3.1 12.2 %copy-start = (f32[3,4]{1,0:T(4,128)S(1)}, f32[3,4]{1,0:T(4,128)}, u32[]{:S(2)}) copy-start(f32[3,4]{1,0:T(4,128)} %palette_ref.5) | copy-start | bytes 148
  3.1 6.5 %collective-permute-start = (f32[4,16,2,8,128]{4,3,2,1,0:T(8,128)S(1)}, f32[4,16,2,8,128]{4,3,2,1,0:T(8,128)S(1)}, u32[]{:S(2)}, u32[]{:S(2)}) collective-permute-start(f32[4,16,2,8,128]{4,3,2,1,0:T(8,128)S(1)} %get-tuple-element.29), channel_id=1, source_target_pairs={{0,4},{4,0},{8,12},{12,8},{16,20},{20,16},{24,28},{28,24},{1,5},{5... | collective-permute-start | bytes 1572872 | tf_op jit(solution)/shard_map/ppermute | solution.py:32
  3.2 6.4 %collective-permute-start.1 = (f32[2,4,8,128]{3,2,1,0:T(8,128)S(1)}, f32[2,4,8,128]{3,2,1,0:T(8,128)S(1)}, u32[]{:S(2)}, u32[]{:S(2)}) collective-permute-start(f32[2,4,8,128]{3,2,1,0:T(8,128)S(1)} %get-tuple-element.30), channel_id=1, source_target_pairs={{4,8},{8,4},{12,16},{16,12},{20,24},{24,20},{5,9},{9,5},{13,17},{1... | collective-permute-start | bytes 98312 | tf_op jit(solution)/shard_map/ppermute | solution.py:32
  9.6 20.3 %collective-permute-start.2 = (f32[4,272,128]{2,1,0:T(8,128)S(1)}, f32[4,272,128]{2,1,0:T(8,128)S(1)}, u32[]{:S(2)}, u32[]{:S(2)}) collective-permute-start(f32[4,272,128]{2,1,0:T(8,128)S(1)} %get-tuple-element.31), channel_id=1, source_target_pairs={{0,1},{1,0},{2,3},{3,2},{4,5},{5,4},{6,7},{7,6},{8,9},{9,8},{10,11... | collective-permute-start | bytes 1671176 | tf_op jit(solution)/shard_map/ppermute | solution.py:36
  11.7 18.3 %collective-permute-start.3 = (f32[4,272,128]{2,1,0:T(8,128)S(1)}, f32[4,272,128]{2,1,0:T(8,128)S(1)}, u32[]{:S(2)}, u32[]{:S(2)}) collective-permute-start(f32[4,272,128]{2,1,0:T(8,128)S(1)} %get-tuple-element.32), channel_id=1, source_target_pairs={{1,2},{2,1},{5,6},{6,5},{9,10},{10,9},{13,14},{14,13},{17,18},{18,... | collective-permute-start | bytes 1671176 | tf_op jit(solution)/shard_map/ppermute | solution.py:36
  12.4 14.9 %collective-permute-start.4 = (f32[4,16,2,8,128]{4,3,2,1,0:T(8,128)S(1)}, f32[4,16,2,8,128]{4,3,2,1,0:T(8,128)S(1)}, u32[]{:S(2)}, u32[]{:S(2)}) collective-permute-start(f32[4,16,2,8,128]{4,3,2,1,0:T(8,128)S(1)} %get-tuple-element.37), channel_id=1, source_target_pairs={{4,8},{8,4},{12,16},{16,12},{20,24},{24,20},{5,9},{9,5},{13,17},{1... | collective-permute-start | bytes 1572872 | tf_op jit(solution)/shard_map/ppermute | solution.py:32
  32.5 5.8 %collective-permute-start.5 = (f32[16,1152]{1,0:T(8,128)S(1)}, f32[16,1152]{1,0:T(8,128)S(1)}, u32[]{:S(2)}, u32[]{:S(2)}) collective-permute-start(f32[16,1152]{1,0:T(8,128)S(1)} %get-tuple-element.42), channel_id=1, source_target_pairs={{0,2},{1,3},{2,0},{3,1},{4,6},{5,7},{6,4},{7,5},{8,10},{9,11},{10,... | collective-permute-start | bytes 221192 | tf_op jit(solution)/shard_map/ppermute | solution.py:837
  36.4 3.2 %collective-permute-start.6 = (f32[16,1152]{1,0:T(8,128)S(1)}, f32[16,1152]{1,0:T(8,128)S(1)}, u32[]{:S(2)}, u32[]{:S(2)}) collective-permute-start(f32[16,1152]{1,0:T(8,128)S(1)} %get-tuple-element.43), channel_id=1, source_target_pairs={{0,1},{1,0},{2,3},{3,2},{4,5},{5,4},{6,7},{7,6},{8,9},{9,8},{10,11... | collective-permute-start | bytes 221192 | tf_op jit(solution)/shard_map/ppermute | solution.py:837
  36.4 5.2 %collective-permute-start.7 = (f32[16,1152]{1,0:T(8,128)S(1)}, f32[16,1152]{1,0:T(8,128)S(1)}, u32[]{:S(2)}, u32[]{:S(2)}) collective-permute-start(f32[16,1152]{1,0:T(8,128)S(1)} %get-tuple-element.44), channel_id=1, source_target_pairs={{0,3},{1,2},{2,1},{3,0},{4,7},{5,6},{6,5},{7,4},{8,11},{9,10},{10,... | collective-permute-start | bytes 221192 | tf_op jit(solution)/shard_map/ppermute | solution.py:837
  41.8 8.2 %collective-permute-start.8 = (f32[2,1152]{1,0:T(2,128)S(1)}, f32[2,1152]{1,0:T(2,128)S(1)}, u32[]{:S(2)}, u32[]{:S(2)}) collective-permute-start(f32[2,1152]{1,0:T(2,128)S(1)} %get-tuple-element.46), channel_id=1, source_target_pairs={{0,4},{4,0},{8,12},{12,8},{16,20},{20,16},{24,28},{28,24},{1,5},{5... | collective-permute-start | bytes 27656 | tf_op jit(solution)/shard_map/ppermute | solution.py:32
  41.9 8.2 %collective-permute-start.9 = (f32[2,1152]{1,0:T(2,128)S(1)}, f32[2,1152]{1,0:T(2,128)S(1)}, u32[]{:S(2)}, u32[]{:S(2)}) collective-permute-start(f32[2,1152]{1,0:T(2,128)S(1)} %get-tuple-element.47), channel_id=1, source_target_pairs={{4,8},{8,4},{12,16},{16,12},{20,24},{24,20},{5,9},{9,5},{13,17},{1... | collective-permute-start | bytes 27656 | tf_op jit(solution)/shard_map/ppermute | solution.py:32

commit v5 on v3

--- a/solution.py
+++ b/solution.py
@@ -344,15 +344,17 @@
     def edges(z):
         edge_rows(z, rowbuf, early_ref, share_ref, edge_ref, srow, places, rows, spans)
 
-    @pl.loop(0, (layers - 2) // 2)
-    def _(pair):
-        edges(2 * pair + 1)
-        edges(2 * pair + 2)
-
-    @pl.loop(0, (layers - 4) // 2)
-    def _(pair):
-        outer_rows(2 * pair + 2)
-        outer_rows(2 * pair + 3)
+    by = 7 if (layers - 2) % 7 == 0 else 2
+
+    @pl.loop(0, (layers - 2) // by)
+    def _(group):
+        for n in range(by):
+            edges(by * group + n + 1)
+
+    @pl.loop(0, (layers - 4) // 4)
+    def _(group):
+        for n in range(4):
+            outer_rows(4 * group + n + 2)
 
 
 def settle_kernel(

time: 48.9 us -> 48.4 us (0.990)
  Pallas kernels: 18.8 us -> 18.3 us
  transfers between devices with their start and end apart: 11 -> 11, of which waited for: 4 -> 4; matrix products, arithmetic and copies ran while one was open for 0% -> 0% of each run, Pallas kernels for 26% -> 25%
where the time goes in v5:
time: 48.4 us; the launch traced here: 48.2 us
  starting transfers between devices  23.9 us (49%)
  Pallas kernels  18.3 us (38%)
  waiting for transfers between devices  5.22 us (11%)
  between operations  0.77 us (2%)
    ppermute x4, starting transfers between devices, swap_rows(): return lax.ppermute(array, 'row', row_pairs(kind, lax.axis_size('row')))  9.3 us
    pallas_call x1, Pallas kernels, compute(): pl.pallas_call(functools.partial(interior_kernel, layers=layers, rows=row...  7.05 us
    ppermute x2, starting transfers between devices, swap_corners(): return lax.ppermute(array, AXES, pairs)  6.38 us
    ppermute x3, starting transfers between devices, compute(): lax.ppermute(parts[k], 'depth', [(i, i ^ k) for i in range(depth_count)])  5.02 us
    ppermute x3, waiting for transfers between devices, compute(): lax.ppermute(parts[k], 'depth', [(i, i ^ k) for i in range(depth_count)])  3.31 us
    ppermute x2, starting transfers between devices, swap_depths(): return lax.ppermute(array, 'depth', row_pairs(kind, lax.axis_size('depth')))  3.16 us
    pallas_call x1, Pallas kernels, compute(): pl.pallas_call(functools.partial(assemble_kernel, layers=layers, rows=row...  2.75 us
    pallas_call x1, Pallas kernels, compute(): pl.pallas_call(functools.partial(settle_kernel, layers=layers, rows=rows,...  2.55 us
  transfers between devices with their start and end apart: 11, of which 4 were waited for; matrix products, arithmetic and copies ran while one was open for 0% of the time, Pallas kernels for 25%

profile of v5, /device:TPU:1, one launch (start us, length us, event | category | flops | bytes accessed | tf_op | source)
XLA Modules:
  0.0 48.2 jit_solution(7782205649479720252)
XLA Ops:
  0.6 2.4 %pack.1 = (f32[4,16,16,1024]{3,2,1,0:T(8,128)S(1)}, f32[4,16,2,8,128]{4,3,2,1,0:T(8,128)S(1)}, f32[4,16,2,8,128]{4,3,2,1,0:T(8,128)S(1)}, f32[4,8,128]{2,1,0:T(8,128)S(1)}, f32[4,8,128]{2,1,0:T(8,128)S(1)}) custom-call(f32[16,16,1024]{2,1,0:T(8,128)} %den_ref.1, f32[3,16,16,1024]{3,2,1,0:T(8,128)} %vel_ref.1), custom_call_target="tpu_custom_call" | custom-call | tf_op jit(solution)/shard_map/pack/pallas_call | solution.py:736
  3.1 0.0 copy-start
  3.1 0.1 collective-permute-start
  3.2 1.9 %collective-permute-done.row0_ref = f32[4,16,2,8,128]{4,3,2,1,0:T(8,128)S(1)} collective-permute-done((f32[4,16,2,8,128]{4,3,2,1,0:T(8,128)S(1)}, f32[4,16,2,8,128]{4,3,2,1,0:T(8,128)S(1)}, u32[]{:S(2)}, u32[]{:S(2)}) %collective-permute-start) | collective-permute-done | bytes 524320 | tf_op jit(solution)/shard_map/ppermute | solution.py:33
  5.1 0.1 pack_depth.1
  5.1 2.5 %collective-permute-start.1 = (f32[4,264,128]{2,1,0:T(8,128)S(1)}, f32[4,264,128]{2,1,0:T(8,128)S(1)}, u32[]{:S(2)}, u32[]{:S(2)}) collective-permute-start(f32[4,264,128]{2,1,0:T(8,128)S(1)} %get-tuple-element.31), channel_id=1, source_target_pairs={{0,1},{1,0},{2,3},{3,2},{4,5},{5,4},{6,7},{7,6},{8,9},{9,8},{10,11... | collective-permute-start | bytes 1622024 | tf_op jit(solution)/shard_map/ppermute | solution.py:37
  7.6 0.7 %collective-permute-start.2 = (f32[4,264,128]{2,1,0:T(8,128)S(1)}, f32[4,264,128]{2,1,0:T(8,128)S(1)}, u32[]{:S(2)}, u32[]{:S(2)}) collective-permute-start(f32[4,264,128]{2,1,0:T(8,128)S(1)} %get-tuple-element.32), channel_id=1, source_target_pairs={{1,2},{2,1},{5,6},{6,5},{9,10},{10,9},{13,14},{14,13},{17,18},{18,... | collective-permute-start | bytes 1622024 | tf_op jit(solution)/shard_map/ppermute | solution.py:37
  8.3 3.7 %collective-permute-start.5 = (f32[4,16,2,8,128]{4,3,2,1,0:T(8,128)S(1)}, f32[4,16,2,8,128]{4,3,2,1,0:T(8,128)S(1)}, u32[]{:S(2)}, u32[]{:S(2)}) collective-permute-start(f32[4,16,2,8,128]{4,3,2,1,0:T(8,128)S(1)} %get-tuple-element.39), channel_id=1, source_target_pairs={{4,8},{8,4},{12,16},{16,12},{20,24},{24,20},{5,9},{9,5},{13,17},{1... | collective-permute-start | bytes 1572872 | tf_op jit(solution)/shard_map/ppermute | solution.py:33
  12.0 5.7 %collective-permute-start.3 = (f32[4,8,128]{2,1,0:T(8,128)S(1)}, f32[4,8,128]{2,1,0:T(8,128)S(1)}, u32[]{:S(2)}, u32[]{:S(2)}) collective-permute-start(f32[4,8,128]{2,1,0:T(8,128)S(1)} %get-tuple-element.33), channel_id=1, source_target_pairs={{4,9},{5,8},{6,11},{7,10},{8,5},{9,4},{10,7},{11,6},{12,17},{13,16... | collective-permute-start | bytes 49160 | tf_op jit(solution)/shard_map/ppermute | solution.py:47
  17.7 0.7 %collective-permute-start.4 = (f32[4,8,128]{2,1,0:T(8,128)S(1)}, f32[4,8,128]{2,1,0:T(8,128)S(1)}, u32[]{:S(2)}, u32[]{:S(2)}) collective-permute-start(f32[4,8,128]{2,1,0:T(8,128)S(1)} %get-tuple-element.34), channel_id=1, source_target_pairs={{5,10},{6,9},{9,6},{10,5},{13,18},{14,17},{17,14},{18,13},{21,26},... | collective-permute-start | bytes 49160 | tf_op jit(solution)/shard_map/ppermute | solution.py:47
  18.4 7.0 %interior.1 = (f32[16,4,128,128]{3,2,1,0:T(8,128)S(1)}, f32[16,128,128]{2,1,0:T(8,128)S(1)}, f32[16,2,4,8,128]{4,3,2,1,0:T(8,128)S(1)}, f32[16,4,128,128]{3,2,1,0:T(8,128)S(1)}, f32[4,128,128]{2,1,0:T(8,128)S(1)}) custom-call(f32[3,4]{1,0:T(4,128)S(1)} %copy-done, f32[4,16,16,1024]{3,2,1,0:T(8,128)S(1)} %get-tuple-element.29.block), custom_call_target="tpu_custom_call" | custom-call | flops 20971520 | bytes 4194304 | tf_op jit(solution)/shard_map/interior/pallas_call | solution.py:764
  25.5 2.2 %outer.1 = (f32[2,4,18,2,8,128]{5,4,3,2,1,0:T(8,128)S(1)}, f32[16,4,4,8,128]{4,3,2,1,0:T(8,128)S(1)}, f32[16,4,4,8,128]{4,3,2,1,0:T(8,128)S(1)}, f32[4,32,128]{2,1,0:T(8,128)S(1)}) custom-call(f32[3,4]{1,0:T(4,128)S(1)} %copy-done, f32[4,16,2,8,128]{4,3,2,1,0:T(8,128)S(1)} %collective-permute-done.row0_ref, ...), custom_call_target="tpu_custom_call" | custom-call | flops 10485760 | bytes 1048576 | tf_op jit(solution)/shard_map/outer/pallas_call | solution.py:788
  27.7 2.5 %settle.1 = (f32[4,4,128,128]{3,2,1,0:T(8,128)S(1)}, f32[2,4,18,2,8,128]{5,4,3,2,1,0:T(8,128)S(1)}, f32[16,4,4,8,128]{4,3,2,1,0:T(8,128)S(1)}, f32[16,1152]{1,0:...) custom-call(f32[3,4]{1,0:T(4,128)S(1)} %copy-done, ...), custom_call_target="tpu_custom_call", output_to_operand_aliasing={{1}: (11, {}), {2}: (12, {})} | custom-call | tf_op jit(solution)/shard_map/settle/pallas_call | solution.py:807
  30.3 2.5 %collective-permute-start.6 = (f32[16,1152]{1,0:T(8,128)S(1)}, f32[16,1152]{1,0:T(8,128)S(1)}, u32[]{:S(2)}, u32[]{:S(2)}) collective-permute-start(f32[16,1152]{1,0:T(8,128)S(1)} %get-tuple-element.44), channel_id=1, source_target_pairs={{0,2},{1,3},{2,0},{3,1},{4,6},{5,7},{6,4},{7,5},{8,10},{9,11},{10,... | collective-permute-start | bytes 221192 | tf_op jit(solution)/shard_map/ppermute | solution.py:853
  32.8 0.5 %collective-permute-start.7 = (f32[16,1152]{1,0:T(8,128)S(1)}, f32[16,1152]{1,0:T(8,128)S(1)}, u32[]{:S(2)}, u32[]{:S(2)}) collective-permute-start(f32[16,1152]{1,0:T(8,128)S(1)} %get-tuple-element.45), channel_id=1, source_target_pairs={{0,1},{1,0},{2,3},{3,2},{4,5},{5,4},{6,7},{7,6},{8,9},{9,8},{10,11... | collective-permute-start | bytes 221192 | tf_op jit(solution)/shard_map/ppermute | solution.py:853
  33.3 2.0 %collective-permute-start.8 = (f32[16,1152]{1,0:T(8,128)S(1)}, f32[16,1152]{1,0:T(8,128)S(1)}, u32[]{:S(2)}, u32[]{:S(2)}) collective-permute-start(f32[16,1152]{1,0:T(8,128)S(1)} %get-tuple-element.46), channel_id=1, source_target_pairs={{0,3},{1,2},{2,1},{3,0},{4,7},{5,6},{6,5},{7,4},{8,11},{9,10},{10,... | collective-permute-start | bytes 221192 | tf_op jit(solution)/shard_map/ppermute | solution.py:853
  35.3 0.6 %collective-permute-done.6.refs_1_ = f32[16,1152]{1,0:T(8,128)S(1)} collective-permute-done((f32[16,1152]{1,0:T(8,128)S(1)}, f32[16,1152]{1,0:T(8,128)S(1)}, u32[]{:S(2)}, u32[]{:S(2)}) %collective-permute-start.6) | collective-permute-done | bytes 73760 | tf_op jit(solution)/shard_map/ppermute | solution.py:853
  35.9 0.4 collective-permute-done.7.refs_2_
  36.4 2.3 %collective-permute-done.8.refs_3_ = f32[16,1152]{1,0:T(8,128)S(1)} collective-permute-done((f32[16,1152]{1,0:T(8,128)S(1)}, f32[16,1152]{1,0:T(8,128)S(1)}, u32[]{:S(2)}, u32[]{:S(2)}) %collective-permute-start.8) | collective-permute-done | bytes 73760 | tf_op jit(solution)/shard_map/ppermute | solution.py:853
  38.6 0.2 over.1
  38.8 0.1 collective-permute-start.9
  38.9 5.5 %collective-permute-start.10 = (f32[2,1152]{1,0:T(2,128)S(1)}, f32[2,1152]{1,0:T(2,128)S(1)}, u32[]{:S(2)}, u32[]{:S(2)}) collective-permute-start(f32[2,1152]{1,0:T(2,128)S(1)} %get-tuple-element.49), channel_id=1, source_target_pairs={{4,8},{8,4},{12,16},{16,12},{20,24},{24,20},{5,9},{9,5},{13,17},{1... | collective-permute-start | bytes 27656 | tf_op jit(solution)/shard_map/ppermute | solution.py:33
  44.4 2.7 %assemble.1 = (f32[16,16,1024]{2,1,0:T(8,128)}, f32[3,16,16,1024]{3,2,1,0:T(8,128)}) custom-call(f32[4,4,128,128]{3,2,1,0:T(8,128)S(1)} %get-tuple-element.50.whole_ref, f32[16,4,4,8,128]{4,3,2,1,0:T(8,128)S(1)} %get-tuple-element.51.lines_ref, f32[16,4,128,128]{3,2,1,0:T(8,128)S(1)} %get-tuple-element.52.late_ref), custom_call_target="tpu_custom_call" | custom-call | flops 5242880 | bytes 4194304 | tf_op jit(solution)/shard_map/assemble/pallas_call | solution.py:835
  47.1 1.1 %bilateral.1 = f32[4,16,256]{2,1,0:T(8,128)} custom-call(f32[16,1152]{1,0:T(8,128)S(1)} %get-tuple-element.47.picture_ref, f32[2,1152]{1,0:T(2,128)S(1)} %collective-permute-done.9.swap0_ref, f32[2,1152]{1,0:T(2,128)S(1)} %collective-permute-done.10.swap1_ref), custom_call_target="tpu_custom_call" | custom-call | tf_op jit(solution)/shard_map/bilateral/pallas_call | solution.py:864
  (8 shorter events, 0.0 us)
Async XLA Ops:
  3.1 15.3 %copy-start = (f32[3,4]{1,0:T(4,128)S(1)}, f32[3,4]{1,0:T(4,128)}, u32[]{:S(2)}) copy-start(f32[3,4]{1,0:T(4,128)} %palette_ref.5) | copy-start | bytes 148
  3.1 2.0 %collective-permute-start = (f32[4,16,2,8,128]{4,3,2,1,0:T(8,128)S(1)}, f32[4,16,2,8,128]{4,3,2,1,0:T(8,128)S(1)}, u32[]{:S(2)}, u32[]{:S(2)}) collective-permute-start(f32[4,16,2,8,128]{4,3,2,1,0:T(8,128)S(1)} %get-tuple-element.30), channel_id=1, source_target_pairs={{0,4},{4,0},{8,12},{12,8},{16,20},{20,16},{24,28},{28,24},{1,5},{5... | collective-permute-start | bytes 1572872 | tf_op jit(solution)/shard_map/ppermute | solution.py:33
  5.1 22.6 %collective-permute-start.1 = (f32[4,264,128]{2,1,0:T(8,128)S(1)}, f32[4,264,128]{2,1,0:T(8,128)S(1)}, u32[]{:S(2)}, u32[]{:S(2)}) collective-permute-start(f32[4,264,128]{2,1,0:T(8,128)S(1)} %get-tuple-element.31), channel_id=1, source_target_pairs={{0,1},{1,0},{2,3},{3,2},{4,5},{5,4},{6,7},{7,6},{8,9},{9,8},{10,11... | collective-permute-start | bytes 1622024 | tf_op jit(solution)/shard_map/ppermute | solution.py:37
  7.6 20.1 %collective-permute-start.2 = (f32[4,264,128]{2,1,0:T(8,128)S(1)}, f32[4,264,128]{2,1,0:T(8,128)S(1)}, u32[]{:S(2)}, u32[]{:S(2)}) collective-permute-start(f32[4,264,128]{2,1,0:T(8,128)S(1)} %get-tuple-element.32), channel_id=1, source_target_pairs={{1,2},{2,1},{5,6},{6,5},{9,10},{10,9},{13,14},{14,13},{17,18},{18,... | collective-permute-start | bytes 1622024 | tf_op jit(solution)/shard_map/ppermute | solution.py:37
  8.3 17.1 %collective-permute-start.5 = (f32[4,16,2,8,128]{4,3,2,1,0:T(8,128)S(1)}, f32[4,16,2,8,128]{4,3,2,1,0:T(8,128)S(1)}, u32[]{:S(2)}, u32[]{:S(2)}) collective-permute-start(f32[4,16,2,8,128]{4,3,2,1,0:T(8,128)S(1)} %get-tuple-element.39), channel_id=1, source_target_pairs={{4,8},{8,4},{12,16},{16,12},{20,24},{24,20},{5,9},{9,5},{13,17},{1... | collective-permute-start | bytes 1572872 | tf_op jit(solution)/shard_map/ppermute | solution.py:33
  12.0 15.7 %collective-permute-start.3 = (f32[4,8,128]{2,1,0:T(8,128)S(1)}, f32[4,8,128]{2,1,0:T(8,128)S(1)}, u32[]{:S(2)}, u32[]{:S(2)}) collective-permute-start(f32[4,8,128]{2,1,0:T(8,128)S(1)} %get-tuple-element.33), channel_id=1, source_target_pairs={{4,9},{5,8},{6,11},{7,10},{8,5},{9,4},{10,7},{11,6},{12,17},{13,16... | collective-permute-start | bytes 49160 | tf_op jit(solution)/shard_map/ppermute | solution.py:47
  17.7 10.0 %collective-permute-start.4 = (f32[4,8,128]{2,1,0:T(8,128)S(1)}, f32[4,8,128]{2,1,0:T(8,128)S(1)}, u32[]{:S(2)}, u32[]{:S(2)}) collective-permute-start(f32[4,8,128]{2,1,0:T(8,128)S(1)} %get-tuple-element.34), channel_id=1, source_target_pairs={{5,10},{6,9},{9,6},{10,5},{13,18},{14,17},{17,14},{18,13},{21,26},... | collective-permute-start | bytes 49160 | tf_op jit(solution)/shard_map/ppermute | solution.py:47
  30.3 5.7 %collective-permute-start.6 = (f32[16,1152]{1,0:T(8,128)S(1)}, f32[16,1152]{1,0:T(8,128)S(1)}, u32[]{:S(2)}, u32[]{:S(2)}) collective-permute-start(f32[16,1152]{1,0:T(8,128)S(1)} %get-tuple-element.44), channel_id=1, source_target_pairs={{0,2},{1,3},{2,0},{3,1},{4,6},{5,7},{6,4},{7,5},{8,10},{9,11},{10,... | collective-permute-start | bytes 221192 | tf_op jit(solution)/shard_map/ppermute | solution.py:853
  32.8 3.6 %collective-permute-start.7 = (f32[16,1152]{1,0:T(8,128)S(1)}, f32[16,1152]{1,0:T(8,128)S(1)}, u32[]{:S(2)}, u32[]{:S(2)}) collective-permute-start(f32[16,1152]{1,0:T(8,128)S(1)} %get-tuple-element.45), channel_id=1, source_target_pairs={{0,1},{1,0},{2,3},{3,2},{4,5},{5,4},{6,7},{7,6},{8,9},{9,8},{10,11... | collective-permute-start | bytes 221192 | tf_op jit(solution)/shard_map/ppermute | solution.py:853
  33.3 5.3 %collective-permute-start.8 = (f32[16,1152]{1,0:T(8,128)S(1)}, f32[16,1152]{1,0:T(8,128)S(1)}, u32[]{:S(2)}, u32[]{:S(2)}) collective-permute-start(f32[16,1152]{1,0:T(8,128)S(1)} %get-tuple-element.46), channel_id=1, source_target_pairs={{0,3},{1,2},{2,1},{3,0},{4,7},{5,6},{6,5},{7,4},{8,11},{9,10},{10,... | collective-permute-start | bytes 221192 | tf_op jit(solution)/shard_map/ppermute | solution.py:853
  38.8 8.3 %collective-permute-start.9 = (f32[2,1152]{1,0:T(2,128)S(1)}, f32[2,1152]{1,0:T(2,128)S(1)}, u32[]{:S(2)}, u32[]{:S(2)}) collective-permute-start(f32[2,1152]{1,0:T(2,128)S(1)} %get-tuple-element.48), channel_id=1, source_target_pairs={{0,4},{4,0},{8,12},{12,8},{16,20},{20,16},{24,28},{28,24},{1,5},{5... | collective-permute-start | bytes 27656 | tf_op jit(solution)/shard_map/ppermute | solution.py:33
  38.9 8.2 %collective-permute-start.10 = (f32[2,1152]{1,0:T(2,128)S(1)}, f32[2,1152]{1,0:T(2,128)S(1)}, u32[]{:S(2)}, u32[]{:S(2)}) collective-permute-start(f32[2,1152]{1,0:T(2,128)S(1)} %get-tuple-element.49), channel_id=1, source_target_pairs={{4,8},{8,4},{12,16},{16,12},{20,24},{24,20},{5,9},{9,5},{13,17},{1... | collective-permute-start | bytes 27656 | tf_op jit(solution)/shard_map/ppermute | solution.py:33
